TPU v7x, 32 devices: a whole 2x2x4 slice. The times are simulated.
32 devices in a mesh: ep: 8 (over z, x), tp: 4 (over y, core).
Axes of the slice: x: 2, y: 2, z: 4, core: 2. Of those that a mesh axis runs over, the one named last changes fastest.
Arguments:
- tokens: bfloat16 [16384, 768], P(('ep', 'tp')), may hold values from -6 to 6
- d_out: bfloat16 [16384, 768], P(('ep', 'tp')), may hold values from -6 to 6
- segment: int32 [16384], P(('ep', 'tp')), may hold values from -1 to 15, as said below
- route: int32 [16384, 1], P(('ep', 'tp')), may hold values from 0 to 15; in each aligned block of 512 rows (0 to 511, 512 to 1023, ...) at most 48 rows name the same one
- gain_one: bfloat16 [768], replicated, may hold values from 0.5 to 1.5
- w_in: bfloat16 [768, 3072], replicated, may hold values from -0.21875 to 0.21875
- conv_w: bfloat16 [4, 1536], replicated, may hold values from -3 to 3
- conv_b: bfloat16 [1536], replicated, may hold values from -3 to 3
- w_x: bfloat16 [1536, 80], replicated, may hold values from -0.15625 to 0.15625
- w_dt: bfloat16 [48, 1536], replicated, may hold values from -0.875 to 0.875
- b_dt: bfloat16 [1536], replicated, may hold values from -6 to -2
- a_log: bfloat16 [16, 1536], replicated, may hold values from 0 to 2.765625
- d_skip: bfloat16 [1536], replicated, may hold values from 0.5 to 1.5
- w_out: bfloat16 [1536, 768], replicated, may hold values from -0.15625 to 0.15625
- gain_two: bfloat16 [768], replicated, may hold values from 0.5 to 1.5
- w_router: bfloat16 [768, 16], replicated, may hold values from -0.15625 to 0.15625
- w_up: bfloat16 [16, 768, 3072], P('ep', None, 'tp'), may hold values from -0.21875 to 0.21875
- w_down: bfloat16 [16, 3072, 768], P('ep', 'tp'), may hold values from -1.75 to 1.75
Outputs:
- block_out: bfloat16 [16384, 768], P(('ep', 'tp'))
- d_tokens: float32 [16384, 768], P(('ep', 'tp'))
- counts: int32 [2, 16], replicated
- g_gain_one: float32 [768], replicated
- g_w_in: float32 [768, 3072], replicated
- g_conv_w: float32 [4, 1536], replicated
- g_conv_b: float32 [1536], replicated
- g_w_x: float32 [1536, 80], replicated
- g_w_dt: float32 [48, 1536], replicated
- g_b_dt: float32 [1536], replicated
- g_a_log: float32 [16, 1536], replicated
- g_d_skip: float32 [1536], replicated
- g_w_out: float32 [1536, 768], replicated
- g_gain_two: float32 [768], replicated
- g_w_router: float32 [768, 16], replicated
- g_w_up: float32 [16, 768, 3072], P('ep', None, 'tp')
- g_w_down: float32 [16, 3072, 768], P('ep', 'tp')
Inputs may be any that keep to these rules, and one draw needn't show every extreme that they name: `segment`: in each device's block of 512 tokens the samples are numbered 0, 1, 2 in order up to at most 15, each a run of consecutive positions beginning with the block's first position; padding tokens (-1) follow the last sample. No sample crosses a block. In every draw some block holds one sample of all 512 tokens, and some block reaches the largest number. `route`: within the tokens of one device, no expert is named by more than 48 tokens, padding included; some device reaches 48 for some expert.
All inputs are finite; a program needn't handle non-finite values.
Results may differ from a plain program's by a relative error of at most 0.0092.
Values may be sent and summed in bfloat16 or wider, within the bound.
A program may use at most 576 MiB of HBM per device.

v0:
```python
from functools import partial

import jax
import jax.numpy as jnp
from jax import lax
from jax.sharding import PartitionSpec as P

SCAN_BLOCK = 16


EPS = 1e-06
HIGH = lax.Precision.HIGHEST


def prefix(part, axis, combine, identity):
    place = lax.axis_index(axis)
    gathered = lax.all_gather(part, axis)
    state = jnp.zeros_like(part) + jnp.asarray(identity, part.dtype)

    def one(lap, state):
        return combine(state, lax.dynamic_index_in_dim(gathered, lap, 0, False))

    return lax.fori_loop(0, place, one, state)


def rms_scale(values, gain):
    return values * lax.rsqrt(jnp.mean(values * values, axis=-1, keepdims=True) + EPS) * gain


def sample_masks(segment, taps):
    length = segment.shape[0]
    masks = []
    for shift in range(taps):
        earlier = jnp.concatenate([jnp.full((shift,), -2, jnp.int32), segment[: length - shift]])
        masks.append((earlier == segment).astype(jnp.float32)[:, None])
    return masks


def causal_conv(inner, conv_w, conv_b, masks):
    taps = conv_w.shape[0]
    length = inner.shape[0]
    total = conv_b[None, :] + conv_w[taps - 1][None, :] * inner
    for shift in range(1, taps):
        moved = jnp.concatenate(
            [jnp.zeros((shift, inner.shape[1]), jnp.float32), inner[: length - shift]], axis=0
        )
        total = total + conv_w[taps - 1 - shift][None, :] * moved * masks[shift]
    return total


def combine_pairs(first, second):
    return (first[0] * second[0], second[0] * first[1] + second[1])


def to_blocks(values, blocks):
    length = values.shape[0]
    return jnp.swapaxes(values.reshape((blocks, length // blocks) + values.shape[1:]), 0, 1)


def selective_scan(step, in_b, out_c, conv, keep, rates):
    length, width = conv.shape
    blocks = length // SCAN_BLOCK
    states = rates.shape[0]
    step_p = to_blocks(step, blocks)
    inb_p = to_blocks(in_b, blocks)
    outc_p = to_blocks(out_c, blocks)
    conv_p = to_blocks(conv, blocks)
    keep_p = to_blocks(keep, blocks)

    def terms_at(step_t, inb_t, conv_t, keep_t):
        decay = keep_t[:, None, None] * jnp.exp(step_t[:, None, :] * rates[None])
        source = inb_t[:, :, None] * (step_t * conv_t)[:, None, :]
        return (decay, source)

    def first_pass(carry, item):
        decay, source = terms_at(item[0], item[1], item[2], item[3])
        return ((decay * carry[0] + source, decay * carry[1]), None)

    zero_state = jnp.zeros((blocks, states, width), jnp.float32)
    (block_ends, products), _ = lax.scan(
        jax.checkpoint(first_pass),
        (zero_state, jnp.ones_like(zero_state)),
        (step_p, inb_p, conv_p, keep_p),
    )
    _, reached = lax.associative_scan(combine_pairs, (products, block_ends), axis=0)
    starts = jnp.concatenate([jnp.zeros_like(reached[:1]), reached[:-1]], axis=0)

    def second_pass(state, item):
        decay, source = terms_at(item[0], item[1], item[2], item[3])
        state = decay * state + source
        return (state, jnp.sum(item[4][:, :, None] * state, axis=1))

    _, outputs = lax.scan(
        jax.checkpoint(second_pass), starts, (step_p, inb_p, conv_p, keep_p, outc_p)
    )
    return jnp.swapaxes(outputs, 0, 1).reshape(length, width)


def middle(inner, gate_z, conv_w, conv_b, w_x, w_dt, b_dt, a_log, d_skip, masks):
    conv = jax.nn.silu(causal_conv(inner, conv_w, conv_b, masks))
    proj = jnp.dot(conv, w_x, precision=HIGH)
    rank_dt = w_dt.shape[0]
    states = a_log.shape[0]
    step = jax.nn.softplus(jnp.dot(proj[:, :rank_dt], w_dt, precision=HIGH) + b_dt)
    in_b = proj[:, rank_dt : rank_dt + states]
    out_c = proj[:, rank_dt + states :]
    rates = -jnp.exp(a_log)
    ssm_out = selective_scan(step, in_b, out_c, conv, masks[1][:, 0], rates)
    result = ssm_out + d_skip * conv
    return result * jax.nn.silu(gate_z)


def add_counts(earlier, later):
    return earlier + later


def contract_rows(left, right):
    return lax.dot_general(
        left, right, (((0,), (0,)), ((), ())), preferred_element_type=jnp.float32
    )


def local(
    tokens,
    d_out,
    segment,
    route,
    gain_one,
    w_in,
    conv_w,
    conv_b,
    w_x,
    w_dt,
    b_dt,
    a_log,
    d_skip,
    w_out,
    gain_two,
    w_router,
    w_up,
    w_down,
):
    length, width = tokens.shape
    inner_w = w_in.shape[1] // 2
    experts = w_router.shape[1]
    local_experts = w_up.shape[0]
    groups = lax.axis_size("ep")
    slots = 3 * length // (2 * experts)
    capacity = 5 * length * lax.axis_size("ep") * lax.axis_size("tp") // (4 * experts)
    token_f = tokens.astype(jnp.float32)
    valid = (segment >= 0).astype(jnp.float32)[:, None]
    masks = sample_masks(segment, conv_w.shape[0])
    small_f = [
        item.astype(jnp.float32) for item in (conv_w, conv_b, w_x, w_dt, b_dt, a_log, d_skip)
    ]
    normed_one, norm_one_pull = jax.vjp(rms_scale, token_f, gain_one.astype(jnp.float32))
    normed_low = normed_one.astype(jnp.bfloat16)
    both = jnp.dot(normed_low, w_in, preferred_element_type=jnp.float32)

    def middle_fixed(inner, gate_z, conv_wf, conv_bf, w_xf, w_dtf, b_dtf, a_logf, d_skipf):
        return middle(inner, gate_z, conv_wf, conv_bf, w_xf, w_dtf, b_dtf, a_logf, d_skipf, masks)

    gated, middle_pull = jax.vjp(
        middle_fixed,
        both[:, :inner_w],
        both[:, inner_w:],
        small_f[0],
        small_f[1],
        small_f[2],
        small_f[3],
        small_f[4],
        small_f[5],
        small_f[6],
    )
    gated_low = gated.astype(jnp.bfloat16)
    mixed = jnp.dot(gated_low, w_out, preferred_element_type=jnp.float32)
    after_mix = token_f + mixed * valid
    normed_two, norm_two_pull = jax.vjp(rms_scale, after_mix, gain_two.astype(jnp.float32))
    pick_int = (
        (route == jnp.arange(experts, dtype=jnp.int32)[None, :]) & (segment >= 0)[:, None]
    ).astype(jnp.int32)
    picks = pick_int.astype(jnp.float32)

    def router(normed_in, router_w):
        probs = jax.nn.softmax(jnp.dot(normed_in, router_w, precision=HIGH), axis=-1)
        return jnp.sum(probs * picks, axis=-1)

    gate, router_pull = jax.vjp(router, normed_two, w_router.astype(jnp.float32))
    local_count = jnp.sum(pick_int, axis=0)
    prior = prefix(local_count, ("ep", "tp"), add_counts, jnp.zeros_like(local_count))
    local_rank = jnp.sum(jnp.cumsum(pick_int, axis=0) * pick_int, axis=1) - 1
    global_rank = jnp.sum(pick_int * prior[None, :], axis=1) + local_rank
    kept = (segment >= 0) & (global_rank < capacity)
    slot_id = jnp.where(kept, route[:, 0] * slots + local_rank, -1)
    dispatch = (jnp.arange(experts * slots, dtype=jnp.int32)[:, None] == slot_id[None, :]).astype(
        jnp.bfloat16
    )
    expert_in = normed_two.astype(jnp.bfloat16)
    outgoing = jnp.dot(dispatch, expert_in, preferred_element_type=jnp.float32).astype(jnp.bfloat16)
    outgoing = outgoing.reshape(groups, local_experts, slots, width)
    received = lax.all_to_all(outgoing, "ep", split_axis=0, concat_axis=2, tiled=True)
    full_up, full_down = (w_up, w_down)
    expert_rows = lax.all_gather(received, "tp", axis=2, tiled=True)
    hidden_pre = jnp.einsum(
        "axrd,xdf->axrf", expert_rows, full_up, preferred_element_type=jnp.float32
    )
    gelu_value, gelu_pull = jax.vjp(partial(jax.nn.gelu, approximate=False), hidden_pre)
    hidden_low = gelu_value.astype(jnp.bfloat16)
    terms = jnp.einsum("axrf,xfd->axrd", hidden_low, full_down, preferred_element_type=jnp.float32)
    expert_out = lax.psum_scatter(terms, "tp", scatter_dimension=2, tiled=True)
    returned = lax.all_to_all(
        expert_out.astype(jnp.bfloat16), "ep", split_axis=2, concat_axis=0, tiled=True
    )
    returned = returned.reshape(experts * slots, width)
    token_out = contract_rows(dispatch, returned)
    keep_f = kept.astype(jnp.float32)[:, None]
    weighting = gate[:, None] * keep_f
    final = after_mix + weighting * token_out
    upstream = d_out.astype(jnp.float32)
    d_token_out = (weighting * upstream).astype(jnp.bfloat16)
    d_slots = jnp.dot(dispatch, d_token_out, preferred_element_type=jnp.float32).astype(
        jnp.bfloat16
    )
    d_slots = d_slots.reshape(groups, local_experts, slots, width)
    d_gate = keep_f[:, 0] * jnp.sum(upstream * token_out, axis=1)
    d_received = lax.all_to_all(d_slots, "ep", split_axis=0, concat_axis=2, tiled=True)
    d_rows_all = lax.all_gather(d_received, "tp", axis=2, tiled=True)
    again = jnp.einsum("axrd,xdf->axrf", expert_rows, full_up, preferred_element_type=jnp.float32)
    again_value, gelu_back = jax.vjp(partial(jax.nn.gelu, approximate=False), again)
    hidden_back = again_value.astype(jnp.bfloat16)
    grad_down = jnp.einsum(
        "axrf,axrd->xfd", hidden_back, d_rows_all, preferred_element_type=jnp.float32
    )
    d_hidden = jnp.einsum(
        "axrd,xfd->axrf", d_rows_all, full_down, preferred_element_type=jnp.float32
    )
    d_pre = gelu_back(d_hidden)[0].astype(jnp.bfloat16)
    grad_up = jnp.einsum("axrd,axrf->xdf", expert_rows, d_pre, preferred_element_type=jnp.float32)
    row_terms = jnp.einsum("axrf,xdf->axrd", d_pre, full_up, preferred_element_type=jnp.float32)
    d_expert_in = lax.psum_scatter(row_terms, "tp", scatter_dimension=2, tiled=True)
    d_back = lax.all_to_all(
        d_expert_in.astype(jnp.bfloat16), "ep", split_axis=2, concat_axis=0, tiled=True
    )
    d_normed = contract_rows(dispatch, d_back.reshape(experts * slots, width))
    d_norm_router, grad_router = router_pull(d_gate)
    d_after, grad_gain_two = norm_two_pull(d_normed + d_norm_router)
    d_after = d_after + upstream
    d_mixed = (d_after * valid).astype(jnp.bfloat16)
    grad_out = contract_rows(gated_low, d_mixed)
    d_gated = lax.dot_general(
        d_mixed, w_out, (((1,), (1,)), ((), ())), preferred_element_type=jnp.float32
    )
    middle_grads = middle_pull(d_gated)
    d_both = jnp.concatenate([middle_grads[0], middle_grads[1]], axis=1).astype(jnp.bfloat16)
    grad_in = contract_rows(normed_low, d_both)
    d_normed_one = lax.dot_general(
        d_both, w_in, (((1,), (1,)), ((), ())), preferred_element_type=jnp.float32
    )
    d_tokens_norm, grad_gain_one = norm_one_pull(d_normed_one)
    d_tokens = d_after + d_tokens_norm
    held = jnp.sum(pick_int * kept.astype(jnp.int32)[:, None], axis=0)
    count_f = jnp.stack([local_count, local_count - held]).astype(jnp.float32)
    summed = lax.psum(
        (
            grad_gain_one,
            grad_in,
            middle_grads[2],
            middle_grads[3],
            middle_grads[4],
            middle_grads[5],
            middle_grads[6],
            middle_grads[7],
            middle_grads[8],
            grad_out,
            grad_gain_two,
            grad_router,
            count_f,
        ),
        ("ep", "tp"),
    )
    return (
        final.astype(jnp.bfloat16),
        d_tokens,
        summed[12].astype(jnp.int32),
        summed[0],
        summed[1],
        summed[2],
        summed[3],
        summed[4],
        summed[5],
        summed[6],
        summed[7],
        summed[8],
        summed[9],
        summed[10],
        summed[11],
        grad_up,
        grad_down,
    )


def solution(mesh):
    in_specs = (
        P(("ep", "tp"), None),
        P(("ep", "tp"), None),
        P(("ep", "tp")),
        P(("ep", "tp"), None),
        P(),
        P(),
        P(),
        P(),
        P(),
        P(),
        P(),
        P(),
        P(),
        P(),
        P(),
        P(),
        P("ep", None, "tp"),
        P("ep", "tp", None),
    )
    out_specs = (
        P(("ep", "tp"), None),
        P(("ep", "tp"), None),
        P(),
        P(),
        P(),
        P(),
        P(),
        P(),
        P(),
        P(),
        P(),
        P(),
        P(),
        P(),
        P(),
        P("ep", None, "tp"),
        P("ep", "tp", None),
    )
    return jax.shard_map(local, mesh=mesh, in_specs=in_specs, out_specs=out_specs, check_vma=False)
```

profile of v0, /device:TPU:1, one launch (start us, length us, event | category | flops | bytes accessed | tf_op | source)
XLA Modules:
  0.0 2524.4 jit_solution(8566170891215152491)
XLA Ops:
  22.3 7.7 fusion.49
  47.1 16.5 broadcast.378.clone
  63.6 16.4 broadcast.378.clone.1
  80.0 250.0 %while.93 = (s32[]{:T(128)}, f32[32,16,1536]{2,1,0:T(8,128)}, f32[32,16,1536]{2,1,0:T(8,128)}, f32[16,32,16,1536]{3,2,1,0:T(8,128)}, f32[16,32,16,1536]{3,2,1,0:...) while((s32[]{:T(128)}, f32[32,16,1536]{2,1,0:T(8,128)}, ...), condition=%wide.region_2.3_spmd.clone, body=%wide.region_1.2_spmd.clone.sunk | while | flops 7913475 | bytes 26647568 | solution.py:80
  90.4 6.6 bitcast_dynamic-update-slice_fusion.21
  99.7 6.6 fusion.186
  106.3 6.7 bitcast_dynamic-update-slice_fusion.21
  115.7 6.6 fusion.186
  122.3 6.7 bitcast_dynamic-update-slice_fusion.21
  131.8 6.6 fusion.186
  138.4 6.5 bitcast_dynamic-update-slice_fusion.21
  147.6 6.6 fusion.186
  154.2 6.6 bitcast_dynamic-update-slice_fusion.21
  163.5 6.6 fusion.186
  170.1 6.6 bitcast_dynamic-update-slice_fusion.21
  179.5 6.6 fusion.186
  186.1 6.6 bitcast_dynamic-update-slice_fusion.21
  195.4 6.6 fusion.186
  202.0 6.7 bitcast_dynamic-update-slice_fusion.21
  211.5 6.6 fusion.186
  218.1 6.5 bitcast_dynamic-update-slice_fusion.21
  227.3 6.6 fusion.186
  233.9 6.6 bitcast_dynamic-update-slice_fusion.21
  243.2 6.6 fusion.186
  249.8 6.6 bitcast_dynamic-update-slice_fusion.21
  259.1 6.6 fusion.186
  265.8 6.6 bitcast_dynamic-update-slice_fusion.21
  275.1 6.6 fusion.186
  281.7 6.6 bitcast_dynamic-update-slice_fusion.21
  291.0 6.6 fusion.186
  297.6 6.6 bitcast_dynamic-update-slice_fusion.21
  306.9 6.6 fusion.186
  313.6 6.6 bitcast_dynamic-update-slice_fusion.21
  322.9 6.6 fusion.186
  379.9 10.9 pad.393
  393.5 10.9 pad.299
  409.9 16.5 broadcast.378
  428.5 197.7 %while.91 = (s32[]{:T(128)}, f32[32,16,1536]{2,1,0:T(8,128)}, f32[16,32,1536]{2,1,0:T(8,128)}, f32[16,32,16,1536]{3,2,1,0:T(8,128)}, f32[16,32]{1,0:T(8,128)S(1)...) while((s32[]{:T(128)}, f32[32,16,1536]{2,1,0:T(8,128)}, ...), condition=%wide.region_5.6_spmd, body=%wide.region_3.5_spmd.sunk | while | flops 5505026 | bytes 14661117 | solution.py:93
  637.8 40.7 %all-reduce.62 = s32[512]{0:T(512)S(1)} all-reduce(s32[512]{0:T(512)S(1)} %dynamic-update-slice), channel_id=2, replica_groups=mesh['ep'=8,'tp'=4] {'ep','tp'}, use_global_device_ids=true, to_apply=%add.62 | all-reduce | flops 512 | bytes 4096
  683.1 32.1 %all_to_all.66 = bf16[8,2,48,768]{3,2,1,0:T(8,128)(2,1)S(1)} all-to-all(bf16[8,2,48,768]{3,2,1,0:T(8,128)(2,1)S(1)} %bitcast.381), channel_id=1, replica_groups=mesh['ep'=8,'tp'=4] {'ep'}, dimensions={0} | all-to-all | bytes 2359296 | tf_op jit(solution)/shard_map/all_to_all | solution.py:201
  716.4 38.8 %all-gather.4.cloned.1.call-done = bf16[1,2,1536,768]{3,2,1,0:T(8,128)(2,1)} async-done(((bf16[1,2,384,768]{3,2,1,0:T(8,128)(2,1)}), bf16[1,2,1536,768]{3,2,1,0:T(8,128)(2,1)}) %all-gather.4.cloned.1.call-update) | async-done | bytes 4718608 | tf_op jit(solution)/shard_map/all_gather | solution.py:203
  765.3 25.9 %convolution_bitcast_fusion.1 = f32[1,2,1536,768]{3,2,1,0:T(8,128)} fusion(bf16[2,768,768]{2,1,0:T(8,128)(2,1)S(1)} %copy-done, f32[2,1536,768]{2,1,0:T(8,128)S(1)} %fusion.38), kind=kOutput, calls=%fused_computation.96 | convolution fusion | flops 3777232896 | bytes 21233664 | tf_op jit(solution)/shard_map/axrf,xfd->axrd/dot_general | solution.py:209
  791.3 78.2 %reduce-scatter.3.cloned.1.call-done = f32[1,2,384,768]{3,2,1,0:T(8,128)} async-done(((f32[1,2,1536,768]{3,2,1,0:T(8,128)}), f32[1,2,384,768]{3,2,1,0:T(8,128)}) %reduce-scatter.3.cloned.1.call-update) | async-done | bytes 2359312 | tf_op jit(solution)/shard_map/reduce_scatter | solution.py:210
  883.0 23.5 all-to-all-done.1
  911.4 32.1 %all_to_all.67 = bf16[8,2,48,768]{3,2,1,0:T(8,128)(2,1)S(1)} all-to-all(bf16[8,2,48,768]{3,2,1,0:T(8,128)(2,1)S(1)} %bitcast.382), channel_id=1, replica_groups=mesh['ep'=8,'tp'=4] {'ep'}, dimensions={0} | all-to-all | bytes 2359296 | tf_op jit(solution)/shard_map/all_to_all | solution.py:226
  944.7 37.3 %all-gather.6.cloned.1.call-done = bf16[1,2,1536,768]{3,2,1,0:T(8,128)(2,1)} async-done(((bf16[1,2,384,768]{3,2,1,0:T(8,128)(2,1)}), bf16[1,2,1536,768]{3,2,1,0:T(8,128)(2,1)}) %all-gather.6.cloned.1.call-update) | async-done | bytes 4718608 | tf_op jit(solution)/shard_map/all_gather | solution.py:227
  982.0 26.4 %fusion.18 = bf16[1,2,1536,768]{3,2,1,0:T(8,128)(2,1)S(1)} fusion(f32[2,1536,768]{2,1,0:T(8,128)} %copy-done.159, bf16[2,768,768]{2,1,0:T(8,128)(2,1)S(1)} %copy-done, bf16[1,2,1536,768]{3,2,1,0:T(8,128)(2,1)} %all-gather.6.cloned.1.call-done), kind=kOutput, calls=%fused_computation.74 | convolution fusion | flops 3793747968 | bytes 21233664 | tf_op jit(solution)/shard_map/axrd,xfd->axrf/dot_general | solution.py:234
  1017.0 78.2 %reduce-scatter.5.cloned.1.call-done = f32[1,2,384,768]{3,2,1,0:T(8,128)} async-done(((f32[1,2,1536,768]{3,2,1,0:T(8,128)}), f32[1,2,384,768]{3,2,1,0:T(8,128)}) %reduce-scatter.5.cloned.1.call-update) | async-done | bytes 2359312 | tf_op jit(solution)/shard_map/reduce_scatter | solution.py:240
  1107.1 25.2 all-to-all-done.3
  1156.7 280.6 %while.94 = (s32[]{:T(128)}, f32[16,1536]{1,0:T(8,128)}, f32[32,16,1536]{2,1,0:T(8,128)}, f32[16,32,1536]{2,1,0:T(8,128)}, f32[16,32,16]{2,1,0:T(8,128)}, /*inde...) while((s32[]{:T(128)}, f32[16,1536]{1,0:T(8,128)}, ...), condition=%wide.region_28.29_spmd.clone, body=%wide.region_22.28_spmd.clone.sunk | while | flops 17423364 | bytes 28472580 | solution.py:93
  1514.2 8.1 multiply_add_fusion.4
  1524.9 6.9 pad.257
  1531.8 10.9 pad.270
  1542.7 6.9 pad.271
  1549.6 10.4 pad.259
  1560.0 6.8 pad.258
  1566.9 6.9 pad.228
  1587.8 183.8 %while.95 = (s32[]{:T(128)}, f32[16,1536]{1,0:T(8,128)S(1)}, f32[32,16,1536]{2,1,0:T(8,128)}, f32[32,16,1536]{2,1,0:T(8,128)S(1)}, f32[16,32,1536]{2,1,0:T(8,128...) while((s32[]{:T(128)}, f32[16,1536]{1,0:T(8,128)S(1)}, ...), condition=%wide.region_34.35_spmd.clone, body=%wide.region_29.34_spmd.clone.sunk | while | flops 13491716 | bytes 67070592 | solution.py:80
  1798.3 7.3 multiply_reduce_fusion.14
  1828.0 10.1 fusion.31
  1838.1 25.2 %fusion.34 = f32[2,768,768]{2,1,0:T(8,128)} fusion(bf16[1,2,1536,768]{3,2,1,0:T(8,128)(2,1)S(1)} %bitcast.403, f32[2,1536,768]{2,1,0:T(8,128)} %copy-done.159), kind=kOutput, calls=%fused_computation.103 | convolution fusion | flops 3777232896 | bytes 18874368 | tf_op jit(solution)/shard_map/axrf,axrd->xfd/dot_general | solution.py:231
  1864.9 82.5 %all-reduce.68.cloned.1.call-done = (f32[2,16]{1,0:T(2,128)}, f32[768]{0:T(1024)}, f32[4,1536]{1,0:T(4,128)}, f32[1536]{0:T(1024)}, f32[1536]{0:T(1024)}, /*inde...) async-done(((f32[2,16]{1,0:T(2,128)}, f32[768]{0:T(1024)}, f32[4,1536]{1,0:T(4,128)}, f32[1536]{0:T(1024)}, f32[1536]{0:T(1024)}, /*index=5*/f32[1536]{0:T(1024)}, ...) | async-done | bytes 98448 | tf_op jit(solution)/shard_map/psum | solution.py:263
  1948.6 550.6 %all-reduce.70.cloned.1.call-done = (f32[768,3072]{1,0:T(8,128)}, f32[1536,80]{0,1:T(8,128)}, f32[48,1536]{1,0:T(8,128)}, f32[16,1536]{1,0:T(8,128)}, f32[1536,768]{1,0:T(8,128)}) async-done(((f32[768,3072]{1,0:T(8,128)}, f32[1536,80]{0,1:T(8,128)}, f32[48,1536]{1,0:T(8,128)}, f32[16,1536]{1,0:T(8,128)}, f32[1536,768]{1,0:T(8,128)}), (f32[768,3072]{1,0:T(8,128)}, f32[1536,80]{0,1:T(8,128)}, ...) | async-done | bytes 15040528 | tf_op jit(solution)/shard_map/psum | solution.py:263
  2500.7 8.7 copy.269
  (1338 shorter events, 1048.7 us)
Async XLA Ops:
  7.2 758.1 %copy-start = (bf16[2,768,768]{2,1,0:T(8,128)(2,1)S(1)}, bf16[2,768,768]{2,1,0:T(8,128)(2,1)}, u32[]{:S(2)}) copy-start(bf16[2,768,768]{2,1,0:T(8,128)(2,1)} %param.45) | copy-start | bytes 7077892
  7.2 748.0 %all-gather.4.cloned.1.call-start = ((), (), s32[]{:S(2)}) async-start(), calls=%async_computation.6 | async-start | bytes 5898240 | tf_op jit(solution)/shard_map/all_gather | solution.py:203
  21.6 8.5 copy-start.106
  21.6 8.5 copy-start.108
  21.6 8.5 copy-start.110
  21.6 8.5 copy-start.112
  22.2 7.9 copy-start.123
  22.2 7.9 copy-start.128
  22.2 7.9 copy-start.130
  22.3 657.8 %copy-start.120 = (pred[512]{0:T(512)(128)(4,1)}, pred[512]{0:T(512)(128)(4,1)S(1)}, u32[]{:S(2)}) copy-start(pred[512]{0:T(512)(128)(4,1)S(1)} %get-tuple-element.1214) | copy-start | bytes 1540
  22.3 9.4 copy-start.80
  333.9 9.0 copy-start.23
  349.1 8.5 copy-start.37
  634.5 46.2 %copy-start.150 = (bf16[768]{0:T(1024)(128)(2,1)S(1)}, bf16[768]{0:T(1024)(128)(2,1)}, u32[]{:S(2)}) copy-start(bf16[768]{0:T(1024)(128)(2,1)} %param.42) | copy-start | bytes 4612
  680.7 35.6 %copy-start.135 = (pred[512]{0:T(512)(128)(4,1)}, pred[512]{0:T(512)(128)(4,1)S(1)}, u32[]{:S(2)}) copy-start(pred[512]{0:T(512)(128)(4,1)S(1)} %get-tuple-element.1204) | copy-start | bytes 1540
  680.7 35.6 %copy-start.151 = (s32[512]{0:T(512)}, s32[512]{0:T(512)S(1)}, u32[]{:S(2)}) copy-start(s32[512]{0:T(512)S(1)} %add_select_fusion) | copy-start | bytes 6148
  716.3 153.2 %reduce-scatter.3.cloned.1.call-start = ((), (), s32[]{:S(2)}) async-start(), calls=%async_computation.7 | async-start | bytes 11796480 | tf_op jit(solution)/shard_map/reduce_scatter | solution.py:210
  873.5 33.0 %all-to-all-start.1 = ((bf16[1,2,384,768]{3,1,0,2:T(2,128)(2,1)}), bf16[1,2,384,768]{3,1,0,2:T(2,128)(2,1)S(1)}, u32[]{:S(2)}, u32[]{:S(2)}) async-start(bf16[1,2,384,768]{3,1,0,2:T(2,128)(2,1)} %copy.110), calls=%async_computation.2 | async-start | bytes 2359296 | tf_op jit(solution)/shard_map/all_to_all | solution.py:211
  878.7 103.2 %all-gather.6.cloned.1.call-start = ((), (), s32[]{:S(2)}) async-start(), calls=%async_computation.8 | async-start | bytes 5898240 | tf_op jit(solution)/shard_map/all_gather | solution.py:227
  944.6 150.6 %reduce-scatter.5.cloned.1.call-start = ((), (), s32[]{:S(2)}) async-start(), calls=%async_computation.9 | async-start | bytes 11796480 | tf_op jit(solution)/shard_map/reduce_scatter | solution.py:240
  982.0 28.6 %copy-start.156 = (bf16[2,768,768]{2,1,0:T(8,128)(2,1)S(1)}, bf16[2,768,768]{2,1,0:T(8,128)(2,1)}, u32[]{:S(2)}) copy-start(bf16[2,768,768]{2,1,0:T(8,128)(2,1)} %param.44) | copy-start | bytes 7077892
  1097.0 7.7 copy-start.139
  1097.0 7.8 copy-start.154
  1097.0 8.4 copy-start.17
  1099.3 33.0 %all-to-all-start.3 = ((bf16[1,2,384,768]{3,1,0,2:T(2,128)(2,1)}), bf16[1,2,384,768]{3,1,0,2:T(2,128)(2,1)S(1)}, u32[]{:S(2)}, u32[]{:S(2)}) async-start(bf16[1,2,384,768]{3,1,0,2:T(2,128)(2,1)} %copy.114), calls=%async_computation.5 | async-start | bytes 2359296 | tf_op jit(solution)/shard_map/all_to_all | solution.py:241
  1104.6 842.8 %all-reduce.68.cloned.1.call-start = ((), (), s32[]{:S(2)}) async-start(), calls=%async_computation.10 | async-start | bytes 215040 | tf_op jit(solution)/shard_map/psum | solution.py:263
  1200.3 7.3 copy-start.59
  1235.6 7.3 copy-start.59
  1253.2 7.3 copy-start.59
  1306.0 7.3 copy-start.59
  1323.7 7.3 copy-start.59
  1358.9 7.3 copy-start.59
  1429.4 7.3 copy-start.59
  1439.5 11.7 copy-start.49
  1452.2 8.5 copy-start.44
  1466.2 15.4 copy-start.79
  1466.2 17.5 copy-start.26
  1466.2 17.5 slice-start.8
  1488.8 10.1 copy-start.64
  1489.0 13.7 copy-start.63
  1498.9 7.5 copy-start.67
  1498.9 11.3 copy-start.66
  1502.7 11.5 slice-start.7
  1549.6 10.4 copy-start.50
  1790.4 7.3 copy-start.36
  1798.3 7.3 copy-start.113
  1808.8 9.5 slice-start.9
  1809.9 8.5 slice-start.10
  1824.3 674.9 %all-reduce.70.cloned.1.call-start = ((), (), s32[]{:S(2)}) async-start(), calls=%async_computation.11 | async-start | bytes 30081024 | tf_op jit(solution)/shard_map/psum | solution.py:263
  1827.9 10.1 slice-start.11
  1827.9 10.1 slice-start.12
  1838.0 25.3 %copy-start.127 = (f32[512]{0:T(512)S(1)}, f32[512]{0:T(512)}, u32[]{:S(2)}) copy-start(f32[512]{0:T(512)} %copy-done.126) | copy-start | bytes 6148
  1838.0 25.3 %copy-start.28 = (f32[512,768]{1,0:T(8,128)S(1)}, f32[512,768]{1,0:T(8,128)}, u32[]{:S(2)}) copy-start(f32[512,768]{1,0:T(8,128)} %copy-done.27) | copy-start | bytes 4718596
  1838.0 25.3 %copy-start.48 = (bf16[512,768]{1,0:T(8,128)(2,1)S(1)}, bf16[512,768]{1,0:T(8,128)(2,1)}, u32[]{:S(2)}) copy-start(bf16[512,768]{1,0:T(8,128)(2,1)} %param.28) | copy-start | bytes 2359300
  1838.0 25.3 %copy-start.76 = (f32[512,768]{1,0:T(8,128)S(1)}, f32[512,768]{1,0:T(8,128)}, u32[]{:S(2)}) copy-start(f32[512,768]{1,0:T(8,128)} %get-tuple-element.1305) | copy-start | bytes 4718596
  2499.2 14.7 slice-start.5
  2500.6 8.8 copy-start.125
  2500.6 9.4 copy-start.143
  2500.7 10.0 copy-start.91
  2500.7 10.8 copy-start.93
  2500.7 11.5 copy-start.142
  2500.7 12.1 copy-start.105
  2500.7 12.7 copy-start.141
  2500.7 13.3 slice-start.6
  (238 other events, 694.7 us)
Sparse Core Ops, SparseCore 0:
  716.4 38.6 all-gather.3
  791.4 78.0 reduce-scatter.2
  944.7 37.1 all-gather.5
  1017.2 78.0 reduce-scatter.4
  1824.4 122.9 all-reduce.67
  1956.0 543.2 all-reduce.69
where the time goes:
time: 2540 us; the launch traced here: 2520 us
  waiting for transfers between devices  914 us (36%)
  local copies, waits for them, and re-layouts  676 us (27%)
  other arithmetic  638 us (25%)
  matrix products  161 us (6%)
  blocking collectives  105 us (4%)
    psum x2, waiting for transfers between devices, local(): lax.psum((grad_gain_one, grad_in, middle_grads[2], middle_grads[3], middl...  633 us
    mul x32, other arithmetic, first_pass(): return ((decay * carry[0] + source, decay * carry[1]), None)  151 us
    pad x32, local copies, waits for them, and re-layouts, selective_scan(): lax.associative_scan(combine_pairs, (products, block_ends), axis=0)  124 us
    squeeze x112, local copies, waits for them, and re-layouts, selective_scan(): lax.scan(jax.checkpoint(first_pass), (zero_state, jnp.ones_like(zero_stat...  124 us
    dynamic_update_slice x16, other arithmetic, selective_scan(): lax.scan(jax.checkpoint(first_pass), (zero_state, jnp.ones_like(zero_stat...  103 us
    reduce_sum x32, other arithmetic, terms_at(): decay = keep_t[:, None, None] * jnp.exp(step_t[:, None, :] * rates[None])  98.2 us
    squeeze x32, local copies, waits for them, and re-layouts, selective_scan(): lax.scan(jax.checkpoint(second_pass), starts, (step_p, inb_p, conv_p, kee...  89.3 us
    reduce_sum x16, other arithmetic, second_pass(): return (state, jnp.sum(item[4][:, :, None] * state, axis=1))  80.5 us
  transfers between devices with their start and end apart: 8, of which 8 were waited for; matrix products, arithmetic and copies ran while one was open for 2% of the time, Pallas kernels for 0%

commit v1 on v0

--- a/solution.py
+++ b/solution.py
@@ -1,15 +1,321 @@
+import functools
 from functools import partial
 
 import jax
 import jax.numpy as jnp
 from jax import lax
+from jax.experimental import pallas as pl
+from jax.experimental.pallas import tpu as pltpu
 from jax.sharding import PartitionSpec as P
-
-SCAN_BLOCK = 16
-
 
 EPS = 1e-06
 HIGH = lax.Precision.HIGHEST
+
+TB = 128
+CH = 16
+LB = 512
+LOG2E = 1.4426950408889634
+LN2 = 0.6931471805599453
+F32 = jnp.float32
+BF16 = jnp.bfloat16
+NN = (((1,), (0,)), ((), ()))
+NT = (((1,), (1,)), ((), ()))
+TN = (((0,), (0,)), ((), ()))
+
+
+def mxu(left, right, dims):
+    return lax.dot_general(left, right, dims, preferred_element_type=F32)
+
+
+def split(x):
+    high = x.astype(BF16)
+    return high, (x - high.astype(F32)).astype(BF16)
+
+
+def dot2(x, w, dims):
+    high, rest = split(x)
+    return mxu(high, w, dims) + mxu(rest, w, dims)
+
+
+def dot3(x, w, dims):
+    high, rest = split(x)
+    high_w, rest_w = split(w)
+    return mxu(high, high_w, dims) + mxu(high, rest_w, dims) + mxu(rest, high_w, dims)
+
+
+def sigmoid(x):
+    return 1.0 / (1.0 + jnp.exp(-x))
+
+
+def softplus(x):
+    return jnp.maximum(x, 0.0) + jnp.log1p(jnp.exp(-jnp.abs(x)))
+
+
+def mid_fwd_kernel(rank, both_ref, mask_ref, vec_ref, wx_ref, wdt_ref, rates_ref,
+                   gated_ref, pre_ref, pdt_ref, y_ref, proj_ref, hs_ref,
+                   ext_ref, conv_ref, h_ref, turned_ref):
+    states, width = rates_ref.shape
+
+    @pl.when(pl.program_id(0) == 0)
+    def _():
+        ext_ref[:8, :] = jnp.zeros((8, width), F32)
+        h_ref[...] = jnp.zeros_like(h_ref)
+
+    @pl.when(pl.program_id(0) > 0)
+    def _():
+        ext_ref[:8, :] = ext_ref[TB:, :]
+
+    def conv_chunk(c, _):
+        rows = pl.ds(pl.multiple_of(c * CH, CH), CH)
+        masks = mask_ref[rows, :]
+        for b in range(width // LB):
+            lanes = slice(b * LB, (b + 1) * LB)
+            ext_ref[pl.ds(pl.multiple_of(c * CH + 8, 8), CH), lanes] = both_ref[rows, lanes]
+            window = ext_ref[pl.ds(pl.multiple_of(c * CH, 8), CH + 8), lanes]
+            total = vec_ref[4:5, lanes] + vec_ref[3:4, lanes] * window[8:]
+            for k in range(1, 4):
+                total = total + vec_ref[3 - k:4 - k, lanes] * window[8 - k:8 - k + CH] * masks[:, k - 1:k]
+            pre_ref[rows, lanes] = total
+            conv_ref[rows, lanes] = total * sigmoid(total)
+        return 0
+
+    lax.fori_loop(0, TB // CH, conv_chunk, 0)
+    proj = dot2(conv_ref[...], wx_ref[...], NN)
+    proj_ref[...] = proj
+    turned_ref[...] = proj.T
+    pdt_ref[...] = dot2(proj, wdt_ref[...], NN) + vec_ref[5:6, :]
+
+    def scan_chunk(c, _):
+        rows = pl.ds(pl.multiple_of(c * CH, CH), CH)
+        tile = pltpu.roll(turned_ref[rank:rank + 2 * states, :], TB - c * CH, 1)
+        keep = mask_ref[rows, 0:1]
+        for b in range(width // LB):
+            lanes = slice(b * LB, (b + 1) * LB)
+            rates = rates_ref[:, lanes]
+            h = h_ref[:, lanes]
+            hs_ref[c, :, lanes] = h
+            conv = conv_ref[rows, lanes]
+            step = softplus(pdt_ref[rows, lanes])
+            source = step * conv
+            step = jnp.where(keep > 0.0, step, 1e4)
+            outs = []
+            for k in range(CH):
+                h = jnp.exp2(step[k:k + 1, :] * rates) * h + tile[:states, k:k + 1] * source[k:k + 1, :]
+                outs.append(jnp.sum(tile[states:, k:k + 1] * h, axis=0, keepdims=True))
+            h_ref[:, lanes] = h
+            y = jnp.concatenate(outs, axis=0)
+            y_ref[rows, lanes] = y
+            gate = both_ref[rows, width + b * LB:width + (b + 1) * LB]
+            gated_ref[rows, lanes] = ((y + vec_ref[6:7, lanes] * conv) * (gate * sigmoid(gate))).astype(BF16)
+        return 0
+
+    lax.fori_loop(0, TB // CH, scan_chunk, 0)
+
+
+def mid_fwd(both, masks, vec, wx, wdt, rates, rank):
+    length = both.shape[0]
+    states, width = rates.shape
+    row = lambda i: (i, 0)
+    fix = lambda i: (0, 0)
+    tall = pl.BlockSpec((TB, width), row)
+    like = jax.ShapeDtypeStruct((length, width), F32)
+    return pl.pallas_call(
+        functools.partial(mid_fwd_kernel, rank),
+        grid=(length // TB,),
+        out_shape=(jax.ShapeDtypeStruct((length, width), BF16), like, like, like,
+                   jax.ShapeDtypeStruct((length, 128), F32),
+                   jax.ShapeDtypeStruct((length // CH, states, width), F32)),
+        in_specs=[pl.BlockSpec((TB, 2 * width), row), pl.BlockSpec((TB, 8), row), pl.BlockSpec(vec.shape, fix),
+                  pl.BlockSpec(wx.shape, fix), pl.BlockSpec(wdt.shape, fix), pl.BlockSpec(rates.shape, fix)],
+        out_specs=(tall, tall, tall, tall, pl.BlockSpec((TB, 128), row),
+                   pl.BlockSpec((TB // CH, states, width), lambda i: (i, 0, 0))),
+        scratch_shapes=[pltpu.VMEM((TB + 8, width), F32), pltpu.VMEM((TB, width), F32),
+                        pltpu.VMEM((states, width), F32), pltpu.VMEM((128, TB), F32)],
+        compiler_params=pltpu.CompilerParams(vmem_limit_bytes=40 << 20),
+        name="mid_fwd",
+    )(both, masks, vec, wx, wdt, rates)
+
+
+def mid_bwd_kernel(rank, both_ref, dg_ref, pre_ref, pdt_ref, y_ref, proj_ref, hs_ref, mask_ref, vec_ref, wxt_ref,
+                   wdt_ref, rates_ref,
+                   dboth_ref, gvec_ref, gwx_ref, gwdt_ref, gr_ref,
+                   ext_ref, g_ref, dec_ref, p_ref, part_ref, dproj_ref, dconv_ref, dpdt_ref, conv_ref, turned_ref,
+                   acc_ref):
+    states, width = rates_ref.shape
+    steps = TB // CH
+
+    @pl.when(pl.program_id(0) == 0)
+    def _():
+        ext_ref[TB:, :] = jnp.zeros((8, width), F32)
+        g_ref[...] = jnp.zeros_like(g_ref)
+        acc_ref[...] = jnp.zeros_like(acc_ref)
+        gwx_ref[...] = jnp.zeros_like(gwx_ref)
+        gwdt_ref[...] = jnp.zeros_like(gwdt_ref)
+        gr_ref[...] = jnp.zeros_like(gr_ref)
+
+    @pl.when(pl.program_id(0) > 0)
+    def _():
+        ext_ref[TB:, :] = ext_ref[:8, :]
+
+    turned_ref[...] = proj_ref[...].T
+    ones = jnp.ones((128, 128), BF16)
+    lane = lax.broadcasted_iota(jnp.int32, (2 * states, 128), 1)
+    place = lax.broadcasted_iota(jnp.int32, (2 * states, 128), 0) + rank
+
+    def fold(x):
+        out = x[:, :128]
+        for i in range(1, LB // 128):
+            out = out + x[:, i * 128:(i + 1) * 128]
+        return out
+
+    def halves(x):
+        out = x[:8]
+        for i in range(1, CH // 8):
+            out = out + x[i * 8:(i + 1) * 8]
+        return out
+
+    def scan_chunk(i, _):
+        c = steps - 1 - i
+        rows = pl.ds(pl.multiple_of(c * CH, CH), CH)
+        tile = pltpu.roll(turned_ref[rank:rank + 2 * states, :], TB - c * CH, 1)
+        keep = mask_ref[rows, 0:1]
+        for b in range(width // LB):
+            lanes = slice(b * LB, (b + 1) * LB)
+            rates = rates_ref[:, lanes]
+            h = hs_ref[c, :, lanes]
+            pre = pre_ref[rows, lanes]
+            conv = pre * sigmoid(pre)
+            conv_ref[rows, lanes] = conv
+            pdt = pdt_ref[rows, lanes]
+            step = softplus(pdt)
+            source = step * conv
+            decay_step = jnp.where(keep > 0.0, step, 1e4)
+            skip = vec_ref[6:7, lanes]
+            gate = both_ref[rows, width + b * LB:width + (b + 1) * LB]
+            sig = sigmoid(gate)
+            dg = dg_ref[rows, lanes]
+            dboth_ref[rows, width + b * LB:width + (b + 1) * LB] = (
+                dg * (y_ref[rows, lanes] + skip * conv) * (sig * (1.0 + gate * (1.0 - sig)))).astype(BF16)
+            dy = dg * (gate * sig)
+            for k in range(CH):
+                dec = jnp.exp2(decay_step[k:k + 1, :] * rates)
+                p = dec * h
+                dec_ref[k] = dec
+                p_ref[k] = p
+                h = p + tile[:states, k:k + 1] * source[k:k + 1, :]
+                out = fold(dy[k:k + 1, :] * h)
+                part_ref[k, states:, :] = out if b == 0 else part_ref[k, states:, :] + out
+            g = g_ref[:, lanes]
+            dr = gr_ref[:, lanes]
+            dus, dss = [None] * CH, [None] * CH
+            for k in reversed(range(CH)):
+                dh = g + tile[states:, k:k + 1] * dy[k:k + 1, :]
+                out = fold(dh * source[k:k + 1, :])
+                part_ref[k, :states, :] = out if b == 0 else part_ref[k, :states, :] + out
+                dus[k] = jnp.sum(dh * tile[:states, k:k + 1], axis=0, keepdims=True)
+                da = dh * p_ref[k]
+                dss[k] = jnp.sum(da * rates, axis=0, keepdims=True)
+                dr = dr + da * decay_step[k:k + 1, :]
+                g = dec_ref[k] * dh
+            g_ref[:, lanes] = g
+            gr_ref[:, lanes] = dr
+            du = jnp.concatenate(dus, axis=0)
+            dpdt = (jnp.concatenate(dss, axis=0) * LN2 + du * conv) * sigmoid(pdt)
+            dpdt_ref[rows, lanes] = dpdt
+            dconv_ref[rows, lanes] = dy * skip + du * step
+            acc_ref[5, :, lanes] += halves(dpdt)
+            acc_ref[6, :, lanes] += halves(dy * conv)
+        high, rest = split(part_ref[...].reshape(CH * 2 * states, 128))
+        sums = (mxu(high, ones, NN) + mxu(rest, ones, NN)).reshape(CH, 2 * states, 128)
+        picked = jnp.where((lane == place)[None], sums, 0.0)
+        dproj_ref[rows, :] = jnp.sum(picked, axis=1)
+        return 0
+
+    lax.fori_loop(0, steps, scan_chunk, 0)
+    dpdt = dpdt_ref[...]
+    dproj = dproj_ref[...] + dot2(dpdt, wdt_ref[...], NT)
+    gwdt_ref[...] += dot3(turned_ref[...], dpdt, NN)
+    gwx_ref[...] += dot3(dproj.T, conv_ref[...], NN)
+    dconv_ref[...] += dot2(dproj, wxt_ref[...], NN)
+
+    def act_chunk(c, _):
+        rows = pl.ds(pl.multiple_of(c * CH, CH), CH)
+        for b in range(width // LB):
+            lanes = slice(b * LB, (b + 1) * LB)
+            pre = pre_ref[rows, lanes]
+            sig = sigmoid(pre)
+            ext_ref[rows, lanes] = dconv_ref[rows, lanes] * (sig * (1.0 + pre * (1.0 - sig)))
+        return 0
+
+    lax.fori_loop(0, steps, act_chunk, 0)
+
+    def conv_chunk(c, _):
+        rows = pl.ds(pl.multiple_of(c * CH, CH), CH)
+        masks = mask_ref[rows, :]
+        for b in range(width // LB):
+            lanes = slice(b * LB, (b + 1) * LB)
+            inner = both_ref[rows, lanes]
+            window = ext_ref[pl.ds(pl.multiple_of(c * CH, 8), CH + 8), lanes]
+            here = window[:CH]
+            total = vec_ref[3:4, lanes] * here
+            acc_ref[4, :, lanes] += halves(here)
+            acc_ref[3, :, lanes] += halves(here * inner)
+            for k in range(1, 4):
+                later = window[k:k + CH] * masks[:, 2 + k:3 + k]
+                total = total + vec_ref[3 - k:4 - k, lanes] * later
+                acc_ref[3 - k, :, lanes] += halves(later * inner)
+            dboth_ref[rows, lanes] = total.astype(BF16)
+        return 0
+
+    lax.fori_loop(0, steps, conv_chunk, 0)
+
+    @pl.when(pl.program_id(0) == pl.num_programs(0) - 1)
+    def _():
+        gvec_ref[...] = jnp.concatenate(
+            [jnp.sum(acc_ref[k], axis=0, keepdims=True) for k in range(8)], axis=0)
+
+
+def mid_bwd(both, dg, pre, pdt, y, proj, hs, masks, vec, wxt, wdt, rates, rank):
+    length = both.shape[0]
+    states, width = rates.shape
+    blocks = length // TB
+    row = lambda i: (blocks - 1 - i, 0)
+    fix = lambda i: (0, 0)
+    tall = pl.BlockSpec((TB, width), row)
+    return pl.pallas_call(
+        functools.partial(mid_bwd_kernel, rank),
+        grid=(blocks,),
+        out_shape=(jax.ShapeDtypeStruct((length, 2 * width), BF16), jax.ShapeDtypeStruct((8, width), F32),
+                   jax.ShapeDtypeStruct((128, width), F32), jax.ShapeDtypeStruct((128, width), F32),
+                   jax.ShapeDtypeStruct((states, width), F32)),
+        in_specs=[pl.BlockSpec((TB, 2 * width), row), tall, tall, tall, tall, pl.BlockSpec((TB, 128), row),
+                  pl.BlockSpec((TB // CH, states, width), lambda i: (blocks - 1 - i, 0, 0)),
+                  pl.BlockSpec((TB, 8), row), pl.BlockSpec(vec.shape, fix), pl.BlockSpec(wxt.shape, fix),
+                  pl.BlockSpec(wdt.shape, fix), pl.BlockSpec(rates.shape, fix)],
+        out_specs=(pl.BlockSpec((TB, 2 * width), row), pl.BlockSpec((8, width), fix),
+                   pl.BlockSpec((128, width), fix), pl.BlockSpec((128, width), fix), pl.BlockSpec((states, width), fix)),
+        scratch_shapes=[pltpu.VMEM((TB + 8, width), F32), pltpu.VMEM((states, width), F32),
+                        pltpu.VMEM((CH, states, LB), F32), pltpu.VMEM((CH, states, LB), F32),
+                        pltpu.VMEM((CH, 2 * states, 128), F32), pltpu.VMEM((TB, 128), F32),
+                        pltpu.VMEM((TB, width), F32), pltpu.VMEM((TB, width), F32), pltpu.VMEM((TB, width), F32),
+                        pltpu.VMEM((128, TB), F32), pltpu.VMEM((8, 8, width), F32)],
+        compiler_params=pltpu.CompilerParams(vmem_limit_bytes=56 << 20),
+        name="mid_bwd",
+    )(both, dg, pre, pdt, y, proj, hs, masks, vec, wxt, wdt, rates)
+
+
+def flags(segment):
+    length = segment.shape[0]
+    cols = []
+    for k in range(1, 4):
+        moved = jnp.concatenate([jnp.full((k,), -2, jnp.int32), segment[:length - k]])
+        cols.append(moved == segment)
+    for k in range(1, 4):
+        moved = jnp.concatenate([segment[k:], jnp.full((k,), -2, jnp.int32)])
+        cols.append(moved == segment)
+    cols.append(segment >= 0)
+    cols.append(segment >= 0)
+    return jnp.stack(cols, axis=1).astype(F32)
 
 
 def prefix(part, axis, combine, identity):
@@ -25,89 +331,6 @@
 
 def rms_scale(values, gain):
     return values * lax.rsqrt(jnp.mean(values * values, axis=-1, keepdims=True) + EPS) * gain
-
-
-def sample_masks(segment, taps):
-    length = segment.shape[0]
-    masks = []
-    for shift in range(taps):
-        earlier = jnp.concatenate([jnp.full((shift,), -2, jnp.int32), segment[: length - shift]])
-        masks.append((earlier == segment).astype(jnp.float32)[:, None])
-    return masks
-
-
-def causal_conv(inner, conv_w, conv_b, masks):
-    taps = conv_w.shape[0]
-    length = inner.shape[0]
-    total = conv_b[None, :] + conv_w[taps - 1][None, :] * inner
-    for shift in range(1, taps):
-        moved = jnp.concatenate(
-            [jnp.zeros((shift, inner.shape[1]), jnp.float32), inner[: length - shift]], axis=0
-        )
-        total = total + conv_w[taps - 1 - shift][None, :] * moved * masks[shift]
-    return total
-
-
-def combine_pairs(first, second):
-    return (first[0] * second[0], second[0] * first[1] + second[1])
-
-
-def to_blocks(values, blocks):
-    length = values.shape[0]
-    return jnp.swapaxes(values.reshape((blocks, length // blocks) + values.shape[1:]), 0, 1)
-
-
-def selective_scan(step, in_b, out_c, conv, keep, rates):
-    length, width = conv.shape
-    blocks = length // SCAN_BLOCK
-    states = rates.shape[0]
-    step_p = to_blocks(step, blocks)
-    inb_p = to_blocks(in_b, blocks)
-    outc_p = to_blocks(out_c, blocks)
-    conv_p = to_blocks(conv, blocks)
-    keep_p = to_blocks(keep, blocks)
-
-    def terms_at(step_t, inb_t, conv_t, keep_t):
-        decay = keep_t[:, None, None] * jnp.exp(step_t[:, None, :] * rates[None])
-        source = inb_t[:, :, None] * (step_t * conv_t)[:, None, :]
-        return (decay, source)
-
-    def first_pass(carry, item):
-        decay, source = terms_at(item[0], item[1], item[2], item[3])
-        return ((decay * carry[0] + source, decay * carry[1]), None)
-
-    zero_state = jnp.zeros((blocks, states, width), jnp.float32)
-    (block_ends, products), _ = lax.scan(
-        jax.checkpoint(first_pass),
-        (zero_state, jnp.ones_like(zero_state)),
-        (step_p, inb_p, conv_p, keep_p),
-    )
-    _, reached = lax.associative_scan(combine_pairs, (products, block_ends), axis=0)
-    starts = jnp.concatenate([jnp.zeros_like(reached[:1]), reached[:-1]], axis=0)
-
-    def second_pass(state, item):
-        decay, source = terms_at(item[0], item[1], item[2], item[3])
-        state = decay * state + source
-        return (state, jnp.sum(item[4][:, :, None] * state, axis=1))
-
-    _, outputs = lax.scan(
-        jax.checkpoint(second_pass), starts, (step_p, inb_p, conv_p, keep_p, outc_p)
-    )
-    return jnp.swapaxes(outputs, 0, 1).reshape(length, width)
-
-
-def middle(inner, gate_z, conv_w, conv_b, w_x, w_dt, b_dt, a_log, d_skip, masks):
-    conv = jax.nn.silu(causal_conv(inner, conv_w, conv_b, masks))
-    proj = jnp.dot(conv, w_x, precision=HIGH)
-    rank_dt = w_dt.shape[0]
-    states = a_log.shape[0]
-    step = jax.nn.softplus(jnp.dot(proj[:, :rank_dt], w_dt, precision=HIGH) + b_dt)
-    in_b = proj[:, rank_dt : rank_dt + states]
-    out_c = proj[:, rank_dt + states :]
-    rates = -jnp.exp(a_log)
-    ssm_out = selective_scan(step, in_b, out_c, conv, masks[1][:, 0], rates)
-    result = ssm_out + d_skip * conv
-    return result * jax.nn.silu(gate_z)
 
 
 def add_counts(earlier, later):
@@ -149,30 +372,19 @@
     capacity = 5 * length * lax.axis_size("ep") * lax.axis_size("tp") // (4 * experts)
     token_f = tokens.astype(jnp.float32)
     valid = (segment >= 0).astype(jnp.float32)[:, None]
-    masks = sample_masks(segment, conv_w.shape[0])
-    small_f = [
-        item.astype(jnp.float32) for item in (conv_w, conv_b, w_x, w_dt, b_dt, a_log, d_skip)
-    ]
+    rank_dt, states = w_dt.shape[0], a_log.shape[0]
+    masks = flags(segment)
+    vec = jnp.concatenate([conv_w, conv_b[None], b_dt[None], d_skip[None], d_skip[None]], axis=0).astype(F32)
+    wx_pad = jnp.pad(w_x, ((0, 0), (0, 128 - rank_dt - 2 * states)))
+    wdt_pad = jnp.pad(w_dt, ((0, 128 - rank_dt), (0, 0)))
+    rates = -jnp.exp(a_log.astype(F32))
     normed_one, norm_one_pull = jax.vjp(rms_scale, token_f, gain_one.astype(jnp.float32))
     normed_low = normed_one.astype(jnp.bfloat16)
     both = jnp.dot(normed_low, w_in, preferred_element_type=jnp.float32)
 
-    def middle_fixed(inner, gate_z, conv_wf, conv_bf, w_xf, w_dtf, b_dtf, a_logf, d_skipf):
-        return middle(inner, gate_z, conv_wf, conv_bf, w_xf, w_dtf, b_dtf, a_logf, d_skipf, masks)
-
-    gated, middle_pull = jax.vjp(
-        middle_fixed,
-        both[:, :inner_w],
-        both[:, inner_w:],
-        small_f[0],
-        small_f[1],
-        small_f[2],
-        small_f[3],
-        small_f[4],
-        small_f[5],
-        small_f[6],
-    )
-    gated_low = gated.astype(jnp.bfloat16)
+    gated_low, pre, pre_dt, scanned, proj, starts = mid_fwd(
+        both, masks, vec, wx_pad, wdt_pad, rates * LOG2E, rank_dt
+    )
     mixed = jnp.dot(gated_low, w_out, preferred_element_type=jnp.float32)
     after_mix = token_f + mixed * valid
     normed_two, norm_two_pull = jax.vjp(rms_scale, after_mix, gain_two.astype(jnp.float32))
@@ -225,9 +437,7 @@
     d_gate = keep_f[:, 0] * jnp.sum(upstream * token_out, axis=1)
     d_received = lax.all_to_all(d_slots, "ep", split_axis=0, concat_axis=2, tiled=True)
     d_rows_all = lax.all_gather(d_received, "tp", axis=2, tiled=True)
-    again = jnp.einsum("axrd,xdf->axrf", expert_rows, full_up, preferred_element_type=jnp.float32)
-    again_value, gelu_back = jax.vjp(partial(jax.nn.gelu, approximate=False), again)
-    hidden_back = again_value.astype(jnp.bfloat16)
+    gelu_back, hidden_back = gelu_pull, hidden_low
     grad_down = jnp.einsum(
         "axrf,axrd->xfd", hidden_back, d_rows_all, preferred_element_type=jnp.float32
     )
@@ -250,8 +460,13 @@
     d_gated = lax.dot_general(
         d_mixed, w_out, (((1,), (1,)), ((), ())), preferred_element_type=jnp.float32
     )
-    middle_grads = middle_pull(d_gated)
-    d_both = jnp.concatenate([middle_grads[0], middle_grads[1]], axis=1).astype(jnp.bfloat16)
+    d_both, grad_vec, grad_x, grad_dt, grad_rates = mid_bwd(
+        both, d_gated, pre, pre_dt, scanned, proj, starts, masks, vec, wx_pad.T, wdt_pad, rates * LOG2E, rank_dt
+    )
+    middle_grads = (
+        grad_vec[: conv_w.shape[0]], grad_vec[4], grad_x[: rank_dt + 2 * states].T, grad_dt[:rank_dt], grad_vec[5],
+        grad_rates * rates, grad_vec[6],
+    )
     grad_in = contract_rows(normed_low, d_both)
     d_normed_one = lax.dot_general(
         d_both, w_in, (((1,), (1,)), ((), ())), preferred_element_type=jnp.float32
@@ -264,13 +479,13 @@
         (
             grad_gain_one,
             grad_in,
+            middle_grads[0],
+            middle_grads[1],
             middle_grads[2],
             middle_grads[3],
             middle_grads[4],
             middle_grads[5],
             middle_grads[6],
-            middle_grads[7],
-            middle_grads[8],
             grad_out,
             grad_gain_two,
             grad_router,

time: 2540 us -> 1380 us (0.54)
  local copies, waits for them, and re-layouts: 676 us -> 55.1 us
  other arithmetic: 638 us -> 21.7 us
  Pallas kernels: 0 us -> 112 us
    squeeze x144 -> x0, local copies, waits for them, and re-layouts: 213 us -> none  [the longest x112 124 us: selective_scan(): lax.scan(jax.checkpoint(first_pass), (zero_state, jnp.ones_like(zero_stat...]
    mul x110 -> x2, other arithmetic: 209 us -> 1.49 us  [the longest x1 0.82 us: local(): rates * LOG2E]
    reduce_sum x50 -> x0, other arithmetic: 185 us -> none  [the longest x32 98.2 us: terms_at(): decay = keep_t[:, None, None] * jnp.exp(step_t[:, None, :] * rates[None])]
    dynamic_update_slice x48 -> x0, other arithmetic: 130 us -> none  [the longest x16 103 us: selective_scan(): lax.scan(jax.checkpoint(first_pass), (zero_state, jnp.ones_like(zero_stat...]
    pad x32 -> x2, local copies, waits for them, and re-layouts: 124 us -> 1.02 us  [the longest x1 0.94 us: local(): wdt_pad = jnp.pad(w_dt, ((0, 128 - rank_dt), (0, 0)))]
    pallas_call x0 -> x2, Pallas kernels: none -> 112 us  [the longest x1 76.8 us: mid_bwd(): pl.pallas_call(functools.partial(mid_bwd_kernel, rank), grid=(blocks,), o...]
    dynamic_update_slice x80 -> x0, local copies, waits for them, and re-layouts: 102 us -> none  [the longest x16 62.2 us: selective_scan(): lax.scan(jax.checkpoint(first_pass), (zero_state, jnp.ones_like(zero_stat...]
    another operation x15 -> x12, local copies, waits for them, and re-layouts: 62 us -> 0.27 us  [the longest x9 0.26 us: flags(): return jnp.stack(cols, axis=1).astype(F32)]
  transfers between devices with their start and end apart: 8 -> 8, of which waited for: 8 -> 8; matrix products, arithmetic and copies ran while one was open for 2% -> 4% of each run, Pallas kernels for 0% -> 0%
where the time goes in v1:
time: 1380 us; the launch traced here: 1370 us
  waiting for transfers between devices  909 us (66%)
  matrix products  144 us (10%)
  Pallas kernels  112 us (8%)
  blocking collectives  105 us (8%)
  local copies, waits for them, and re-layouts  55.1 us (4%)
  other arithmetic  21.7 us (2%)
  between operations  15.2 us (1%)
    psum x2, waiting for transfers between devices, local(): lax.psum((grad_gain_one, grad_in, middle_grads[0], middle_grads[1], middl...  629 us
    reduce_scatter x1, waiting for transfers between devices, local(): expert_out = lax.psum_scatter(terms, 'tp', scatter_dimension=2, tiled=True)  78.2 us
    reduce_scatter x1, waiting for transfers between devices, local(): lax.psum_scatter(row_terms, 'tp', scatter_dimension=2, tiled=True)  78.2 us
    pallas_call x1, Pallas kernels, mid_bwd(): pl.pallas_call(functools.partial(mid_bwd_kernel, rank), grid=(blocks,), o...  76.8 us
    unnamed x1, blocking collectives  40.6 us
    all_gather x1, waiting for transfers between devices, local(): expert_rows = lax.all_gather(received, 'tp', axis=2, tiled=True)  38.5 us
    all_gather x1, waiting for transfers between devices, local(): d_rows_all = lax.all_gather(d_received, 'tp', axis=2, tiled=True)  36.8 us
    pallas_call x1, Pallas kernels, mid_fwd(): pl.pallas_call(functools.partial(mid_fwd_kernel, rank), grid=(length // T...  34.9 us
  transfers between devices with their start and end apart: 8, of which 8 were waited for; matrix products, arithmetic and copies ran while one was open for 4% of the time, Pallas kernels for 0%

profile of v1, /device:TPU:1, one launch (start us, length us, event | category | flops | bytes accessed | tf_op | source)
XLA Modules:
  0.0 1372.6 jit_solution(4122133744129162204)
XLA Ops:
  7.3 0.9 fusion.94
  8.2 0.8 fusion.92
  9.8 1.4 fusion.35
  14.5 40.6 %all-reduce.6 = s32[512]{0:T(512)S(1)} all-reduce(s32[512]{0:T(512)S(1)} %dynamic-update-slice), channel_id=2, replica_groups=mesh['ep'=8,'tp'=4] {'ep','tp'}, use_global_device_ids=true, to_apply=%add.6 | all-reduce | flops 512 | bytes 4096
  58.8 1.1 reduce-window.6
  63.3 1.3 copy.83
  64.6 0.9 pad.13.wdt_ref
  65.7 8.0 fusion.61.both_ref
  73.7 34.9 %mid_fwd.1 = (bf16[512,1536]{1,0:T(8,128)(2,1)S(1)}, f32[512,1536]{1,0:T(8,128)S(1)}, f32[512,1536]{1,0:T(8,128)S(1)}, f32[512,1536]{1,0:T(8,128)S(1)}, f32[512,128]{1,0:T(8,128)S(1)}, /*index=5*/f32[32,16,1536]{2,1,0:T(8,128)}) custom-call(f32[512,3072]{1,0:T(8,128)} %fusion.61.both_ref, f32[512,8]{1,0:T(8,128)S(1)} %convert_element_type.86.mask_ref, ...), custom_call_target="tpu_custom_call" | custom-call | tf_op jit(solution)/shard_map/mid_fwd/pallas_call | solution.py:122
  108.7 1.7 copy-done.3
  110.3 1.7 copy-done.4
  112.0 1.6 copy-done.5
  113.6 1.2 copy-done.6
  114.8 1.5 multiply_reduce_fusion.2
  116.4 1.1 copy-done.12
  117.5 1.0 fusion.41
  118.4 31.9 %all_to_all.66 = bf16[8,2,48,768]{3,2,1,0:T(8,128)(2,1)S(1)} all-to-all(bf16[8,2,48,768]{3,2,1,0:T(8,128)(2,1)S(1)} %bitcast.192), channel_id=1, replica_groups=mesh['ep'=8,'tp'=4] {'ep'}, dimensions={0} | all-to-all | bytes 2359296 | tf_op jit(solution)/shard_map/all_to_all | solution.py:413
  150.4 1.1 copy.69
  151.8 38.5 %all-gather.4.cloned.1.call-done = bf16[1,2,1536,768]{3,2,1,0:T(8,128)(2,1)} async-done(((bf16[1,2,384,768]{3,2,1,0:T(8,128)(2,1)}), bf16[1,2,1536,768]{3,2,1,0:T(8,128)(2,1)}) %all-gather.4.cloned.1.call-update) | async-done | bytes 4718608 | tf_op jit(solution)/shard_map/all_gather | solution.py:415
  190.4 6.4 fusion.26
  196.8 3.7 copy-done.67
  200.5 25.9 %convolution_bitcast_fusion.1 = f32[1,2,1536,768]{3,2,1,0:T(8,128)} fusion(bf16[2,768,768]{2,1,0:T(8,128)(2,1)S(1)} %copy-done, f32[2,1536,768]{2,1,0:T(8,128)S(1)} %fusion.26), kind=kOutput, calls=%fused_computation.29 | convolution fusion | flops 3777232896 | bytes 21233664 | tf_op jit(solution)/shard_map/axrf,xfd->axrd/dot_general | solution.py:421
  226.5 78.2 %reduce-scatter.3.cloned.1.call-done = f32[1,2,384,768]{3,2,1,0:T(8,128)} async-done(((f32[1,2,1536,768]{3,2,1,0:T(8,128)}), f32[1,2,384,768]{3,2,1,0:T(8,128)}) %reduce-scatter.3.cloned.1.call-update) | async-done | bytes 2359312 | tf_op jit(solution)/shard_map/reduce_scatter | solution.py:422
  304.6 1.8 convert_element_type.97
  306.4 2.2 copy.70
  308.7 5.2 all-to-all-start.1
  313.9 2.4 fusion.95
  317.6 24.0 %all-to-all-done.1 = bf16[1,2,384,768]{3,1,0,2:T(2,128)(2,1)S(1)} async-done(((bf16[1,2,384,768]{3,1,0,2:T(2,128)(2,1)}), bf16[1,2,384,768]{3,1,0,2:T(2,128)(2,1)S(1)}, u32[]{:S(2)}, u32[]{:S(2)}) %all-to-all-start.1) | async-done | bytes 1179680 | tf_op jit(solution)/shard_map/all_to_all | solution.py:423
  341.8 3.2 fusion.33
  345.7 1.4 fusion.72
  347.7 2.1 fusion.42
  349.8 32.1 %all_to_all.67 = bf16[8,2,48,768]{3,2,1,0:T(8,128)(2,1)S(1)} all-to-all(bf16[8,2,48,768]{3,2,1,0:T(8,128)(2,1)S(1)} %bitcast.193), channel_id=1, replica_groups=mesh['ep'=8,'tp'=4] {'ep'}, dimensions={0} | all-to-all | bytes 2359296 | tf_op jit(solution)/shard_map/all_to_all | solution.py:438
  381.9 1.1 copy.73
  383.6 36.8 %all-gather.6.cloned.1.call-done = bf16[1,2,1536,768]{3,2,1,0:T(8,128)(2,1)} async-done(((bf16[1,2,384,768]{3,2,1,0:T(8,128)(2,1)}), bf16[1,2,1536,768]{3,2,1,0:T(8,128)(2,1)}) %all-gather.6.cloned.1.call-update) | async-done | bytes 4718608 | tf_op jit(solution)/shard_map/all_gather | solution.py:439
  420.4 26.3 %fusion.6 = bf16[1,2,1536,768]{3,2,1,0:T(8,128)(2,1)S(1)} fusion(f32[2,1536,768]{2,1,0:T(8,128)} %copy-done.67, bf16[2,768,768]{2,1,0:T(8,128)(2,1)S(1)} %copy-done, bf16[1,2,1536,768]{3,2,1,0:T(8,128)(2,1)} %all-gather.6.cloned.1.call-done), kind=kOutput, calls=%fused_computation.10 | convolution fusion | flops 3793747968 | bytes 21233664 | tf_op jit(solution)/shard_map/axrd,xfd->axrf/dot_general | solution.py:444
  446.7 2.2 copy-done.68
  448.9 6.3 convolution_bitcast_fusion
  455.4 78.2 %reduce-scatter.5.cloned.1.call-done = f32[1,2,384,768]{3,2,1,0:T(8,128)} async-done(((f32[1,2,1536,768]{3,2,1,0:T(8,128)}), f32[1,2,384,768]{3,2,1,0:T(8,128)}) %reduce-scatter.5.cloned.1.call-update) | async-done | bytes 2359312 | tf_op jit(solution)/shard_map/reduce_scatter | solution.py:450
  533.5 1.8 convert_element_type.103
  535.3 2.2 copy.74
  537.5 5.4 all-to-all-start.3
  544.7 1.7 fusion.43
  546.4 24.2 %all-to-all-done.3 = bf16[1,2,384,768]{3,1,0,2:T(2,128)(2,1)S(1)} async-done(((bf16[1,2,384,768]{3,1,0,2:T(2,128)(2,1)}), bf16[1,2,384,768]{3,1,0,2:T(2,128)(2,1)S(1)}, u32[]{:S(2)}, u32[]{:S(2)}) %all-to-all-start.3) | async-done | bytes 1179680 | tf_op jit(solution)/shard_map/all_to_all | solution.py:451
  570.9 0.9 fusion.37
  571.8 1.7 multiply_reduce_fusion
  573.5 1.4 convert_add_fusion.1
  575.0 1.1 copy-done.14
  576.1 3.1 fusion.86.dg_ref
  579.2 76.8 %mid_bwd.1 = (bf16[512,3072]{1,0:T(8,128)(2,1)}, f32[8,1536]{1,0:T(8,128)}, f32[128,1536]{1,0:T(8,128)}, f32[128,1536]{1,0:T(8,128)}, f32[16,1536]{1,0:T(8,128)}) custom-call(f32[512,3072]{1,0:T(8,128)} %fusion.61.both_ref, f32[512,1536]{1,0:T(8,128)} %fusion.86.dg_ref, f32[512,1536]{1,0:T(8,128)} %copy-done.3, f32[512,1536]{1,0:T(8,128)} %copy-done.4, ...), custom_call_target="tpu_custom_call" | custom-call | tf_op jit(solution)/shard_map/mid_bwd/pallas_call | solution.py:285
  656.0 1.6 slice.50
  657.6 1.6 slice_reduce_fusion.1
  659.2 6.4 fusion.31
  665.6 5.4 fusion.59
  672.8 5.1 fusion.85
  677.8 1.7 slice.53
  679.6 9.9 fusion.19
  689.5 26.3 %fusion.22 = f32[2,768,768]{2,1,0:T(8,128)} fusion(bf16[1,2,1536,768]{3,2,1,0:T(8,128)(2,1)} %all-gather.6.cloned.1.call-done, f32[2,1536,768]{2,1,0:T(8,128)} %copy-done.67), kind=kOutput, calls=%fused_computation.34 | convolution fusion | flops 3777232896 | bytes 18874368 | tf_op jit(solution)/shard_map/axrf,axrd->xfd/dot_general | solution.py:441
  715.8 1.6 fusion.34
  717.4 78.3 %all-reduce.12.cloned.1.call-done = (f32[2,16]{1,0:T(2,128)}, f32[768]{0:T(1024)}, f32[4,1536]{1,0:T(4,128)}, f32[1536]{0:T(1024)}, f32[1536]{0:T(1024)}, /*inde...) async-done(((f32[2,16]{1,0:T(2,128)}, f32[768]{0:T(1024)}, f32[4,1536]{1,0:T(4,128)}, f32[1536]{0:T(1024)}, f32[1536]{0:T(1024)}, /*index=5*/f32[1536]{0:T(1024)}, ...) | async-done | bytes 98448 | tf_op jit(solution)/shard_map/psum | solution.py:478
  795.7 1.2 convert_element_type.107
  796.9 550.5 %all-reduce.14.cloned.1.call-done = (f32[768,3072]{1,0:T(8,128)}, f32[1536,80]{0,1:T(8,128)}, f32[48,1536]{1,0:T(8,128)}, f32[16,1536]{1,0:T(8,128)}, f32[1536,768]{1,0:T(8,128)}) async-done(((f32[768,3072]{1,0:T(8,128)}, f32[1536,80]{0,1:T(8,128)}, f32[48,1536]{1,0:T(8,128)}, f32[16,1536]{1,0:T(8,128)}, f32[1536,768]{1,0:T(8,128)}), (f32[768,3072]{1,0:T(8,128)}, f32[1536,80]{0,1:T(8,128)}, ...) | async-done | bytes 15040528 | tf_op jit(solution)/shard_map/psum | solution.py:478
  1347.4 1.3 copy.104
  1348.7 8.8 copy.105
  1362.0 2.2 copy.113
  (209 shorter events, 24.7 us)
Async XLA Ops:
  7.2 193.3 %copy-start = (bf16[2,768,768]{2,1,0:T(8,128)(2,1)S(1)}, bf16[2,768,768]{2,1,0:T(8,128)(2,1)}, u32[]{:S(2)}) copy-start(bf16[2,768,768]{2,1,0:T(8,128)(2,1)} %param.37) | copy-start | bytes 7077892
  7.2 183.1 %all-gather.4.cloned.1.call-start = ((), (), s32[]{:S(2)}) async-start(), calls=%async_computation.6 | async-start | bytes 5898240 | tf_op jit(solution)/shard_map/all_gather | solution.py:415
  11.2 97.4 %copy-start.32 = (f32[512]{0:T(512)}, f32[512]{0:T(512)S(1)}, u32[]{:S(2)}) copy-start(f32[512]{0:T(512)S(1)} %fusion.81) | copy-start | bytes 6148
  12.6 96.0 %copy-start.29 = (f32[768]{0:T(1024)}, f32[768]{0:T(1024)S(1)}, u32[]{:S(2)}) copy-start(f32[768]{0:T(1024)S(1)} %convert_element_type.84) | copy-start | bytes 9220
  13.4 95.2 %copy-start.39 = (pred[512]{0:T(512)(128)(4,1)}, pred[512]{0:T(512)(128)(4,1)S(1)}, u32[]{:S(2)}) copy-start(pred[512]{0:T(512)(128)(4,1)S(1)} %get-tuple-element.98) | copy-start | bytes 1540
  13.4 100.3 %copy-start.57 = (f32[512]{0:T(512)}, f32[512]{0:T(512)S(1)}, u32[]{:S(2)}) copy-start(f32[512]{0:T(512)S(1)} %get-tuple-element.97) | copy-start | bytes 6148
  14.2 40.8 %copy-start.62 = (s32[16]{0:T(128)}, s32[16]{0:T(128)S(1)}, u32[]{:S(2)}) copy-start(s32[16]{0:T(128)S(1)} %convert_reduce_fusion) | copy-start | bytes 196
  58.0 50.5 %copy-start.10 = (f32[8,1536]{1,0:T(8,128)}, f32[8,1536]{1,0:T(8,128)S(1)}, u32[]{:S(2)}) copy-start(f32[8,1536]{1,0:T(8,128)S(1)} %convert_element_type.87.vec_ref) | copy-start | bytes 147460
  61.5 47.1 %copy-start.49 = (pred[512]{0:T(512)(128)(4,1)}, pred[512]{0:T(512)(128)(4,1)S(1)}, u32[]{:S(2)}) copy-start(pred[512]{0:T(512)(128)(4,1)S(1)} %get-tuple-element.96) | copy-start | bytes 1540
  62.2 54.1 %copy-start.60 = (s32[512]{0:T(512)}, s32[512]{0:T(512)S(1)}, u32[]{:S(2)}) copy-start(s32[512]{0:T(512)S(1)} %add_select_fusion) | copy-start | bytes 6148
  63.3 45.3 %copy-start.9 = (f32[16,1536]{1,0:T(8,128)}, f32[16,1536]{1,0:T(8,128)S(1)}, u32[]{:S(2)}) copy-start(f32[16,1536]{1,0:T(8,128)S(1)} %fusion.64.rates_ref) | copy-start | bytes 294916
  63.3 45.3 %copy-start.8 = (f32[512,8]{1,0:T(8,128)}, f32[512,8]{1,0:T(8,128)S(1)}, u32[]{:S(2)}) copy-start(f32[512,8]{1,0:T(8,128)S(1)} %convert_element_type.86.mask_ref) | copy-start | bytes 49156
  65.6 43.1 %copy-start.2 = (bf16[128,1536]{1,0:T(8,128)(2,1)}, bf16[128,1536]{1,0:T(8,128)(2,1)S(1)}, u32[]{:S(2)}) copy-start(bf16[128,1536]{1,0:T(8,128)(2,1)S(1)} %pad.13.wdt_ref) | copy-start | bytes 1179652
  65.6 49.1 %copy-start.16 = (bf16[512,768]{1,0:T(8,128)(2,1)S(1)}, bf16[512,768]{1,0:T(8,128)(2,1)}, u32[]{:S(2)}) copy-start(bf16[512,768]{1,0:T(8,128)(2,1)} %param.20) | copy-start | bytes 2359300
  65.7 49.1 %copy-start.65 = (bf16[1536,768]{1,0:T(8,128)(2,1)S(1)}, bf16[1536,768]{1,0:T(8,128)(2,1)}, u32[]{:S(2)}) copy-start(bf16[1536,768]{1,0:T(8,128)(2,1)} %param.33) | copy-start | bytes 7077892
  116.3 35.1 %copy-start.50 = (f32[512]{0:T(512)}, f32[512]{0:T(512)S(1)}, u32[]{:S(2)}) copy-start(f32[512]{0:T(512)S(1)} %get-tuple-element.113) | copy-start | bytes 6148
  151.5 153.2 %reduce-scatter.3.cloned.1.call-start = ((), (), s32[]{:S(2)}) async-start(), calls=%async_computation.7 | async-start | bytes 11796480 | tf_op jit(solution)/shard_map/reduce_scatter | solution.py:422
  226.5 119.2 %copy-start.34 = (s32[512,1]{0,1:T(1,128)S(1)}, s32[512,1]{0,1:T(1,128)}, u32[]{:S(2)}) copy-start(s32[512,1]{0,1:T(1,128)} %param.23) | copy-start | bytes 6148
  308.7 32.9 %all-to-all-start.1 = ((bf16[1,2,384,768]{3,1,0,2:T(2,128)(2,1)}), bf16[1,2,384,768]{3,1,0,2:T(2,128)(2,1)S(1)}, u32[]{:S(2)}, u32[]{:S(2)}) async-start(bf16[1,2,384,768]{3,1,0,2:T(2,128)(2,1)} %copy.70), calls=%async_computation.2 | async-start | bytes 2359296 | tf_op jit(solution)/shard_map/all_to_all | solution.py:423
  313.9 106.5 %all-gather.6.cloned.1.call-start = ((), (), s32[]{:S(2)}) async-start(), calls=%async_computation.8 | async-start | bytes 5898240 | tf_op jit(solution)/shard_map/all_gather | solution.py:439
  383.1 150.5 %reduce-scatter.5.cloned.1.call-start = ((), (), s32[]{:S(2)}) async-start(), calls=%async_computation.9 | async-start | bytes 11796480 | tf_op jit(solution)/shard_map/reduce_scatter | solution.py:450
  420.4 28.5 %copy-start.64 = (bf16[2,768,768]{2,1,0:T(8,128)(2,1)S(1)}, bf16[2,768,768]{2,1,0:T(8,128)(2,1)}, u32[]{:S(2)}) copy-start(bf16[2,768,768]{2,1,0:T(8,128)(2,1)} %param.36) | copy-start | bytes 7077892
  455.3 87.9 %copy-start.40 = (pred[512]{0:T(512)(128)(4,1)S(1)}, pred[512]{0:T(512)(128)(4,1)}, u32[]{:S(2)}) copy-start(pred[512]{0:T(512)(128)(4,1)} %copy-done.39) | copy-start | bytes 1540
  455.3 87.9 %copy-start.52 = (s32[512]{0:T(512)S(1)}, s32[512]{0:T(512)}, u32[]{:S(2)}) copy-start(s32[512]{0:T(512)} %get-tuple-element.95) | copy-start | bytes 6148
  455.3 88.0 %copy-start.63 = (s32[16]{0:T(128)S(1)}, s32[16]{0:T(128)}, u32[]{:S(2)}) copy-start(s32[16]{0:T(128)} %copy-done.62) | copy-start | bytes 196
  455.3 88.6 %copy-start.22 = (bf16[1536,80]{0,1:T(8,128)(2,1)S(1)}, bf16[1536,80]{0,1:T(8,128)(2,1)}, u32[]{:S(2)}) copy-start(bf16[1536,80]{0,1:T(8,128)(2,1)} %param.28) | copy-start | bytes 737284
  455.3 89.4 %copy-start.53 = (f32[512]{0:T(512)S(1)}, f32[512]{0:T(512)}, u32[]{:S(2)}) copy-start(f32[512]{0:T(512)} %get-tuple-element.70) | copy-start | bytes 6148
  455.3 89.4 %copy-start.13 = (f32[512,768]{1,0:T(8,128)S(1)}, f32[512,768]{1,0:T(8,128)}, u32[]{:S(2)}) copy-start(f32[512,768]{1,0:T(8,128)} %copy-done.12) | copy-start | bytes 4718596
  455.3 89.3 %copy-start.24 = (f32[512,16]{0,1:T(8,128)S(1)}, f32[512,16]{0,1:T(8,128)}, u32[]{:S(2)}) copy-start(f32[512,16]{0,1:T(8,128)} %copy-done.23) | copy-start | bytes 98308
  455.3 89.3 %copy-start.38 = (f32[512]{0:T(512)S(1)}, f32[512]{0:T(512)}, u32[]{:S(2)}) copy-start(f32[512]{0:T(512)} %fusion.79) | copy-start | bytes 6148
  455.3 89.3 %copy-start.43 = (f32[512]{0:T(512)S(1)}, f32[512]{0:T(512)}, u32[]{:S(2)}) copy-start(f32[512]{0:T(512)} %copy-done.42) | copy-start | bytes 6148
  455.4 115.5 %copy-start.61 = (s32[512]{0:T(512)S(1)}, s32[512]{0:T(512)}, u32[]{:S(2)}) copy-start(s32[512]{0:T(512)} %copy-done.60) | copy-start | bytes 6148
  535.3 36.5 %copy-start.35 = (bf16[768,16]{0,1:T(8,128)(2,1)S(1)}, bf16[768,16]{0,1:T(8,128)(2,1)}, u32[]{:S(2)}) copy-start(bf16[768,16]{0,1:T(8,128)(2,1)} %param.35) | copy-start | bytes 73732
  537.5 35.9 %copy-start.51 = (f32[512]{0:T(512)S(1)}, f32[512]{0:T(512)}, u32[]{:S(2)}) copy-start(f32[512]{0:T(512)} %copy-done.50) | copy-start | bytes 6148
  537.5 36.0 %copy-start.48 = (f32[512]{0:T(512)S(1)}, f32[512]{0:T(512)}, u32[]{:S(2)}) copy-start(f32[512]{0:T(512)} %copy-done.47) | copy-start | bytes 6148
  537.5 33.1 %all-to-all-start.3 = ((bf16[1,2,384,768]{3,1,0,2:T(2,128)(2,1)}), bf16[1,2,384,768]{3,1,0,2:T(2,128)(2,1)S(1)}, u32[]{:S(2)}, u32[]{:S(2)}) async-start(bf16[1,2,384,768]{3,1,0,2:T(2,128)(2,1)} %copy.74), calls=%async_computation.5 | async-start | bytes 2359296 | tf_op jit(solution)/shard_map/all_to_all | solution.py:451
  542.9 252.8 %all-reduce.12.cloned.1.call-start = ((), (), s32[]{:S(2)}) async-start(), calls=%async_computation.10 | async-start | bytes 215040 | tf_op jit(solution)/shard_map/psum | solution.py:478
  570.8 5.3 copy-start.58
  570.8 5.3 copy-start.66
  576.1 83.0 %slice-start = ((s8[4718592]{0:T(1024)(128)(4,1)}), s8[4194304]{0:T(1024)(128)(4,1)S(1)}, s32[]{:S(2)}) async-start(s8[4718592]{0:T(1024)(128)(4,1)} %bitcast.204), calls=%async_computation.12 | async-start | bytes 8388608
  579.2 79.9 %copy-start.17 = (bf16[512,768]{1,0:T(8,128)(2,1)S(1)}, bf16[512,768]{1,0:T(8,128)(2,1)}, u32[]{:S(2)}) copy-start(bf16[512,768]{1,0:T(8,128)(2,1)} %param.20) | copy-start | bytes 2359300
  579.2 79.9 %copy-start.30 = (f32[768]{0:T(1024)S(1)}, f32[768]{0:T(1024)}, u32[]{:S(2)}) copy-start(f32[768]{0:T(1024)} %copy-done.29) | copy-start | bytes 9220
  579.2 79.9 %copy-start.33 = (f32[512]{0:T(512)S(1)}, f32[512]{0:T(512)}, u32[]{:S(2)}) copy-start(f32[512]{0:T(512)} %copy-done.32) | copy-start | bytes 6148
  579.2 79.9 %slice-start.1 = ((s8[4718592]{0:T(1024)(128)(4,1)}), s8[524288]{0:T(1024)(128)(4,1)S(1)}, s32[]{:S(2)}) async-start(s8[4718592]{0:T(1024)(128)(4,1)} %bitcast.204), calls=%async_computation.13 | async-start | bytes 1048576
  656.0 9.6 copy-start.19
  665.5 5.4 copy-start.27
  665.5 6.2 copy-start.31
  665.5 6.2 copy-start.37
  665.6 7.2 copy-start.7
  672.4 674.9 %all-reduce.14.cloned.1.call-start = ((), (), s32[]{:S(2)}) async-start(), calls=%async_computation.11 | async-start | bytes 30081024 | tf_op jit(solution)/shard_map/psum | solution.py:478
  689.5 26.3 %copy-start.46 = (f32[512]{0:T(512)S(1)}, f32[512]{0:T(512)}, u32[]{:S(2)}) copy-start(f32[512]{0:T(512)} %copy-done.45) | copy-start | bytes 6148
  689.5 26.3 %copy-start.15 = (f32[512,768]{1,0:T(8,128)S(1)}, f32[512,768]{1,0:T(8,128)}, u32[]{:S(2)}) copy-start(f32[512,768]{1,0:T(8,128)} %copy-done.14) | copy-start | bytes 4718596
  689.5 26.3 %copy-start.21 = (f32[512,768]{1,0:T(8,128)S(1)}, f32[512,768]{1,0:T(8,128)}, u32[]{:S(2)}) copy-start(f32[512,768]{1,0:T(8,128)} %get-tuple-element.120) | copy-start | bytes 4718596
  1348.6 8.8 copy-start.44
  1348.6 9.4 copy-start.56
  1348.6 10.0 copy-start.26
  1348.6 10.8 copy-start.28
  1348.6 11.5 copy-start.55
  1348.6 12.1 copy-start.36
  1348.7 12.7 copy-start.54
  1348.7 13.3 copy-start.18
  1348.7 16.7 %copy-start.1 = (bf16[2,768,768]{2,1,0:T(8,128)(2,1)S(1)}, bf16[2,768,768]{2,1,0:T(8,128)(2,1)}, u32[]{:S(2)}) copy-start(bf16[2,768,768]{2,1,0:T(8,128)(2,1)} %param.37) | copy-start | bytes 7077892
  1357.4 6.8 copy-start.59
  1357.4 7.3 copy-start.41
  (15 other events, 28.4 us)
Sparse Core Ops, SparseCore 0:
  151.6 38.6 all-gather.3
  226.6 78.0 reduce-scatter.2
  383.2 37.1 all-gather.5
  455.5 77.9 reduce-scatter.4
  672.6 123.0 all-reduce.11
  804.2 543.0 all-reduce.13

commit v2 on v1

--- a/solution.py
+++ b/solution.py
@@ -11,6 +11,7 @@
 EPS = 1e-06
 HIGH = lax.Precision.HIGHEST
 
+MESH = pl.DeviceIdType.MESH
 TB = 128
 CH = 16
 LB = 512
@@ -318,23 +319,150 @@
     return jnp.stack(cols, axis=1).astype(F32)
 
 
-def prefix(part, axis, combine, identity):
-    place = lax.axis_index(axis)
-    gathered = lax.all_gather(part, axis)
-    state = jnp.zeros_like(part) + jnp.asarray(identity, part.dtype)
-
-    def one(lap, state):
-        return combine(state, lax.dynamic_index_in_dim(gathered, lap, 0, False))
-
-    return lax.fori_loop(0, place, one, state)
+def bit_orders(groups, members):
+    ep_bits, tp_bits = groups.bit_length() - 1, members.bit_length() - 1
+    x = [("ep", b) for b in range(ep_bits - 2)]
+    z = [("ep", b) for b in range(ep_bits - 2, ep_bits)]
+    y = [("tp", b) for b in range(1, tp_bits)]
+    core = [("tp", 0)]
+    return [core + x + y + z, core + y + x + z]
+
+
+def region_sizes(stages, rows, cols):
+    sizes = []
+    for _ in range(stages):
+        if rows > 16:
+            rows //= 2
+            sizes.append((rows, cols, True))
+        else:
+            cols //= 2
+            sizes.append((rows, cols, False))
+    return sizes
+
+
+def sum_kernel(orders, g_ref, out_ref, *rest):
+    stages = len(orders[0])
+    land = rest[:stages]
+    work_ref, send_sem, recv_sem = rest[stages:]
+    chunks, rows, cols = g_ref.shape
+    sizes = region_sizes(stages, rows, cols)
+    me = {"ep": lax.axis_index("ep"), "tp": lax.axis_index("tp")}
+
+    def bit(stage):
+        axis, b = stage
+        return lax.rem(me[axis] // (1 << b), 2)
+
+    def partner(stage):
+        axis, b = stage
+        there = dict(me)
+        there[axis] = me[axis] + (1 << b) - 2 * (1 << b) * bit(stage)
+        return (there["ep"], there["tp"])
+
+    barrier = pltpu.get_barrier_semaphore()
+    for stage in orders[0]:
+        pl.semaphore_signal(barrier, inc=1, device_id=partner(stage), device_id_type=MESH)
+    pl.semaphore_wait(barrier, stages)
+
+    def place(order, upto, flip):
+        r0, c0 = 0, 0
+        for s in range(upto + 1):
+            b = bit(order[s])
+            if s == upto and flip:
+                b = 1 - b
+            if sizes[s][2]:
+                r0 = r0 + b * sizes[s][0]
+            else:
+                c0 = c0 + b * sizes[s][1]
+        return pl.multiple_of(r0, 16), (pl.multiple_of(c0, 128) if not isinstance(c0, int) else c0)
+
+    def part(ref, c, order, upto, flip):
+        r0, c0 = place(order, upto, flip)
+        return ref.at[c, pl.ds(r0, sizes[upto][0]), pl.ds(c0, sizes[upto][1])]
+
+    def scatter(s, p, c):
+        order = orders[p]
+        return pltpu.make_async_remote_copy(
+            src_ref=part(g_ref if s == 0 else work_ref, c, order, s, True), dst_ref=land[s].at[c],
+            send_sem=send_sem.at[s, c], recv_sem=recv_sem.at[s, c], device_id=partner(order[s]), device_id_type=MESH)
+
+    def gather(s, p, c):
+        order = orders[p]
+        mine = part(out_ref, c, order, s, False)
+        return pltpu.make_async_remote_copy(
+            src_ref=mine, dst_ref=mine,
+            send_sem=send_sem.at[stages + s, c], recv_sem=recv_sem.at[stages + s, c], device_id=partner(order[s]),
+            device_id_type=MESH)
+
+    def gathered(s, p, c):
+        order = orders[p]
+        other = part(out_ref, c, order, s, True)
+        return pltpu.make_async_remote_copy(
+            src_ref=other, dst_ref=other,
+            send_sem=send_sem.at[stages + s, c], recv_sem=recv_sem.at[stages + s, c], device_id=partner(order[s]),
+            device_id_type=MESH)
+
+    def each(body):
+        def pair(i, _):
+            body(0, 2 * i)
+            body(1, 2 * i + 1)
+            return 0
+
+        lax.fori_loop(0, chunks // 2, pair, 0)
+        if chunks % 2:
+            body(0, chunks - 1)
+
+    each(lambda p, c: scatter(0, p, c).start())
+    for s in range(stages):
+        def step(p, c):
+            scatter(s, p, c).wait_recv()
+            order = orders[p]
+            r0, c0 = place(order, s, False)
+            where = (c, pl.ds(r0, sizes[s][0]), pl.ds(c0, sizes[s][1]))
+            own = (g_ref if s == 0 else work_ref)[where].astype(F32)
+            total = (own + land[s][c].astype(F32)).astype(BF16)
+            if s + 1 < stages:
+                work_ref[where] = total
+                scatter(s + 1, p, c).start()
+            else:
+                out_ref[where] = total
+                gather(s, p, c).start()
+
+        each(step)
+    for s in reversed(range(stages)):
+        def step(p, c):
+            gathered(s, p, c).wait_recv()
+            if s > 0:
+                gather(s - 1, p, c).start()
+
+        each(step)
+
+    def drain(p, c):
+        for s in range(stages):
+            scatter(s, p, c).wait_send()
+            gather(s, p, c).wait_send()
+
+    each(drain)
+
+
+def all_sum(g, groups, members):
+    orders = bit_orders(groups, members)
+    stages = len(orders[0])
+    chunks, rows, cols = g.shape
+    sizes = region_sizes(stages, rows, cols)
+    return pl.pallas_call(
+        functools.partial(sum_kernel, orders),
+        out_shape=jax.ShapeDtypeStruct(g.shape, BF16),
+        in_specs=[pl.BlockSpec(memory_space=pltpu.VMEM)],
+        out_specs=pl.BlockSpec(memory_space=pltpu.VMEM),
+        scratch_shapes=[pltpu.VMEM((chunks, r, c), BF16) for r, c, _ in sizes]
+        + [pltpu.VMEM(g.shape, BF16), pltpu.SemaphoreType.DMA((2 * stages, chunks)), pltpu.SemaphoreType.DMA((2 * stages, chunks))],
+        compiler_params=pltpu.CompilerParams(collective_id=0, has_side_effects=True, vmem_limit_bytes=48 << 20),
+        name="all_sum",
+    )(g)
 
 
 def rms_scale(values, gain):
     return values * lax.rsqrt(jnp.mean(values * values, axis=-1, keepdims=True) + EPS) * gain
-
-
-def add_counts(earlier, later):
-    return earlier + later
 
 
 def contract_rows(left, right):
@@ -399,7 +527,10 @@
 
     gate, router_pull = jax.vjp(router, normed_two, w_router.astype(jnp.float32))
     local_count = jnp.sum(pick_int, axis=0)
-    prior = prefix(local_count, ("ep", "tp"), add_counts, jnp.zeros_like(local_count))
+    everyone = lax.all_gather(local_count, ("ep", "tp"))
+    earlier = jnp.arange(everyone.shape[0]) < lax.axis_index(("ep", "tp"))
+    prior = jnp.sum(jnp.where(earlier[:, None], everyone, 0), axis=0)
+    named = jnp.sum(everyone, axis=0)
     local_rank = jnp.sum(jnp.cumsum(pick_int, axis=0) * pick_int, axis=1) - 1
     global_rank = jnp.sum(pick_int * prior[None, :], axis=1) + local_rank
     kept = (segment >= 0) & (global_rank < capacity)
@@ -463,52 +594,55 @@
     d_both, grad_vec, grad_x, grad_dt, grad_rates = mid_bwd(
         both, d_gated, pre, pre_dt, scanned, proj, starts, masks, vec, wx_pad.T, wdt_pad, rates * LOG2E, rank_dt
     )
-    middle_grads = (
-        grad_vec[: conv_w.shape[0]], grad_vec[4], grad_x[: rank_dt + 2 * states].T, grad_dt[:rank_dt], grad_vec[5],
-        grad_rates * rates, grad_vec[6],
-    )
     grad_in = contract_rows(normed_low, d_both)
     d_normed_one = lax.dot_general(
         d_both, w_in, (((1,), (1,)), ((), ())), preferred_element_type=jnp.float32
     )
     d_tokens_norm, grad_gain_one = norm_one_pull(d_normed_one)
     d_tokens = d_after + d_tokens_norm
-    held = jnp.sum(pick_int * kept.astype(jnp.int32)[:, None], axis=0)
-    count_f = jnp.stack([local_count, local_count - held]).astype(jnp.float32)
-    summed = lax.psum(
-        (
-            grad_gain_one,
-            grad_in,
-            middle_grads[0],
-            middle_grads[1],
-            middle_grads[2],
-            middle_grads[3],
-            middle_grads[4],
-            middle_grads[5],
-            middle_grads[6],
-            grad_out,
-            grad_gain_two,
-            grad_router,
-            count_f,
-        ),
-        ("ep", "tp"),
-    )
+    counts = jnp.stack([named, jnp.maximum(named - capacity, 0)])
+    used = rank_dt + 2 * states
+    small = jnp.concatenate(
+        [
+            grad_x[:used],
+            grad_dt[:rank_dt],
+            grad_rates * rates,
+            grad_vec,
+            jnp.concatenate([grad_gain_one, grad_gain_two])[None],
+            grad_router.T.reshape(-1, inner_w),
+        ],
+        axis=0,
+    )
+    rows_used = small.shape[0]
+    small = jnp.pad(small, ((0, 256 - rows_used), (0, 0))).T
+    tall = grad_in.astype(jnp.bfloat16).reshape(width // 256, 256, 2 * inner_w // 1024, 1024)
+    tall = tall.transpose(0, 2, 1, 3).reshape(-1, 256, 1024)
+    wide = jnp.concatenate([grad_out.astype(jnp.bfloat16), small.astype(jnp.bfloat16)], axis=1)
+    summed = all_sum(jnp.concatenate([tall, wide.reshape(-1, 256, 1024)], axis=0), groups, lax.axis_size("tp"))
+    total_in = summed[: tall.shape[0]].reshape(width // 256, 2 * inner_w // 1024, 256, 1024)
+    total_in = total_in.transpose(0, 2, 1, 3).reshape(width, 2 * inner_w).astype(jnp.float32)
+    wide = summed[tall.shape[0] :].reshape(inner_w, 1024)
+    total_out = wide[:, :width].astype(jnp.float32)
+    small = wide[:, width:].astype(jnp.float32).T
+    at = used + rank_dt + states
+    taps = conv_w.shape[0]
+    gains = small[at + 8].reshape(2, width)
     return (
         final.astype(jnp.bfloat16),
         d_tokens,
-        summed[12].astype(jnp.int32),
-        summed[0],
-        summed[1],
-        summed[2],
-        summed[3],
-        summed[4],
-        summed[5],
-        summed[6],
-        summed[7],
-        summed[8],
-        summed[9],
-        summed[10],
-        summed[11],
+        counts,
+        gains[0],
+        total_in,
+        small[at : at + taps],
+        small[at + taps],
+        small[:used].T,
+        small[used : used + rank_dt],
+        small[at + taps + 1],
+        small[used + rank_dt : at],
+        small[at + taps + 2],
+        total_out,
+        gains[1],
+        small[at + 9 : rows_used].reshape(experts, width).T,
         grad_up,
         grad_down,
     )

time: 1380 us -> 889 us (0.64)
  waiting for transfers between devices: 909 us -> 253 us
  Pallas kernels: 112 us -> 219 us
  local copies, waits for them, and re-layouts: 55.1 us -> 109 us
    psum x2 -> x0, waiting for transfers between devices: 629 us -> none  [local(): lax.psum((grad_gain_one, grad_in, middle_grads[0], middle_grads[1], middl...]
    pallas_call x0 -> x1, Pallas kernels: none -> 107 us  [all_sum(): pl.pallas_call(functools.partial(sum_kernel, orders), out_shape=jax.Shape...]
    all_to_all x1, waiting for transfers between devices: 24.2 us -> 0.01 us  [local(): lax.all_to_all(d_expert_in.astype(jnp.bfloat16), 'ep', split_axis=2, conc...]
    reshape x0 -> x3, local copies, waits for them, and re-layouts: none -> 14.3 us  [the longest x1 13.7 us: local(): grad_in.astype(jnp.bfloat16)]
    unnamed x156 -> x127, local copies, waits for them, and re-layouts: 34.7 us -> 40.1 us
  transfers between devices with their start and end apart: 8 -> 6, of which waited for: 8 -> 5; matrix products, arithmetic and copies ran while one was open for 4% -> 5% of each run, Pallas kernels for 0% -> 0%
where the time goes in v2:
time: 889 us; the launch traced here: 881 us
  waiting for transfers between devices  253 us (28%)
  Pallas kernels  219 us (25%)
  matrix products  139 us (16%)
  local copies, waits for them, and re-layouts  109 us (12%)
  blocking collectives  104 us (12%)
  other arithmetic  31.8 us (4%)
  between operations  15 us (2%)
  starting transfers between devices  11.3 us (1%)
    pallas_call x1, Pallas kernels, all_sum(): pl.pallas_call(functools.partial(sum_kernel, orders), out_shape=jax.Shape...  107 us
    reduce_scatter x1, waiting for transfers between devices, local(): expert_out = lax.psum_scatter(terms, 'tp', scatter_dimension=2, tiled=True)  78.2 us
    pallas_call x1, Pallas kernels, mid_bwd(): pl.pallas_call(functools.partial(mid_bwd_kernel, rank), grid=(blocks,), o...  76.8 us
    reduce_scatter x1, waiting for transfers between devices, local(): lax.psum_scatter(row_terms, 'tp', scatter_dimension=2, tiled=True)  75.1 us
    unnamed x1, blocking collectives  40.6 us
    unnamed x127, local copies, waits for them, and re-layouts  40.1 us
    all_gather x1, waiting for transfers between devices, local(): expert_rows = lax.all_gather(received, 'tp', axis=2, tiled=True)  38.6 us
    all_gather x1, waiting for transfers between devices, local(): d_rows_all = lax.all_gather(d_received, 'tp', axis=2, tiled=True)  37.1 us
  transfers between devices with their start and end apart: 6, of which 5 were waited for; matrix products, arithmetic and copies ran while one was open for 5% of the time, Pallas kernels for 0%

profile of v2, /device:TPU:1, one launch (start us, length us, event | category | flops | bytes accessed | tf_op | source)
XLA Modules:
  0.0 880.9 jit_solution(14681756370963550882)
XLA Ops:
  9.8 1.4 fusion.35
  14.5 40.6 %all-reduce.7 = s32[512]{0:T(512)S(1)} all-reduce(s32[512]{0:T(512)S(1)} %dynamic-update-slice), channel_id=2, replica_groups=mesh['ep'=8,'tp'=4] {'ep','tp'}, use_global_device_ids=true, to_apply=%add.7 | all-reduce | flops 512 | bytes 4096
  58.7 1.1 reduce-window.6
  61.2 1.3 copy.116
  63.6 8.1 fusion.61.both_ref
  71.7 34.9 %mid_fwd.1 = (bf16[512,1536]{1,0:T(8,128)(2,1)S(1)}, f32[512,1536]{1,0:T(8,128)S(1)}, f32[512,1536]{1,0:T(8,128)S(1)}, f32[512,1536]{1,0:T(8,128)S(1)}, f32[512,128]{1,0:T(8,128)S(1)}, /*index=5*/f32[32,16,1536]{2,1,0:T(8,128)}) custom-call(f32[512,3072]{1,0:T(8,128)} %fusion.61.both_ref, f32[512,8]{1,0:T(8,128)S(1)} %convert_element_type.105.mask_ref, ...), custom_call_target="tpu_custom_call" | custom-call | tf_op jit(solution)/shard_map/mid_fwd/pallas_call | solution.py:123
  106.6 1.7 copy-done.3
  108.4 1.6 copy-done.4
  110.0 1.7 copy-done.5
  112.4 1.1 copy-done.10
  113.5 1.5 multiply_reduce_fusion.2
  117.3 31.0 %all_to_all.66 = bf16[8,2,48,768]{3,2,1,0:T(8,128)(2,1)S(1)} all-to-all(bf16[8,2,48,768]{3,2,1,0:T(8,128)(2,1)S(1)} %bitcast.209), channel_id=1, replica_groups=mesh['ep'=8,'tp'=4] {'ep'}, dimensions={0} | all-to-all | bytes 2359296 | tf_op jit(solution)/shard_map/all_to_all | solution.py:544
  148.2 1.1 copy.93
  149.6 38.6 %all-gather.4.cloned.1.call-done = bf16[1,2,1536,768]{3,2,1,0:T(8,128)(2,1)} async-done(((bf16[1,2,384,768]{3,2,1,0:T(8,128)(2,1)}), bf16[1,2,1536,768]{3,2,1,0:T(8,128)(2,1)}) %all-gather.4.cloned.1.call-update) | async-done | bytes 4718608 | tf_op jit(solution)/shard_map/all_gather | solution.py:546
  188.2 6.4 fusion.26
  194.6 3.7 copy-done.56
  198.4 26.0 %convolution_bitcast_fusion.1 = f32[1,2,1536,768]{3,2,1,0:T(8,128)} fusion(bf16[2,768,768]{2,1,0:T(8,128)(2,1)S(1)} %copy-done, f32[2,1536,768]{2,1,0:T(8,128)S(1)} %fusion.26), kind=kOutput, calls=%fused_computation.29 | convolution fusion | flops 3777232896 | bytes 21233664 | tf_op jit(solution)/shard_map/axrf,xfd->axrd/dot_general | solution.py:552
  224.4 78.2 %reduce-scatter.3.cloned.1.call-done = f32[1,2,384,768]{3,2,1,0:T(8,128)} async-done(((f32[1,2,1536,768]{3,2,1,0:T(8,128)}), f32[1,2,384,768]{3,2,1,0:T(8,128)}) %reduce-scatter.3.cloned.1.call-update) | async-done | bytes 2359312 | tf_op jit(solution)/shard_map/reduce_scatter | solution.py:553
  302.6 1.8 convert_element_type.116
  304.4 2.2 copy.94
  306.6 5.2 all-to-all-start.1
  311.9 2.4 fusion.93
  315.5 24.0 %all-to-all-done.1 = bf16[1,2,384,768]{3,1,0,2:T(2,128)(2,1)S(1)} async-done(((bf16[1,2,384,768]{3,1,0,2:T(2,128)(2,1)}), bf16[1,2,384,768]{3,1,0,2:T(2,128)(2,1)S(1)}, u32[]{:S(2)}, u32[]{:S(2)}) %all-to-all-start.1) | async-done | bytes 1179680 | tf_op jit(solution)/shard_map/all_to_all | solution.py:554
  339.8 3.2 fusion.33
  345.2 2.1 fusion.42
  347.3 32.1 %all_to_all.67 = bf16[8,2,48,768]{3,2,1,0:T(8,128)(2,1)S(1)} all-to-all(bf16[8,2,48,768]{3,2,1,0:T(8,128)(2,1)S(1)} %bitcast.210), channel_id=1, replica_groups=mesh['ep'=8,'tp'=4] {'ep'}, dimensions={0} | all-to-all | bytes 2359296 | tf_op jit(solution)/shard_map/all_to_all | solution.py:569
  379.3 1.1 copy.97
  380.7 37.1 %all-gather.6.cloned.1.call-done = bf16[1,2,1536,768]{3,2,1,0:T(8,128)(2,1)} async-done(((bf16[1,2,384,768]{3,2,1,0:T(8,128)(2,1)}), bf16[1,2,1536,768]{3,2,1,0:T(8,128)(2,1)}) %all-gather.6.cloned.1.call-update) | async-done | bytes 4718608 | tf_op jit(solution)/shard_map/all_gather | solution.py:570
  417.8 26.3 %fusion.6 = bf16[1,2,1536,768]{3,2,1,0:T(8,128)(2,1)S(1)} fusion(f32[2,1536,768]{2,1,0:T(8,128)} %copy-done.56, bf16[2,768,768]{2,1,0:T(8,128)(2,1)S(1)} %copy-done, bf16[1,2,1536,768]{3,2,1,0:T(8,128)(2,1)} %all-gather.6.cloned.1.call-done), kind=kOutput, calls=%fused_computation.9 | convolution fusion | flops 3793747968 | bytes 21233664 | tf_op jit(solution)/shard_map/axrd,xfd->axrf/dot_general | solution.py:575
  444.1 2.2 copy-done.57
  446.3 6.3 convolution_bitcast_fusion
  454.7 1.0 fusion.46
  455.8 75.1 %reduce-scatter.5.cloned.1.call-done = f32[1,2,384,768]{3,2,1,0:T(8,128)} async-done(((f32[1,2,1536,768]{3,2,1,0:T(8,128)}), f32[1,2,384,768]{3,2,1,0:T(8,128)}) %reduce-scatter.5.cloned.1.call-update) | async-done | bytes 2359312 | tf_op jit(solution)/shard_map/reduce_scatter | solution.py:581
  530.9 1.8 convert_element_type.122
  532.6 2.3 copy.98
  534.9 5.5 all-to-all-start.3
  540.4 26.2 %fusion.22 = f32[2,768,768]{2,1,0:T(8,128)} fusion(bf16[1,2,1536,768]{3,2,1,0:T(8,128)(2,1)} %all-gather.6.cloned.1.call-done, f32[2,1536,768]{2,1,0:T(8,128)} %copy-done.56), kind=kOutput, calls=%fused_computation.35 | convolution fusion | flops 3777232896 | bytes 18874368 | tf_op jit(solution)/shard_map/axrf,axrd->xfd/dot_general | solution.py:572
  566.6 9.9 %fusion.19 = f32[2,768,768]{2,1,0:T(8,128)} fusion(bf16[1,2,1536,768]{3,2,1,0:T(8,128)(2,1)} %copy-done.57, bf16[1,2,1536,768]{3,2,1,0:T(8,128)(2,1)} %all-gather.4.cloned.1.call-done), kind=kOutput, calls=%fused_computation.32 | convolution fusion | flops 3623878656 | bytes 14155776 | tf_op jit(solution)/shard_map/axrd,axrf->xdf/dot_general | solution.py:579
  578.0 1.2 multiply_reduce_fusion
  579.2 1.4 convert_add_fusion.1
  580.7 2.9 convolution_convert_fusion.1
  583.6 3.1 fusion.84.dg_ref
  586.8 76.8 %mid_bwd.1 = (bf16[512,3072]{1,0:T(8,128)(2,1)}, f32[8,1536]{1,0:T(8,128)}, f32[128,1536]{1,0:T(8,128)}, f32[128,1536]{1,0:T(8,128)}, f32[16,1536]{1,0:T(8,128)}) custom-call(f32[512,3072]{1,0:T(8,128)} %fusion.61.both_ref, f32[512,1536]{1,0:T(8,128)} %fusion.84.dg_ref, f32[512,1536]{1,0:T(8,128)} %copy-done.3, f32[512,1536]{1,0:T(8,128)} %copy-done.4, ...), custom_call_target="tpu_custom_call" | custom-call | tf_op jit(solution)/shard_map/mid_bwd/pallas_call | solution.py:286
  663.6 6.0 fusion.31
  669.6 4.5 convolution_convert_fusion
  674.1 1.1 slice.129
  676.6 3.5 pad_maximum_fusion.1
  680.2 4.7 copy.102
  684.8 13.7 %reshape.203 = bf16[3,256,3,1024]{3,2,1,0:T(4,128)(2,1)} reshape(bf16[768,3072]{1,0:T(8,128)(2,1)} %convolution_convert_fusion) | data formatting | bytes 9437184 | tf_op jit(solution)/shard_map/reshape | solution.py:618
  698.5 6.9 copy.101
  705.4 7.2 pad_maximum_fusion.g_ref
  712.6 106.9 %all_sum.1 = bf16[15,256,1024]{2,1,0:T(8,128)(2,1)} custom-call(bf16[15,256,1024]{2,1,0:T(8,128)(2,1)} %pad_maximum_fusion.g_ref), custom_call_target="tpu_custom_call" | custom-call | tf_op jit(solution)/shard_map/all_sum/pallas_call | solution.py:452
  819.5 2.2 slice.89
  821.7 5.0 slice.92
  826.9 1.1 slice_reduce_fusion.3
  828.0 1.9 slice_reduce_fusion
  830.8 1.2 slice.111
  833.5 2.6 slice_convert_fusion
  836.2 2.0 copy.110
  838.2 2.1 copy.109
  840.3 1.0 copy.108
  843.0 11.2 %copy.103 = f32[3,3,256,1024]{3,1,2,0:T(4,128)} copy(bf16[3,3,256,1024]{3,2,1,0:T(8,128)(2,1)} %bitcast.195) | data formatting | bytes 14155776 | tf_op jit(solution)/shard_map/convert_element_type | solution.py:623
  854.2 18.1 %copy.114 = f32[96,8,3,1024]{3,1,2,0:T(8,128)} copy(f32[96,8,3,1024]{3,2,1,0:T(4,128)} %bitcast.193) | data formatting | bytes 18874368
  872.3 1.6 fusion.34
  (194 shorter events, 28.2 us)
Async XLA Ops:
  7.2 191.2 %copy-start = (bf16[2,768,768]{2,1,0:T(8,128)(2,1)S(1)}, bf16[2,768,768]{2,1,0:T(8,128)(2,1)}, u32[]{:S(2)}) copy-start(bf16[2,768,768]{2,1,0:T(8,128)(2,1)} %param.35) | copy-start | bytes 7077892
  7.2 181.0 %all-gather.4.cloned.1.call-start = ((), (), s32[]{:S(2)}) async-start(), calls=%async_computation.6 | async-start | bytes 5898240 | tf_op jit(solution)/shard_map/all_gather | solution.py:546
  11.2 1.4 copy-start.37
  11.2 95.3 %copy-start.41 = (f32[512]{0:T(512)}, f32[512]{0:T(512)S(1)}, u32[]{:S(2)}) copy-start(f32[512]{0:T(512)S(1)} %fusion.80) | copy-start | bytes 6148
  12.6 94.0 %copy-start.39 = (f32[768]{0:T(1024)}, f32[768]{0:T(1024)S(1)}, u32[]{:S(2)}) copy-start(f32[768]{0:T(1024)S(1)} %convert_element_type.103) | copy-start | bytes 9220
  13.4 99.0 %copy-start.47 = (f32[512]{0:T(512)}, f32[512]{0:T(512)S(1)}, u32[]{:S(2)}) copy-start(f32[512]{0:T(512)S(1)} %get-tuple-element.124) | copy-start | bytes 6148
  13.4 102.4 %copy-start.33 = (pred[512]{0:T(512)(128)(4,1)}, pred[512]{0:T(512)(128)(4,1)S(1)}, u32[]{:S(2)}) copy-start(pred[512]{0:T(512)(128)(4,1)S(1)} %get-tuple-element.125) | copy-start | bytes 1540
  58.0 48.6 %copy-start.8 = (f32[8,1536]{1,0:T(8,128)}, f32[8,1536]{1,0:T(8,128)S(1)}, u32[]{:S(2)}) copy-start(f32[8,1536]{1,0:T(8,128)S(1)} %convert_element_type.106.vec_ref) | copy-start | bytes 147460
  61.2 45.4 %copy-start.7 = (f32[16,1536]{1,0:T(8,128)}, f32[16,1536]{1,0:T(8,128)S(1)}, u32[]{:S(2)}) copy-start(f32[16,1536]{1,0:T(8,128)S(1)} %fusion.63.rates_ref) | copy-start | bytes 294916
  61.2 45.4 %copy-start.6 = (f32[512,8]{1,0:T(8,128)}, f32[512,8]{1,0:T(8,128)S(1)}, u32[]{:S(2)}) copy-start(f32[512,8]{1,0:T(8,128)S(1)} %convert_element_type.105.mask_ref) | copy-start | bytes 49156
  63.5 43.1 %copy-start.2 = (bf16[128,1536]{1,0:T(8,128)(2,1)}, bf16[128,1536]{1,0:T(8,128)(2,1)S(1)}, u32[]{:S(2)}) copy-start(bf16[128,1536]{1,0:T(8,128)(2,1)S(1)} %pad.18.wdt_ref) | copy-start | bytes 1179652
  63.6 50.0 %copy-start.18 = (bf16[512,768]{1,0:T(8,128)(2,1)S(1)}, bf16[512,768]{1,0:T(8,128)(2,1)}, u32[]{:S(2)}) copy-start(bf16[512,768]{1,0:T(8,128)(2,1)} %param.18) | copy-start | bytes 2359300
  63.6 50.0 %copy-start.54 = (bf16[1536,768]{1,0:T(8,128)(2,1)S(1)}, bf16[1536,768]{1,0:T(8,128)(2,1)}, u32[]{:S(2)}) copy-start(bf16[1536,768]{1,0:T(8,128)(2,1)} %param.31) | copy-start | bytes 7077892
  71.7 44.0 %copy-start.28 = (s32[512,1]{0,1:T(1,128)S(1)}, s32[512,1]{0,1:T(1,128)}, u32[]{:S(2)}) copy-start(s32[512,1]{0,1:T(1,128)} %param.21) | copy-start | bytes 6148
  106.6 1.7 copy-start.3
  108.4 1.6 copy-start.4
  110.0 1.7 copy-start.5
  111.7 0.7 copy-start.9
  112.4 1.1 copy-start.10
  115.0 1.3 copy-start.12
  115.1 79.6 %copy-start.45 = (f32[512]{0:T(512)}, f32[512]{0:T(512)S(1)}, u32[]{:S(2)}) copy-start(f32[512]{0:T(512)S(1)} %get-tuple-element.140) | copy-start | bytes 6148
  116.3 78.3 %copy-start.50 = (s32[512]{0:T(512)}, s32[512]{0:T(512)S(1)}, u32[]{:S(2)}) copy-start(s32[512]{0:T(512)S(1)} %get-tuple-element.122) | copy-start | bytes 6148
  149.4 153.2 %reduce-scatter.3.cloned.1.call-start = ((), (), s32[]{:S(2)}) async-start(), calls=%async_computation.7 | async-start | bytes 11796480 | tf_op jit(solution)/shard_map/reduce_scatter | solution.py:553
  194.6 3.7 copy-start.56
  306.6 33.0 %all-to-all-start.1 = ((bf16[1,2,384,768]{3,1,0,2:T(2,128)(2,1)}), bf16[1,2,384,768]{3,1,0,2:T(2,128)(2,1)S(1)}, u32[]{:S(2)}, u32[]{:S(2)}) async-start(bf16[1,2,384,768]{3,1,0,2:T(2,128)(2,1)} %copy.94), calls=%async_computation.2 | async-start | bytes 2359296 | tf_op jit(solution)/shard_map/all_to_all | solution.py:554
  311.9 106.0 %all-gather.6.cloned.1.call-start = ((), (), s32[]{:S(2)}) async-start(), calls=%async_computation.8 | async-start | bytes 5898240 | tf_op jit(solution)/shard_map/all_gather | solution.py:570
  343.7 111.0 %copy-start.35 = (f32[512]{0:T(512)}, f32[512]{0:T(512)S(1)}, u32[]{:S(2)}) copy-start(f32[512]{0:T(512)S(1)} %get-tuple-element.149) | copy-start | bytes 6148
  345.2 98.9 %copy-start.43 = (f32[512]{0:T(512)}, f32[512]{0:T(512)S(1)}, u32[]{:S(2)}) copy-start(f32[512]{0:T(512)S(1)} %broadcast_select_fusion.1) | copy-start | bytes 6148
  380.4 150.4 %reduce-scatter.5.cloned.1.call-start = ((), (), s32[]{:S(2)}) async-start(), calls=%async_computation.9 | async-start | bytes 11796480 | tf_op jit(solution)/shard_map/reduce_scatter | solution.py:581
  417.8 28.5 %copy-start.53 = (bf16[2,768,768]{2,1,0:T(8,128)(2,1)S(1)}, bf16[2,768,768]{2,1,0:T(8,128)(2,1)}, u32[]{:S(2)}) copy-start(bf16[2,768,768]{2,1,0:T(8,128)(2,1)} %param.34) | copy-start | bytes 7077892
  444.1 2.2 copy-start.57
  452.6 1.2 copy-start.23
  452.6 2.0 copy-start.13
  452.6 2.0 copy-start.25
  452.6 2.0 copy-start.31
  452.7 2.0 copy-start.34
  534.9 41.7 %all-to-all-start.3 = ((bf16[1,2,384,768]{3,1,0,2:T(2,128)(2,1)}), bf16[1,2,384,768]{3,1,0,2:T(2,128)(2,1)S(1)}, u32[]{:S(2)}, u32[]{:S(2)}) async-start(bf16[1,2,384,768]{3,1,0,2:T(2,128)(2,1)} %copy.98), calls=%async_computation.5 | async-start | bytes 2359296 | tf_op jit(solution)/shard_map/all_to_all | solution.py:582
  566.6 10.2 %copy-start.51 = (s32[512]{0:T(512)S(1)}, s32[512]{0:T(512)}, u32[]{:S(2)}) copy-start(s32[512]{0:T(512)} %copy-done.50) | copy-start | bytes 6148
  576.5 1.2 copy-start.29
  576.5 1.2 copy-start.36
  576.5 2.7 copy-start.46
  576.5 2.7 copy-start.44
  576.6 1.4 copy-start.14
  576.6 2.7 copy-start.21
  576.6 2.7 copy-start.26
  576.8 3.9 copy-start.11
  576.8 3.9 copy-start.48
  579.2 4.5 copy-start.55
  580.7 6.1 copy-start.15
  583.6 79.9 %slice-start = ((s8[4718592]{0:T(1024)(128)(4,1)}), s8[4194304]{0:T(1024)(128)(4,1)S(1)}, s32[]{:S(2)}) async-start(s8[4718592]{0:T(1024)(128)(4,1)} %bitcast.221), calls=%async_computation.10 | async-start | bytes 8388608
  586.8 76.8 %copy-start.19 = (bf16[512,768]{1,0:T(8,128)(2,1)S(1)}, bf16[512,768]{1,0:T(8,128)(2,1)}, u32[]{:S(2)}) copy-start(bf16[512,768]{1,0:T(8,128)(2,1)} %param.18) | copy-start | bytes 2359300
  586.8 76.8 %copy-start.40 = (f32[768]{0:T(1024)S(1)}, f32[768]{0:T(1024)}, u32[]{:S(2)}) copy-start(f32[768]{0:T(1024)} %copy-done.39) | copy-start | bytes 9220
  586.8 76.8 %copy-start.42 = (f32[512]{0:T(512)S(1)}, f32[512]{0:T(512)}, u32[]{:S(2)}) copy-start(f32[512]{0:T(512)} %copy-done.41) | copy-start | bytes 6148
  586.8 76.8 %slice-start.1 = ((s8[4718592]{0:T(1024)(128)(4,1)}), s8[524288]{0:T(1024)(128)(4,1)S(1)}, s32[]{:S(2)}) async-start(s8[4718592]{0:T(1024)(128)(4,1)} %bitcast.221), calls=%async_computation.11 | async-start | bytes 1048576
  663.5 6.1 copy-start.52
  669.6 5.6 copy-start.32
  669.6 5.6 copy-start.27
  669.6 5.6 copy-start.30
  826.9 9.3 %copy-start.38 = (f32[512]{0:T(512)S(1)}, f32[512]{0:T(512)}, u32[]{:S(2)}) copy-start(f32[512]{0:T(512)} %copy-done.37) | copy-start | bytes 6148
  833.5 6.8 copy-start.17
  854.2 19.7 %copy-start.1 = (bf16[2,768,768]{2,1,0:T(8,128)(2,1)S(1)}, bf16[2,768,768]{2,1,0:T(8,128)(2,1)}, u32[]{:S(2)}) copy-start(bf16[2,768,768]{2,1,0:T(8,128)(2,1)} %param.35) | copy-start | bytes 7077892
  854.2 18.1 %copy-start.16 = (f32[512,768]{1,0:T(8,128)S(1)}, f32[512,768]{1,0:T(8,128)}, u32[]{:S(2)}) copy-start(f32[512,768]{1,0:T(8,128)} %copy-done.15) | copy-start | bytes 4718596
  854.2 18.1 %copy-start.20 = (bf16[512,768]{1,0:T(8,128)(2,1)S(1)}, bf16[512,768]{1,0:T(8,128)(2,1)}, u32[]{:S(2)}) copy-start(bf16[512,768]{1,0:T(8,128)(2,1)} %param.18) | copy-start | bytes 2359300
  854.2 18.1 %copy-start.22 = (f32[512,768]{1,0:T(8,128)S(1)}, f32[512,768]{1,0:T(8,128)}, u32[]{:S(2)}) copy-start(f32[512,768]{1,0:T(8,128)} %get-tuple-element.147) | copy-start | bytes 4718596
  (2 other events, 1.3 us)
Sparse Core Ops, SparseCore 0:
  149.5 38.6 all-gather.3
  224.5 78.0 reduce-scatter.2
  380.6 37.1 all-gather.5
  452.8 77.9 reduce-scatter.4

commit v3 on v2

--- a/solution.py
+++ b/solution.py
@@ -1,5 +1,4 @@
 import functools
-from functools import partial
 
 import jax
 import jax.numpy as jnp
@@ -10,7 +9,6 @@
 
 EPS = 1e-06
 HIGH = lax.Precision.HIGHEST
-
 MESH = pl.DeviceIdType.MESH
 TB = 128
 CH = 16
@@ -340,12 +338,17 @@
     return sizes
 
 
-def sum_kernel(orders, g_ref, out_ref, *rest):
+CHUNK = (256, 1024)
+
+
+def sum_kernel(orders, tall_ref, wide_ref, tall_out, wide_out, *rest):
     stages = len(orders[0])
     land = rest[:stages]
     work_ref, send_sem, recv_sem = rest[stages:]
-    chunks, rows, cols = g_ref.shape
-    sizes = region_sizes(stages, rows, cols)
+    sizes = region_sizes(stages, *CHUNK)
+    across = tall_ref.shape[1] // CHUNK[1]
+    split_at = across * (tall_ref.shape[0] // CHUNK[0])
+    chunks = split_at + wide_ref.shape[0] // CHUNK[0]
     me = {"ep": lax.axis_index("ep"), "tp": lax.axis_index("tp")}
 
     def bit(stage):
@@ -363,7 +366,7 @@
         pl.semaphore_signal(barrier, inc=1, device_id=partner(stage), device_id_type=MESH)
     pl.semaphore_wait(barrier, stages)
 
-    def place(order, upto, flip):
+    def window(order, upto, flip):
         r0, c0 = 0, 0
         for s in range(upto + 1):
             b = bit(order[s])
@@ -373,92 +376,376 @@
                 r0 = r0 + b * sizes[s][0]
             else:
                 c0 = c0 + b * sizes[s][1]
-        return pl.multiple_of(r0, 16), (pl.multiple_of(c0, 128) if not isinstance(c0, int) else c0)
-
-    def part(ref, c, order, upto, flip):
-        r0, c0 = place(order, upto, flip)
-        return ref.at[c, pl.ds(r0, sizes[upto][0]), pl.ds(c0, sizes[upto][1])]
-
-    def scatter(s, p, c):
+        return r0, c0
+
+    def in_work(c, order, upto, flip):
+        r0, c0 = window(order, upto, flip)
+        return (c, pl.ds(pl.multiple_of(r0, 16), sizes[upto][0]),
+                pl.ds(c0 if isinstance(c0, int) else pl.multiple_of(c0, 128), sizes[upto][1]))
+
+    def in_array(tall, c, order, upto, flip):
+        r0, c0 = window(order, upto, flip)
+        if tall:
+            r0 = r0 + (c // across) * CHUNK[0]
+            c0 = c0 + lax.rem(c, across) * CHUNK[1]
+        else:
+            r0 = r0 + (c - split_at) * CHUNK[0]
+        return (pl.ds(pl.multiple_of(r0, 16), sizes[upto][0]),
+                pl.ds(c0 if isinstance(c0, int) else pl.multiple_of(c0, 128), sizes[upto][1]))
+
+    def scatter(s, tall, p, c):
         order = orders[p]
+        if s == 0:
+            src = (tall_ref if tall else wide_ref).at[in_array(tall, c, order, s, True)]
+        else:
+            src = work_ref.at[in_work(c, order, s, True)]
         return pltpu.make_async_remote_copy(
-            src_ref=part(g_ref if s == 0 else work_ref, c, order, s, True), dst_ref=land[s].at[c],
-            send_sem=send_sem.at[s, c], recv_sem=recv_sem.at[s, c], device_id=partner(order[s]), device_id_type=MESH)
-
-    def gather(s, p, c):
+            src_ref=src, dst_ref=land[s].at[c], send_sem=send_sem.at[s, c], recv_sem=recv_sem.at[s, c],
+            device_id=partner(order[s]), device_id_type=MESH)
+
+    def gather(s, tall, p, c, flip=False):
         order = orders[p]
-        mine = part(out_ref, c, order, s, False)
+        piece = (tall_out if tall else wide_out).at[in_array(tall, c, order, s, flip)]
         return pltpu.make_async_remote_copy(
-            src_ref=mine, dst_ref=mine,
-            send_sem=send_sem.at[stages + s, c], recv_sem=recv_sem.at[stages + s, c], device_id=partner(order[s]),
-            device_id_type=MESH)
-
-    def gathered(s, p, c):
-        order = orders[p]
-        other = part(out_ref, c, order, s, True)
-        return pltpu.make_async_remote_copy(
-            src_ref=other, dst_ref=other,
-            send_sem=send_sem.at[stages + s, c], recv_sem=recv_sem.at[stages + s, c], device_id=partner(order[s]),
-            device_id_type=MESH)
+            src_ref=piece, dst_ref=piece, send_sem=send_sem.at[stages + s, c], recv_sem=recv_sem.at[stages + s, c],
+            device_id=partner(order[s]), device_id_type=MESH)
 
     def each(body):
-        def pair(i, _):
-            body(0, 2 * i)
-            body(1, 2 * i + 1)
-            return 0
-
-        lax.fori_loop(0, chunks // 2, pair, 0)
-        if chunks % 2:
-            body(0, chunks - 1)
-
-    each(lambda p, c: scatter(0, p, c).start())
+        for tall, low, high in ((True, 0, split_at), (False, split_at, chunks)):
+            def pair(i, _, tall=tall, low=low):
+                body(tall, 0, low + 2 * i)
+                body(tall, 1, low + 2 * i + 1)
+                return 0
+
+            lax.fori_loop(0, (high - low) // 2, pair, 0)
+            if (high - low) % 2:
+                body(tall, 0, high - 1)
+
+    each(lambda tall, p, c: scatter(0, tall, p, c).start())
     for s in range(stages):
-        def step(p, c):
-            scatter(s, p, c).wait_recv()
+        def step(tall, p, c):
+            scatter(s, tall, p, c).wait_recv()
             order = orders[p]
-            r0, c0 = place(order, s, False)
-            where = (c, pl.ds(r0, sizes[s][0]), pl.ds(c0, sizes[s][1]))
-            own = (g_ref if s == 0 else work_ref)[where].astype(F32)
-            total = (own + land[s][c].astype(F32)).astype(BF16)
+            if s == 0:
+                own = (tall_ref if tall else wide_ref)[in_array(tall, c, order, s, False)]
+            else:
+                own = work_ref[in_work(c, order, s, False)]
+            total = (own.astype(F32) + land[s][c].astype(F32)).astype(BF16)
             if s + 1 < stages:
-                work_ref[where] = total
-                scatter(s + 1, p, c).start()
+                work_ref[in_work(c, order, s, False)] = total
+                scatter(s + 1, tall, p, c).start()
             else:
-                out_ref[where] = total
-                gather(s, p, c).start()
+                (tall_out if tall else wide_out)[in_array(tall, c, order, s, False)] = total
+                gather(s, tall, p, c).start()
 
         each(step)
     for s in reversed(range(stages)):
-        def step(p, c):
-            gathered(s, p, c).wait_recv()
+        def step(tall, p, c):
+            gather(s, tall, p, c, True).wait_recv()
             if s > 0:
-                gather(s - 1, p, c).start()
+                gather(s - 1, tall, p, c).start()
 
         each(step)
 
-    def drain(p, c):
+    def drain(tall, p, c):
         for s in range(stages):
-            scatter(s, p, c).wait_send()
-            gather(s, p, c).wait_send()
+            scatter(s, tall, p, c).wait_send()
+            gather(s, tall, p, c).wait_send()
 
     each(drain)
 
 
-def all_sum(g, groups, members):
+def all_sum(tall, wide, groups, members):
     orders = bit_orders(groups, members)
     stages = len(orders[0])
-    chunks, rows, cols = g.shape
-    sizes = region_sizes(stages, rows, cols)
+    chunks = tall.size // (CHUNK[0] * CHUNK[1]) + wide.size // (CHUNK[0] * CHUNK[1])
+    vmem = pl.BlockSpec(memory_space=pltpu.VMEM)
     return pl.pallas_call(
         functools.partial(sum_kernel, orders),
-        out_shape=jax.ShapeDtypeStruct(g.shape, BF16),
-        in_specs=[pl.BlockSpec(memory_space=pltpu.VMEM)],
-        out_specs=pl.BlockSpec(memory_space=pltpu.VMEM),
-        scratch_shapes=[pltpu.VMEM((chunks, r, c), BF16) for r, c, _ in sizes]
-        + [pltpu.VMEM(g.shape, BF16), pltpu.SemaphoreType.DMA((2 * stages, chunks)), pltpu.SemaphoreType.DMA((2 * stages, chunks))],
+        out_shape=(jax.ShapeDtypeStruct(tall.shape, BF16), jax.ShapeDtypeStruct(wide.shape, BF16)),
+        in_specs=[vmem, vmem],
+        out_specs=(vmem, vmem),
+        scratch_shapes=[pltpu.VMEM((chunks, r, c), BF16) for r, c, _ in region_sizes(stages, *CHUNK)]
+        + [pltpu.VMEM((chunks,) + CHUNK, BF16), pltpu.SemaphoreType.DMA((2 * stages, chunks)),
+           pltpu.SemaphoreType.DMA((2 * stages, chunks))],
         compiler_params=pltpu.CompilerParams(collective_id=0, has_side_effects=True, vmem_limit_bytes=48 << 20),
         name="all_sum",
-    )(g)
+    )(tall, wide)
+
+
+def entry_barrier(groups, chips):
+    e, t = lax.axis_index("ep"), lax.axis_index("tp")
+    y, c = t // 2, lax.rem(t, 2)
+    barrier = pltpu.get_barrier_semaphore()
+    for k in range(1, groups):
+        pl.semaphore_signal(barrier, inc=1, device_id=(lax.rem(e + k, groups), t), device_id_type=MESH)
+    for k in range(1, chips):
+        pl.semaphore_signal(barrier, inc=1, device_id=(e, lax.rem(y + k, chips) * 2 + c), device_id_type=MESH)
+    pl.semaphore_signal(barrier, inc=1, device_id=(e, t + 1 - 2 * c), device_id_type=MESH)
+    pl.semaphore_wait(barrier, groups + chips - 1)
+    return e, t, y, c
+
+
+def dispatch_kernel(groups, chips, rows_ref, count_ref, out_ref, table_ref,
+                    own_sem, far_send, far_recv, row_send, row_recv, pair_send, pair_recv):
+    e, t, y, c = entry_barrier(groups, chips)
+    held = rows_ref.shape[1] // groups
+    sibling = (e, t + 1 - 2 * c)
+
+    def block(kind, ref, i, member):
+        return ref.at[:, :, member, i] if kind == 0 else ref.at[member, i]
+
+    kinds = ((0, rows_ref, out_ref), (1, count_ref, table_ref))
+
+    def mine(kind, src, peer):
+        return src.at[:, pl.ds(peer * held, held)] if kind == 0 else src
+
+    def far(kind, src, dst, peer, source):
+        return pltpu.make_async_remote_copy(
+            src_ref=mine(kind, src, peer), dst_ref=block(kind, dst, source, t), send_sem=far_send.at[kind, peer],
+            recv_sem=far_recv.at[kind, source], device_id=(peer, t), device_id_type=MESH)
+
+    def across(kind, dst, i, to, source):
+        there = block(kind, dst, i, source * 2 + c)
+        return pltpu.make_async_remote_copy(
+            src_ref=there, dst_ref=there, send_sem=row_send.at[kind, i, to], recv_sem=row_recv.at[kind, i, source],
+            device_id=(e, to * 2 + c), device_id_type=MESH)
+
+    def beside(kind, dst, i, source, core):
+        there = block(kind, dst, i, source * 2 + core)
+        return pltpu.make_async_remote_copy(
+            src_ref=there, dst_ref=there, send_sem=pair_send.at[kind, i, source],
+            recv_sem=pair_recv.at[kind, i, source], device_id=sibling, device_id_type=MESH)
+
+    for kind, src, dst in kinds:
+        pltpu.make_async_copy(mine(kind, src, e), block(kind, dst, e, t), own_sem.at[kind]).start()
+
+    def send(k, _):
+        peer = lax.rem(e + k, groups)
+        for kind, src, dst in kinds:
+            far(kind, src, dst, peer, e).start()
+        return 0
+
+    lax.fori_loop(1, groups, send, 0)
+    for kind, src, dst in kinds:
+        pltpu.make_async_copy(mine(kind, src, e), block(kind, dst, e, t), own_sem.at[kind]).wait()
+
+    def pass_on(i):
+        for kind, src, dst in kinds:
+            for k in range(1, chips):
+                across(kind, dst, i, lax.rem(y + k, chips), y).start()
+            beside(kind, dst, i, y, c).start()
+
+    def hand_over(i):
+        for kind, src, dst in kinds:
+            for k in range(1, chips):
+                source = lax.rem(y + k, chips)
+                across(kind, dst, i, source, source).wait_recv()
+                beside(kind, dst, i, source, c).start()
+
+    pass_on(e)
+
+    def middle(k, _):
+        i = lax.rem(e + groups - k, groups)
+        for kind, src, dst in kinds:
+            far(kind, src, dst, i, i).wait_recv()
+        pass_on(i)
+        hand_over(lax.rem(i + 1, groups))
+        return 0
+
+    lax.fori_loop(1, groups, middle, 0)
+    hand_over(lax.rem(e + 1, groups))
+
+    def finish(k, _):
+        i = lax.rem(e + groups - k, groups)
+        for kind, src, dst in kinds:
+            for source in range(chips):
+                beside(kind, dst, i, source, 1 - c).wait_recv()
+                beside(kind, dst, i, source, c).wait_send()
+            for j in range(1, chips):
+                across(kind, dst, i, lax.rem(y + j, chips), y).wait_send()
+        return 0
+
+    lax.fori_loop(0, groups, finish, 0)
+
+    def drain(k, _):
+        peer = lax.rem(e + k, groups)
+        for kind, src, dst in kinds:
+            far(kind, src, dst, peer, e).wait_send()
+        return 0
+
+    lax.fori_loop(1, groups, drain, 0)
+
+
+def dispatch(rows, count, groups, members):
+    kinds, experts, slots, width = rows.shape
+    chips = members // 2
+    any_space = pl.BlockSpec(memory_space=pl.ANY)
+    dma = pltpu.SemaphoreType.DMA
+    return pl.pallas_call(
+        functools.partial(dispatch_kernel, groups, chips),
+        out_shape=(jax.ShapeDtypeStruct((kinds, experts // groups, members, groups, slots, width), BF16),
+                   jax.ShapeDtypeStruct((members, groups) + count.shape, jnp.int32)),
+        in_specs=[any_space, any_space],
+        out_specs=(any_space, any_space),
+        scratch_shapes=[dma((2,)), dma((2, groups)), dma((2, groups)), dma((2, groups, chips)), dma((2, groups, chips)),
+                        dma((2, groups, chips)), dma((2, groups, chips))],
+        compiler_params=pltpu.CompilerParams(collective_id=1, has_side_effects=True),
+        name="dispatch",
+    )(rows, count)
+
+
+def collect_kernel(groups, chips, part_ref, out_ref, own_ref, pair_ref, row_ref, ready_ref,
+                   own_sem, last_sem, pair_send, pair_recv, row_send, row_recv, far_send, far_recv):
+    e, t, y, c = entry_barrier(groups, chips)
+    kinds, held = part_ref.shape[:2]
+    sibling = (e, t + 1 - 2 * c)
+
+    def local(i, to):
+        return pltpu.make_async_copy(part_ref.at[:, :, to * 2 + c, i], own_ref.at[to, i], own_sem.at[to, i])
+
+    def beside(i, to):
+        return pltpu.make_async_remote_copy(
+            src_ref=part_ref.at[:, :, to * 2 + 1 - c, i], dst_ref=pair_ref.at[to, i], send_sem=pair_send.at[to, i],
+            recv_sem=pair_recv.at[to, i], device_id=sibling, device_id_type=MESH)
+
+    def across(i, to, source):
+        return pltpu.make_async_remote_copy(
+            src_ref=own_ref.at[to, i], dst_ref=row_ref.at[source, i], send_sem=row_send.at[to, i],
+            recv_sem=row_recv.at[source, i], device_id=(e, to * 2 + c), device_id_type=MESH)
+
+    def far(i, source):
+        return pltpu.make_async_remote_copy(
+            src_ref=ready_ref.at[i], dst_ref=out_ref.at[:, pl.ds(source * held, held)], send_sem=far_send.at[i],
+            recv_sem=far_recv.at[source], device_id=(i, t), device_id_type=MESH)
+
+    def turn(k):
+        return lax.rem(e + k, groups)
+
+    def start(k, _):
+        i = turn(k)
+        for j in range(1, chips + 1):
+            to = lax.rem(y + j, chips)
+            local(i, to).start()
+            beside(i, to).start()
+        return 0
+
+    lax.fori_loop(1, groups + 1, start, 0)
+
+    def first(k, _):
+        i = turn(k)
+        for j in range(1, chips):
+            to = lax.rem(y + j, chips)
+            local(i, to).wait()
+            beside(i, to).wait_recv()
+            for a in range(kinds):
+                for x in range(held):
+                    own_ref[to, i, a, x] = (own_ref[to, i, a, x].astype(F32) + pair_ref[to, i, a, x].astype(F32)).astype(BF16)
+            across(i, to, y).start()
+        local(i, y).wait()
+        beside(i, y).wait_recv()
+        return 0
+
+    lax.fori_loop(1, groups + 1, first, 0)
+
+    def total(i):
+        for j in range(1, chips):
+            source = lax.rem(y + j, chips)
+            across(i, source, source).wait_recv()
+        for a in range(kinds):
+            for x in range(held):
+                value = own_ref[y, i, a, x].astype(F32) + pair_ref[y, i, a, x].astype(F32)
+                for j in range(1, chips):
+                    value = value + row_ref[lax.rem(y + j, chips), i, a, x].astype(F32)
+                ready_ref[i, a, x] = value.astype(BF16)
+
+    def second(k, _):
+        i = turn(k)
+        total(i)
+        far(i, e).start()
+        return 0
+
+    lax.fori_loop(1, groups, second, 0)
+    total(e)
+    last = pltpu.make_async_copy(ready_ref.at[e], out_ref.at[:, pl.ds(e * held, held)], last_sem)
+    last.start()
+
+    def finish(k, _):
+        i = turn(k)
+        far(i, e).wait_send()
+        far(i, i).wait_recv()
+        return 0
+
+    lax.fori_loop(1, groups, finish, 0)
+
+    def drain(k, _):
+        i = turn(k)
+        for j in range(1, chips + 1):
+            beside(i, lax.rem(y + j, chips)).wait_send()
+        for j in range(1, chips):
+            across(i, lax.rem(y + j, chips), y).wait_send()
+        return 0
+
+    lax.fori_loop(1, groups + 1, drain, 0)
+    last.wait()
+
+
+def collect(parts, groups, members):
+    kinds, held, _, _, slots, width = parts.shape
+    chips = members // 2
+    any_space = pl.BlockSpec(memory_space=pl.ANY)
+    dma = pltpu.SemaphoreType.DMA
+    block = (kinds, held, slots, width)
+    return pl.pallas_call(
+        functools.partial(collect_kernel, groups, chips),
+        out_shape=jax.ShapeDtypeStruct((kinds, held * groups, slots, width), BF16),
+        in_specs=[any_space],
+        out_specs=any_space,
+        scratch_shapes=[pltpu.VMEM((chips, groups) + block, BF16), pltpu.VMEM((chips, groups) + block, BF16),
+                        pltpu.VMEM((chips, groups) + block, BF16), pltpu.VMEM((groups,) + block, BF16),
+                        dma((chips, groups)), dma(()), dma((chips, groups)), dma((chips, groups)),
+                        dma((chips, groups)), dma((chips, groups)), dma((groups,)), dma((groups,))],
+        compiler_params=pltpu.CompilerParams(collective_id=2, has_side_effects=True, vmem_limit_bytes=58 << 20),
+        name="collect",
+    )(parts)
+
+
+def expert_kernel(rows_ref, mask_ref, up_ref, down_ref, out_ref, gup_ref, gdown_ref):
+    @pl.when(pl.program_id(1) == 0)
+    def _():
+        gup_ref[...] = jnp.zeros_like(gup_ref)
+        gdown_ref[...] = jnp.zeros_like(gdown_ref)
+
+    x = rows_ref[0, 0]
+    d = (rows_ref[1, 0].astype(F32) * mask_ref[0]).astype(BF16)
+    up, down = up_ref[0], down_ref[0]
+    pre = mxu(x, up, NN)
+    cdf = 0.5 * (1.0 + lax.erf(pre * 0.7071067811865476))
+    hidden = (pre * cdf).astype(BF16)
+    slope = cdf + pre * (0.3989422804014327 * jnp.exp(-0.5 * pre * pre))
+    out_ref[0, 0] = mxu(hidden, down, NN).astype(BF16)
+    d_pre = (mxu(d, down, NT) * slope).astype(BF16)
+    out_ref[1, 0] = mxu(d_pre, up, NT).astype(BF16)
+    gdown_ref[0] += mxu(hidden, d, TN)
+    gup_ref[0] += mxu(x, d_pre, TN)
+
+
+def expert_block(rows, mask, w_up, w_down, block=256):
+    kinds, held, count, width = rows.shape
+    hidden = w_up.shape[2]
+    both = pl.BlockSpec((kinds, 1, block, width), lambda x, r: (0, x, r, 0))
+    up = pl.BlockSpec((1, width, hidden), lambda x, r: (x, 0, 0))
+    down = pl.BlockSpec((1, hidden, width), lambda x, r: (x, 0, 0))
+    return pl.pallas_call(
+        expert_kernel,
+        grid=(held, count // block),
+        out_shape=(jax.ShapeDtypeStruct(rows.shape, BF16), jax.ShapeDtypeStruct(w_up.shape, F32),
+                   jax.ShapeDtypeStruct(w_down.shape, F32)),
+        in_specs=[both, pl.BlockSpec((1, block, 1), lambda x, r: (x, r, 0)), up, down],
+        out_specs=(both, up, down),
+        compiler_params=pltpu.CompilerParams(vmem_limit_bytes=56 << 20),
+        name="experts",
+    )(rows, mask, w_up, w_down)
 
 
 def rms_scale(values, gain):
@@ -466,142 +753,93 @@
 
 
 def contract_rows(left, right):
-    return lax.dot_general(
-        left, right, (((0,), (0,)), ((), ())), preferred_element_type=jnp.float32
-    )
-
-
-def local(
-    tokens,
-    d_out,
-    segment,
-    route,
-    gain_one,
-    w_in,
-    conv_w,
-    conv_b,
-    w_x,
-    w_dt,
-    b_dt,
-    a_log,
-    d_skip,
-    w_out,
-    gain_two,
-    w_router,
-    w_up,
-    w_down,
-):
+    return lax.dot_general(left, right, TN, preferred_element_type=F32)
+
+
+def local(tokens, d_out, segment, route, gain_one, w_in, conv_w, conv_b, w_x, w_dt, b_dt, a_log, d_skip, w_out,
+          gain_two, w_router, w_up, w_down):
     length, width = tokens.shape
     inner_w = w_in.shape[1] // 2
     experts = w_router.shape[1]
-    local_experts = w_up.shape[0]
-    groups = lax.axis_size("ep")
+    held = w_up.shape[0]
+    groups, members = lax.axis_size("ep"), lax.axis_size("tp")
     slots = 3 * length // (2 * experts)
-    capacity = 5 * length * lax.axis_size("ep") * lax.axis_size("tp") // (4 * experts)
-    token_f = tokens.astype(jnp.float32)
-    valid = (segment >= 0).astype(jnp.float32)[:, None]
+    capacity = 5 * length * groups * members // (4 * experts)
     rank_dt, states = w_dt.shape[0], a_log.shape[0]
+    used = rank_dt + 2 * states
+    taps = conv_w.shape[0]
+    is_valid = segment >= 0
+    valid = is_valid.astype(F32)[:, None]
     masks = flags(segment)
     vec = jnp.concatenate([conv_w, conv_b[None], b_dt[None], d_skip[None], d_skip[None]], axis=0).astype(F32)
-    wx_pad = jnp.pad(w_x, ((0, 0), (0, 128 - rank_dt - 2 * states)))
+    wx_pad = jnp.pad(w_x, ((0, 0), (0, 128 - used)))
     wdt_pad = jnp.pad(w_dt, ((0, 128 - rank_dt), (0, 0)))
     rates = -jnp.exp(a_log.astype(F32))
-    normed_one, norm_one_pull = jax.vjp(rms_scale, token_f, gain_one.astype(jnp.float32))
-    normed_low = normed_one.astype(jnp.bfloat16)
-    both = jnp.dot(normed_low, w_in, preferred_element_type=jnp.float32)
-
-    gated_low, pre, pre_dt, scanned, proj, starts = mid_fwd(
-        both, masks, vec, wx_pad, wdt_pad, rates * LOG2E, rank_dt
-    )
-    mixed = jnp.dot(gated_low, w_out, preferred_element_type=jnp.float32)
+
+    pick_int = ((route == jnp.arange(experts, dtype=jnp.int32)[None, :]) & is_valid[:, None]).astype(jnp.int32)
+    picks = pick_int.astype(F32)
+    local_count = jnp.sum(pick_int, axis=0)
+    local_rank = jnp.sum(jnp.cumsum(pick_int, axis=0) * pick_int, axis=1) - 1
+    slot_id = jnp.where(is_valid, route[:, 0] * slots + local_rank, -1)
+    places = (jnp.arange(experts * slots, dtype=jnp.int32)[:, None] == slot_id[None, :]).astype(BF16)
+
+    token_f = tokens.astype(F32)
+    normed_one, norm_one_pull = jax.vjp(rms_scale, token_f, gain_one.astype(F32))
+    normed_low = normed_one.astype(BF16)
+    both = jnp.dot(normed_low, w_in, preferred_element_type=F32)
+    gated_low, pre, pre_dt, scanned, proj, starts = mid_fwd(both, masks, vec, wx_pad, wdt_pad, rates * LOG2E, rank_dt)
+    mixed = jnp.dot(gated_low, w_out, preferred_element_type=F32)
     after_mix = token_f + mixed * valid
-    normed_two, norm_two_pull = jax.vjp(rms_scale, after_mix, gain_two.astype(jnp.float32))
-    pick_int = (
-        (route == jnp.arange(experts, dtype=jnp.int32)[None, :]) & (segment >= 0)[:, None]
-    ).astype(jnp.int32)
-    picks = pick_int.astype(jnp.float32)
+    normed_two, norm_two_pull = jax.vjp(rms_scale, after_mix, gain_two.astype(F32))
 
     def router(normed_in, router_w):
         probs = jax.nn.softmax(jnp.dot(normed_in, router_w, precision=HIGH), axis=-1)
         return jnp.sum(probs * picks, axis=-1)
 
-    gate, router_pull = jax.vjp(router, normed_two, w_router.astype(jnp.float32))
-    local_count = jnp.sum(pick_int, axis=0)
-    everyone = lax.all_gather(local_count, ("ep", "tp"))
-    earlier = jnp.arange(everyone.shape[0]) < lax.axis_index(("ep", "tp"))
-    prior = jnp.sum(jnp.where(earlier[:, None], everyone, 0), axis=0)
+    gate, router_pull = jax.vjp(router, normed_two, w_router.astype(F32))
+    upstream = d_out.astype(F32)
+    leaving = jnp.stack(
+        [
+            jnp.dot(places, normed_two.astype(BF16), preferred_element_type=F32).astype(BF16),
+            jnp.dot(places, (gate[:, None] * upstream).astype(BF16), preferred_element_type=F32).astype(BF16),
+        ]
+    ).reshape(2, experts, slots, width)
+    count_tile = jnp.broadcast_to(jnp.pad(local_count, (0, 128 - experts))[None], (8, 128))
+    rows, table = dispatch(leaving, count_tile, groups, members)
+
+    everyone = table[:, :, 0, :experts].transpose(1, 0, 2).reshape(groups * members, experts)
+    device = jnp.arange(groups * members)
+    before = device[None, :] < device[:, None]
+    prior = jnp.sum(jnp.where(before[:, :, None], everyone[None], 0), axis=1)
     named = jnp.sum(everyone, axis=0)
-    local_rank = jnp.sum(jnp.cumsum(pick_int, axis=0) * pick_int, axis=1) - 1
-    global_rank = jnp.sum(pick_int * prior[None, :], axis=1) + local_rank
-    kept = (segment >= 0) & (global_rank < capacity)
-    slot_id = jnp.where(kept, route[:, 0] * slots + local_rank, -1)
-    dispatch = (jnp.arange(experts * slots, dtype=jnp.int32)[:, None] == slot_id[None, :]).astype(
-        jnp.bfloat16
-    )
-    expert_in = normed_two.astype(jnp.bfloat16)
-    outgoing = jnp.dot(dispatch, expert_in, preferred_element_type=jnp.float32).astype(jnp.bfloat16)
-    outgoing = outgoing.reshape(groups, local_experts, slots, width)
-    received = lax.all_to_all(outgoing, "ep", split_axis=0, concat_axis=2, tiled=True)
-    full_up, full_down = (w_up, w_down)
-    expert_rows = lax.all_gather(received, "tp", axis=2, tiled=True)
-    hidden_pre = jnp.einsum(
-        "axrd,xdf->axrf", expert_rows, full_up, preferred_element_type=jnp.float32
-    )
-    gelu_value, gelu_pull = jax.vjp(partial(jax.nn.gelu, approximate=False), hidden_pre)
-    hidden_low = gelu_value.astype(jnp.bfloat16)
-    terms = jnp.einsum("axrf,xfd->axrd", hidden_low, full_down, preferred_element_type=jnp.float32)
-    expert_out = lax.psum_scatter(terms, "tp", scatter_dimension=2, tiled=True)
-    returned = lax.all_to_all(
-        expert_out.astype(jnp.bfloat16), "ep", split_axis=2, concat_axis=0, tiled=True
-    )
-    returned = returned.reshape(experts * slots, width)
-    token_out = contract_rows(dispatch, returned)
-    keep_f = kept.astype(jnp.float32)[:, None]
-    weighting = gate[:, None] * keep_f
-    final = after_mix + weighting * token_out
-    upstream = d_out.astype(jnp.float32)
-    d_token_out = (weighting * upstream).astype(jnp.bfloat16)
-    d_slots = jnp.dot(dispatch, d_token_out, preferred_element_type=jnp.float32).astype(
-        jnp.bfloat16
-    )
-    d_slots = d_slots.reshape(groups, local_experts, slots, width)
-    d_gate = keep_f[:, 0] * jnp.sum(upstream * token_out, axis=1)
-    d_received = lax.all_to_all(d_slots, "ep", split_axis=0, concat_axis=2, tiled=True)
-    d_rows_all = lax.all_gather(d_received, "tp", axis=2, tiled=True)
-    gelu_back, hidden_back = gelu_pull, hidden_low
-    grad_down = jnp.einsum(
-        "axrf,axrd->xfd", hidden_back, d_rows_all, preferred_element_type=jnp.float32
-    )
-    d_hidden = jnp.einsum(
-        "axrd,xfd->axrf", d_rows_all, full_down, preferred_element_type=jnp.float32
-    )
-    d_pre = gelu_back(d_hidden)[0].astype(jnp.bfloat16)
-    grad_up = jnp.einsum("axrd,axrf->xdf", expert_rows, d_pre, preferred_element_type=jnp.float32)
-    row_terms = jnp.einsum("axrf,xdf->axrd", d_pre, full_up, preferred_element_type=jnp.float32)
-    d_expert_in = lax.psum_scatter(row_terms, "tp", scatter_dimension=2, tiled=True)
-    d_back = lax.all_to_all(
-        d_expert_in.astype(jnp.bfloat16), "ep", split_axis=2, concat_axis=0, tiled=True
-    )
-    d_normed = contract_rows(dispatch, d_back.reshape(experts * slots, width))
+    counts = jnp.stack([named, jnp.maximum(named - capacity, 0)])
+    mine = lax.dynamic_slice_in_dim(prior.reshape(groups, members, experts), lax.axis_index("ep") * held, held, 2)
+    room = mine.transpose(2, 1, 0)[..., None] + jnp.arange(slots)[None, None, None] < capacity
+    room = room.reshape(held, members * groups * slots, 1).astype(F32)
+    here = jnp.sum(jnp.where((device == lax.axis_index(("ep", "tp")))[:, None], prior, 0), axis=0)
+    keep = (is_valid & (jnp.sum(pick_int * here[None, :], axis=1) + local_rank < capacity)).astype(F32)[:, None]
+
+    parts, grad_up, grad_down = expert_block(rows.reshape(2, held, members * groups * slots, width), room, w_up, w_down)
+    returned = collect(parts.reshape(rows.shape), groups, members).reshape(2, experts * slots, width)
+    token_out = contract_rows(places, returned[0])
+    d_normed = contract_rows(places, returned[1])
+
+    final = after_mix + gate[:, None] * keep * token_out
+    d_gate = keep[:, 0] * jnp.sum(upstream * token_out, axis=1)
     d_norm_router, grad_router = router_pull(d_gate)
     d_after, grad_gain_two = norm_two_pull(d_normed + d_norm_router)
     d_after = d_after + upstream
-    d_mixed = (d_after * valid).astype(jnp.bfloat16)
+    d_mixed = (d_after * valid).astype(BF16)
     grad_out = contract_rows(gated_low, d_mixed)
-    d_gated = lax.dot_general(
-        d_mixed, w_out, (((1,), (1,)), ((), ())), preferred_element_type=jnp.float32
-    )
+    d_gated = lax.dot_general(d_mixed, w_out, NT, preferred_element_type=F32)
     d_both, grad_vec, grad_x, grad_dt, grad_rates = mid_bwd(
         both, d_gated, pre, pre_dt, scanned, proj, starts, masks, vec, wx_pad.T, wdt_pad, rates * LOG2E, rank_dt
     )
     grad_in = contract_rows(normed_low, d_both)
-    d_normed_one = lax.dot_general(
-        d_both, w_in, (((1,), (1,)), ((), ())), preferred_element_type=jnp.float32
-    )
+    d_normed_one = lax.dot_general(d_both, w_in, NT, preferred_element_type=F32)
     d_tokens_norm, grad_gain_one = norm_one_pull(d_normed_one)
     d_tokens = d_after + d_tokens_norm
-    counts = jnp.stack([named, jnp.maximum(named - capacity, 0)])
-    used = rank_dt + 2 * states
+
     small = jnp.concatenate(
         [
             grad_x[:used],
@@ -614,33 +852,26 @@
         axis=0,
     )
     rows_used = small.shape[0]
-    small = jnp.pad(small, ((0, 256 - rows_used), (0, 0))).T
-    tall = grad_in.astype(jnp.bfloat16).reshape(width // 256, 256, 2 * inner_w // 1024, 1024)
-    tall = tall.transpose(0, 2, 1, 3).reshape(-1, 256, 1024)
-    wide = jnp.concatenate([grad_out.astype(jnp.bfloat16), small.astype(jnp.bfloat16)], axis=1)
-    summed = all_sum(jnp.concatenate([tall, wide.reshape(-1, 256, 1024)], axis=0), groups, lax.axis_size("tp"))
-    total_in = summed[: tall.shape[0]].reshape(width // 256, 2 * inner_w // 1024, 256, 1024)
-    total_in = total_in.transpose(0, 2, 1, 3).reshape(width, 2 * inner_w).astype(jnp.float32)
-    wide = summed[tall.shape[0] :].reshape(inner_w, 1024)
-    total_out = wide[:, :width].astype(jnp.float32)
-    small = wide[:, width:].astype(jnp.float32).T
+    small = jnp.pad(small, ((0, 256 - rows_used), (0, 0))).astype(BF16).T
+    wide = jnp.concatenate([grad_out.astype(BF16), small], axis=1)
+    total_in, wide = all_sum(grad_in.astype(BF16), wide, groups, members)
+    small = wide[:, width:].astype(F32).T
     at = used + rank_dt + states
-    taps = conv_w.shape[0]
     gains = small[at + 8].reshape(2, width)
     return (
-        final.astype(jnp.bfloat16),
+        final.astype(BF16),
         d_tokens,
         counts,
         gains[0],
-        total_in,
+        total_in.astype(F32),
         small[at : at + taps],
         small[at + taps],
-        small[:used].T,
+        wide[:, width : width + used].astype(F32),
         small[used : used + rank_dt],
         small[at + taps + 1],
         small[used + rank_dt : at],
         small[at + taps + 2],
-        total_out,
+        wide[:, :width].astype(F32),
         gains[1],
         small[at + 9 : rows_used].reshape(experts, width).T,
         grad_up,

time: 889 us -> 534 us (0.60)
  waiting for transfers between devices: 253 us -> 0 us
  Pallas kernels: 219 us -> 409 us
  blocking collectives: 104 us -> 0 us
  matrix products: 139 us -> 40.1 us
  local copies, waits for them, and re-layouts: 109 us -> 45.3 us
  between operations: 15 us -> 1.64 us
  starting transfers between devices: 11.3 us -> 0 us
    pallas_call x1 -> x4, Pallas kernels: 107 us -> 296 us  [the longest x1 111 us: all_sum(): pl.pallas_call(functools.partial(sum_kernel, orders), out_shape=(jax.Shap...]
    reduce_scatter x2 -> x0, waiting for transfers between devices: 153 us -> none  [the longest x1 78.2 us: local(): expert_out = lax.psum_scatter(terms, 'tp', scatter_dimension=2, tiled=True)]
    dot_general x16 -> x10, matrix products: 134 us -> 36.8 us  [the longest x4 11.7 us: contract_rows(): return lax.dot_general(left, right, TN, preferred_element_type=F32)]
    all_gather x2 -> x0, waiting for transfers between devices: 75.7 us -> none  [the longest x1 38.6 us: local(): expert_rows = lax.all_gather(received, 'tp', axis=2, tiled=True)]
    all_to_all x2 -> x0, blocking collectives: 63 us -> none  [the longest x1 32.1 us: local(): lax.all_to_all(d_slots, 'ep', split_axis=0, concat_axis=2, tiled=True)]
    unnamed x1 -> x0, blocking collectives: 40.6 us -> none
    unnamed x127 -> x95, local copies, waits for them, and re-layouts: 40.1 us -> 13.2 us
    all_to_all x2 -> x0, waiting for transfers between devices: 24 us -> none  [the longest x1 24 us: local(): lax.all_to_all(expert_out.astype(jnp.bfloat16), 'ep', split_axis=2, conca...]
  transfers between devices with their start and end apart: 6 -> 0, of which waited for: 5 -> 0; matrix products, arithmetic and copies ran while one was open for 5% -> 0% of each run, Pallas kernels for 0% -> 0%
where the time goes in v3:
time: 534 us; the launch traced here: 530 us
  Pallas kernels  409 us (77%)
  local copies, waits for them, and re-layouts  45.3 us (8%)
  matrix products  40.1 us (8%)
  other arithmetic  34.7 us (6%)
    pallas_call x1, Pallas kernels, all_sum(): pl.pallas_call(functools.partial(sum_kernel, orders), out_shape=(jax.Shap...  111 us
    pallas_call x1, Pallas kernels, collect(): pl.pallas_call(functools.partial(collect_kernel, groups, chips), out_shap...  77.5 us
    pallas_call x1, Pallas kernels, mid_bwd(): pl.pallas_call(functools.partial(mid_bwd_kernel, rank), grid=(blocks,), o...  76.7 us
    pallas_call x1, Pallas kernels, dispatch(): pl.pallas_call(functools.partial(dispatch_kernel, groups, chips), out_sha...  76.7 us
    pallas_call x1, Pallas kernels, mid_fwd(): pl.pallas_call(functools.partial(mid_fwd_kernel, rank), grid=(length // T...  35.4 us
    pallas_call x1, Pallas kernels, expert_block(): pl.pallas_call(expert_kernel, grid=(held, count // block), out_shape=(jax...  31.6 us
    unnamed x95, local copies, waits for them, and re-layouts  13.2 us
    dot_general x4, matrix products, contract_rows(): return lax.dot_general(left, right, TN, preferred_element_type=F32)  11.7 us

profile of v3, /device:TPU:1, one launch (start us, length us, event | category | flops | bytes accessed | tf_op | source)
XLA Modules:
  0.0 530.3 jit_solution(147574733412710420)
XLA Ops:
  0.7 0.9 fusion.60
  1.6 0.8 fusion.61
  2.4 0.8 fusion.62
  3.2 1.3 fusion.58
  4.5 0.5 copy-done.26
  5.4 1.5 fusion.7
  6.8 0.5 copy-done.30
  7.4 0.7 convert_element_type.85
  8.1 8.1 %fusion.34.both_ref = f32[512,3072]{1,0:T(8,128)} fusion(bf16[768,3072]{1,0:T(8,128)(2,1)} %param.23, bf16[512,768]{1,0:T(8,128)(2,1)} %param.18, f32[768]{0:T(1024)S(1)} %convert_element_type.85, f32[512]{0:T(512)S(1)} %fusion.52), kind=kOutput, calls=%fused_computation.67 | convolution fusion | flops 2417491968 | bytes 11801600 | tf_op jit(solution)/shard_map/dot_general | solution.py:789
  16.2 0.7 exponential_negate_fusion
  17.0 1.2 copy.144
  18.3 35.4 %mid_fwd.1 = (bf16[512,1536]{1,0:T(8,128)(2,1)S(1)}, f32[512,1536]{1,0:T(8,128)S(1)}, f32[512,1536]{1,0:T(8,128)S(1)}, f32[512,1536]{1,0:T(8,128)S(1)}, f32[512,128]{1,0:T(8,128)S(1)}, /*index=5*/f32[32,16,1536]{2,1,0:T(8,128)}) custom-call(f32[512,3072]{1,0:T(8,128)} %fusion.34.both_ref, f32[512,8]{1,0:T(8,128)S(1)} %convert_element_type.87.mask_ref, ...), custom_call_target="tpu_custom_call" | custom-call | tf_op jit(solution)/shard_map/mid_fwd/pallas_call | solution.py:121
  53.8 1.6 copy-done.5
  55.5 3.1 multiply_reduce_fusion.2
  58.7 0.6 copy-done.10
  59.3 1.2 reduce-window.6
  60.9 2.5 fusion.14
  63.4 1.0 fusion.63
  64.5 0.9 fusion.15
  65.5 1.6 pad_maximum_fusion.1.rows_ref
  67.1 0.6 broadcast_in_dim.97.count_ref
  67.7 76.7 %dispatch.1 = (bf16[2,2,4,8,48,768]{5,4,3,2,1,0:T(8,128)(2,1)}, s32[4,8,8,128]{3,2,1,0:T(8,128)}) custom-call(bf16[2,16,48,768]{3,2,1,0:T(8,128)(2,1)} %pad_maximum_fusion.1.rows_ref, s32[8,128]{1,0:T(8,128)} %broadcast_in_dim.97.count_ref), custom_call_target="tpu_custom_call" | custom-call | tf_op jit(solution)/shard_map/dispatch/pallas_call | solution.py:585
  144.4 1.0 slice_reduce_fusion.6
  145.4 0.6 select_reduce_fusion
  146.3 2.0 add.116
  148.3 2.8 fusion.13.mask_ref
  151.2 31.6 %experts.1 = (bf16[2,2,1536,768]{3,2,1,0:T(8,128)(2,1)}, f32[2,768,768]{2,1,0:T(8,128)}, f32[2,768,768]{2,1,0:T(8,128)}) custom-call(bf16[2,2,1536,768]{3,2,1,0:T(8,128)(2,1)} %bitcast.57, f32[2,1536,1]{2,1,0:T(8,128)} %fusion.13.mask_ref, bf16[2,768,768]{2,1,0:T(8,128)(2,1)} %up_ref.1, bf16[2,768,768]{2,1,0:T(8,128)(2,1)} %down_ref.1), custom_call_target="tpu_custom_call" | custom-call | tf_op jit(solution)/shard_map/experts/pallas_call | solution.py:739
  182.8 77.5 %collect.1 = bf16[2,16,48,768]{3,2,1,0:T(8,128)(2,1)} custom-call(bf16[2,2,4,8,48,768]{5,4,3,2,1,0:T(8,128)(2,1)} %bitcast.56), custom_call_target="tpu_custom_call" | custom-call | tf_op jit(solution)/shard_map/collect/pallas_call | solution.py:699
  260.3 2.8 fusion.59
  263.1 2.1 fusion.5
  265.4 2.3 fusion.9
  267.7 1.2 multiply_reduce_fusion
  269.1 1.4 convert_add_fusion.1
  270.6 2.9 convolution_convert_fusion.1
  273.5 1.0 fusion.19
  274.8 4.7 fusion.56.dg_ref
  279.5 0.8 pad_bitcast_fusion.1.wxt_ref
  280.3 76.7 %mid_bwd.1 = (bf16[512,3072]{1,0:T(8,128)(2,1)}, f32[8,1536]{1,0:T(8,128)}, f32[128,1536]{1,0:T(8,128)}, f32[128,1536]{1,0:T(8,128)}, f32[16,1536]{1,0:T(8,128)}) custom-call(f32[512,3072]{1,0:T(8,128)} %fusion.34.both_ref, f32[512,1536]{1,0:T(8,128)} %fusion.56.dg_ref, f32[512,1536]{1,0:T(8,128)} %copy-done.3, f32[512,1536]{1,0:T(8,128)} %copy-done.4, ...), custom_call_target="tpu_custom_call" | custom-call | tf_op jit(solution)/shard_map/mid_bwd/pallas_call | solution.py:284
  357.1 5.9 %fusion.3 = (bf16[768]{0:T(1024)(128)(2,1)S(1)}, f32[512]{0:T(512)S(1)}, f32[512,768]{1,0:T(8,128)}) fusion(bf16[512,768]{1,0:T(8,128)(2,1)S(1)} %copy-done.16, f32[512]{0:T(512)S(1)} %copy-done.36, f32[768]{0:T(1024)S(1)} %copy-done.33, bf16[512,3072]{1,0:T(8,128)(2,1)} %get-tuple-element.44, bf16[768,3072]{1,0:T(8,128)(2,1)S(1)} %bitcast.79), kind=kOutput, calls=%fused_computation.18 | convolution fusion | flops 2418670336 | bytes 10232320 | tf_op jit(solution)/shard_map/dot_general | solution.py:839
  363.0 0.3 broadcast_in_dim.108
  363.8 0.8 multiply_convert_fusion.1
  364.9 1.4 copy.129
  366.5 2.4 concatenate.41
  369.0 3.9 pad_maximum_fusion.wide_ref
  372.9 4.5 convolution_convert_fusion.tall_ref
  377.4 110.7 %all_sum.1 = (bf16[768,3072]{1,0:T(8,128)(2,1)}, bf16[1536,1024]{1,0:T(8,128)(2,1)S(1)}) custom-call(bf16[768,3072]{1,0:T(8,128)(2,1)} %convolution_convert_fusion.tall_ref, bf16[1536,1024]{1,0:T(8,128)(2,1)} %pad_maximum_fusion.wide_ref), custom_call_target="tpu_custom_call" | custom-call | tf_op jit(solution)/shard_map/all_sum/pallas_call | solution.py:463
  488.1 7.4 %convert_element_type.105 = f32[768,3072]{1,0:T(8,128)} convert(bf16[768,3072]{1,0:T(8,128)(2,1)} %get-tuple-element.50) | non-fusion elementwise | flops 2359296 | bytes 14155776 | tf_op jit(solution)/shard_map/convert_element_type | solution.py:866
  495.4 2.6 slice_convert_fusion
  498.1 1.3 convert_bitcast_fusion
  499.4 2.3 slice.115
  501.7 2.1 copy.139
  503.8 2.3 slice.120
  506.1 1.4 copy.136
  507.4 0.6 reshape.227
  508.1 2.1 slice.117
  510.1 2.0 copy.140
  512.1 2.3 slice.113
  514.4 2.0 copy.137
  516.4 3.8 slice_reduce_fusion
  520.2 2.2 slice_reduce_fusion.3
  522.5 1.0 slice_convert_fusion.3
  523.4 2.2 copy.138
  525.6 3.8 fusion.6
  529.5 0.6 pad_add_fusion
  (143 shorter events, 3.5 us)
Async XLA Ops:
  0.7 54.8 %copy-start = (bf16[1536,768]{1,0:T(8,128)(2,1)S(1)}, bf16[1536,768]{1,0:T(8,128)(2,1)}, u32[]{:S(2)}) copy-start(bf16[1536,768]{1,0:T(8,128)(2,1)} %param.31) | copy-start | bytes 7077892
  4.5 0.5 copy-start.26
  5.4 13.0 %copy-start.6 = (f32[512,8]{1,0:T(8,128)}, f32[512,8]{1,0:T(8,128)S(1)}, u32[]{:S(2)}) copy-start(f32[512,8]{1,0:T(8,128)S(1)} %convert_element_type.87.mask_ref) | copy-start | bytes 49156
  6.8 0.5 copy-start.30
  7.3 0.7 copy-start.35
  8.0 8.1 %copy-start.32 = (f32[768]{0:T(1024)}, f32[768]{0:T(1024)S(1)}, u32[]{:S(2)}) copy-start(f32[768]{0:T(1024)S(1)} %convert_element_type.85) | copy-start | bytes 9220
  8.0 8.1 %copy-start.29 = (bf16[16,1536]{1,0:T(8,128)(2,1)S(1)}, bf16[16,1536]{1,0:T(8,128)(2,1)}, u32[]{:S(2)}) copy-start(bf16[16,1536]{1,0:T(8,128)(2,1)} %param.29) | copy-start | bytes 147460
  8.0 8.8 %copy-start.22 = (bf16[48,1536]{1,0:T(8,128)(2,1)S(1)}, bf16[48,1536]{1,0:T(8,128)(2,1)}, u32[]{:S(2)}) copy-start(bf16[48,1536]{1,0:T(8,128)(2,1)} %param.27) | copy-start | bytes 442372
  8.1 8.8 %copy-start.37 = (bf16[1536]{0:T(1024)(128)(2,1)S(1)}, bf16[1536]{0:T(1024)(128)(2,1)}, u32[]{:S(2)}) copy-start(bf16[1536]{0:T(1024)(128)(2,1)} %param.25) | copy-start | bytes 9220
  8.1 8.8 %copy-start.38 = (bf16[1536]{0:T(1024)(128)(2,1)S(1)}, bf16[1536]{0:T(1024)(128)(2,1)}, u32[]{:S(2)}) copy-start(bf16[1536]{0:T(1024)(128)(2,1)} %param.28) | copy-start | bytes 9220
  8.1 8.8 %copy-start.39 = (bf16[1536]{0:T(1024)(128)(2,1)S(1)}, bf16[1536]{0:T(1024)(128)(2,1)}, u32[]{:S(2)}) copy-start(bf16[1536]{0:T(1024)(128)(2,1)} %param.30) | copy-start | bytes 9220
  8.1 8.9 %copy-start.34 = (bf16[4,1536]{1,0:T(4,128)(2,1)S(1)}, bf16[4,1536]{1,0:T(4,128)(2,1)}, u32[]{:S(2)}) copy-start(bf16[4,1536]{1,0:T(4,128)(2,1)} %param.24) | copy-start | bytes 36868
  16.8 36.9 %copy-start.7 = (f32[16,1536]{1,0:T(8,128)}, f32[16,1536]{1,0:T(8,128)S(1)}, u32[]{:S(2)}) copy-start(f32[16,1536]{1,0:T(8,128)S(1)} %get-tuple-element.160.rates_ref) | copy-start | bytes 294916
  16.9 36.9 %copy-start.2 = (bf16[128,1536]{1,0:T(8,128)(2,1)}, bf16[128,1536]{1,0:T(8,128)(2,1)S(1)}, u32[]{:S(2)}) copy-start(bf16[128,1536]{1,0:T(8,128)(2,1)S(1)} %pad.22.wdt_ref) | copy-start | bytes 1179652
  17.0 36.7 %copy-start.8 = (f32[8,1536]{1,0:T(8,128)}, f32[8,1536]{1,0:T(8,128)S(1)}, u32[]{:S(2)}) copy-start(f32[8,1536]{1,0:T(8,128)S(1)} %convert_element_type.88.vec_ref) | copy-start | bytes 147460
  18.3 37.1 %copy-start.15 = (bf16[512,768]{1,0:T(8,128)(2,1)S(1)}, bf16[512,768]{1,0:T(8,128)(2,1)}, u32[]{:S(2)}) copy-start(bf16[512,768]{1,0:T(8,128)(2,1)} %param.18) | copy-start | bytes 2359300
  18.3 37.1 %copy-start.41 = (f32[512]{0:T(512)S(1)}, f32[512]{0:T(512)}, u32[]{:S(2)}) copy-start(f32[512]{0:T(512)} %get-tuple-element.151) | copy-start | bytes 6148
  53.8 1.7 copy-start.5
  55.4 3.2 copy-start.3
  55.4 3.2 copy-start.4
  55.4 3.2 copy-start.9
  55.4 3.8 copy-start.10
  55.5 3.8 copy-start.23
  55.5 3.8 copy-start.27
  55.5 5.4 %copy-start.40 = (bf16[768]{0:T(1024)(128)(2,1)S(1)}, bf16[768]{0:T(1024)(128)(2,1)}, u32[]{:S(2)}) copy-start(bf16[768]{0:T(1024)(128)(2,1)} %param.32) | copy-start | bytes 4612
  60.9 2.5 copy-start.12
  60.9 2.5 copy-start.24
  63.4 1.1 copy-start.19
  265.4 2.3 copy-start.13
  267.7 1.4 copy-start.17
  269.1 1.4 copy-start.11
  270.6 2.9 copy-start.14
  274.8 4.7 copy-start.18
  274.8 82.2 %slice-start = ((s8[4718592]{0:T(1024)(128)(4,1)}), s8[4194304]{0:T(1024)(128)(4,1)S(1)}, s32[]{:S(2)}) async-start(s8[4718592]{0:T(1024)(128)(4,1)} %bitcast.78), calls=%async_computation | async-start | bytes 8388608
  280.3 76.8 %copy-start.16 = (bf16[512,768]{1,0:T(8,128)(2,1)S(1)}, bf16[512,768]{1,0:T(8,128)(2,1)}, u32[]{:S(2)}) copy-start(bf16[512,768]{1,0:T(8,128)(2,1)} %param.18) | copy-start | bytes 2359300
  280.3 76.8 %copy-start.33 = (f32[768]{0:T(1024)S(1)}, f32[768]{0:T(1024)}, u32[]{:S(2)}) copy-start(f32[768]{0:T(1024)} %copy-done.32) | copy-start | bytes 9220
  280.3 76.8 %copy-start.36 = (f32[512]{0:T(512)S(1)}, f32[512]{0:T(512)}, u32[]{:S(2)}) copy-start(f32[512]{0:T(512)} %copy-done.35) | copy-start | bytes 6148
  280.3 76.8 %slice-start.1 = ((s8[4718592]{0:T(1024)(128)(4,1)}), s8[524288]{0:T(1024)(128)(4,1)S(1)}, s32[]{:S(2)}) async-start(s8[4718592]{0:T(1024)(128)(4,1)} %bitcast.78), calls=%async_computation.1 | async-start | bytes 1048576
  357.1 6.2 %copy-start.25 = (f32[16,1536]{1,0:T(8,128)S(1)}, f32[16,1536]{1,0:T(8,128)}, u32[]{:S(2)}) copy-start(f32[16,1536]{1,0:T(8,128)} %get-tuple-element.47) | copy-start | bytes 294916
  357.1 6.5 %copy-start.21 = (f32[16,1536]{1,0:T(8,128)S(1)}, f32[16,1536]{1,0:T(8,128)}, u32[]{:S(2)}) copy-start(f32[16,1536]{1,0:T(8,128)} %get-tuple-element.159) | copy-start | bytes 294916
  363.5 1.1 copy-start.28
  364.6 1.6 copy-start.20
  369.0 3.9 copy-start.42
  520.2 5.4 %copy-start.31 = (f32[512]{0:T(512)S(1)}, f32[512]{0:T(512)}, u32[]{:S(2)}) copy-start(f32[512]{0:T(512)} %copy-done.30) | copy-start | bytes 6148
  525.6 4.4 copy-start.1

commit v4 on v3

v4 whole, which is shorter than its diff:
```python
import functools

import jax
import jax.numpy as jnp
from jax import lax
from jax.experimental import pallas as pl
from jax.experimental.pallas import tpu as pltpu
from jax.sharding import PartitionSpec as P

EPS = 1e-06
MESH = pl.DeviceIdType.MESH
TB = 128
CH = 16
LB = 256
LOG2E = 1.4426950408889634
LN2 = 0.6931471805599453
F32 = jnp.float32
BF16 = jnp.bfloat16
NN = (((1,), (0,)), ((), ()))
NT = (((1,), (1,)), ((), ()))
TN = (((0,), (0,)), ((), ()))


def mxu(left, right, dims):
    return lax.dot_general(left, right, dims, preferred_element_type=F32)


def split(x):
    high = x.astype(BF16)
    return high, (x - high.astype(F32)).astype(BF16)


def dot2(x, w, dims):
    high, rest = split(x)
    return mxu(high, w, dims) + mxu(rest, w, dims)


def dot3(x, w, dims):
    high, rest = split(x)
    high_w, rest_w = split(w)
    return mxu(high, high_w, dims) + mxu(high, rest_w, dims) + mxu(rest, high_w, dims)


def sigmoid(x):
    return 1.0 / (1.0 + jnp.exp(-x))


def softplus(x):
    return jnp.maximum(x, 0.0) + jnp.log1p(jnp.exp(-jnp.abs(x)))


def row_sums(items):
    items = [sum((x[8 * i:8 * i + 8] for i in range(1, x.shape[0] // 8)), x[:8]) for x in items]
    place = lax.broadcasted_iota(jnp.int32, items[0].shape, 0)
    for level in (1, 2, 4):
        odd = (place // level) % 2 == 1
        merged = []
        for low, high in zip(items[::2], items[1::2]):
            merged.append(jnp.where(odd, high, low) + pltpu.roll(jnp.where(odd, low, high), level, 0))
        items = merged
    return items[0]


def mid_fwd_kernel(rank, both_ref, segment_ref, vec_ref, wx_ref, wdt_ref, rates_ref,
                   gated_ref, conv_ref, bend_ref, step_ref, rise_ref, gate_ref, slope_ref, proj_ref, hs_ref,
                   ext_ref, h_ref, turned_ref, seg_ref, spread_ref, decay_ref, source_ref, pdt_ref):
    states, width = rates_ref.shape

    @pl.when(pl.program_id(0) == 0)
    def _():
        ext_ref[:8, :] = jnp.zeros((8, width), F32)
        seg_ref[:8, :] = jnp.full((8, 128), -2, jnp.int32)
        h_ref[...] = jnp.zeros_like(h_ref)

    @pl.when(pl.program_id(0) > 0)
    def _():
        ext_ref[:8, :] = ext_ref[TB:, :]
        seg_ref[:8, :] = seg_ref[TB:, :]

    seg_ref[8:, :] = segment_ref[...]

    def same(c, k):
        at = c * CH + 8
        return (seg_ref[at - k:at - k + CH, :] == seg_ref[at:at + CH, :]).astype(F32)[:, :1]

    def conv_chunk(c):
        rows = slice(c * CH, c * CH + CH)
        masks = [same(c, k) for k in range(1, 4)]
        for b in range(width // LB):
            lanes = slice(b * LB, (b + 1) * LB)
            at = c * CH + 8
            here = both_ref[rows, lanes]
            ext_ref[at:at + CH, lanes] = here
            total = vec_ref[4:5, lanes] + vec_ref[3:4, lanes] * here
            for k in range(1, 4):
                total = total + vec_ref[3 - k:4 - k, lanes] * ext_ref[at - k:at - k + CH, lanes] * masks[k - 1]
            sig = sigmoid(total)
            conv_ref[rows, lanes] = total * sig
            bend_ref[rows, lanes] = sig * (1.0 + total * (1.0 - sig))

    for c in range(TB // CH):
        conv_chunk(c)
    proj = dot2(conv_ref[...], wx_ref[...], NN)
    lane = lax.broadcasted_iota(jnp.int32, (TB, 128), 1)
    keep = (seg_ref[7:7 + TB, :] == seg_ref[8:, :]).astype(F32)
    proj_ref[...] = jnp.where(lane == 127, keep, proj)
    turned_ref[...] = proj.T
    pdt_ref[...] = dot2(proj, wdt_ref[...], NN) + vec_ref[5:6, :]

    def every(ref, k):
        row = ref[pl.ds(k, 8, stride=0), :]
        return jnp.concatenate([row] * (states // 8), axis=0)

    def wide(k, side):
        return jnp.concatenate([spread_ref[k, side * states:(side + 1) * states, :]] * (LB // 128), axis=1)

    def scan_chunk(c, _):
        rows = pl.ds(pl.multiple_of(c * CH, CH), CH)
        tile = pltpu.roll(turned_ref[rank:rank + 2 * states, :], TB - c * CH, 1)
        keep = proj_ref[rows, 127:]
        for k in range(CH):
            spread_ref[k] = jnp.broadcast_to(tile[:, k:k + 1], (2 * states, 128))
        for b in range(width // LB):
            lanes = slice(b * LB, (b + 1) * LB)
            rates = rates_ref[:, lanes]
            h = h_ref[:, lanes]
            hs_ref[c, :, lanes] = h
            conv = conv_ref[rows, lanes]
            pdt = pdt_ref[rows, lanes]
            step = softplus(pdt)
            step_ref[rows, lanes] = step
            rise_ref[rows, lanes] = sigmoid(pdt)
            source_ref[b, :CH] = step * conv
            decay_ref[b, :CH] = jnp.where(keep > 0.0, step, 1e4)
            outs = []
            for k in range(CH):
                h = jnp.exp2(every(decay_ref.at[b], k) * rates) * h + wide(k, 0) * every(source_ref.at[b], k)
                outs.append(wide(k, 1) * h)
            h_ref[:, lanes] = h
            y = jnp.concatenate([row_sums(outs[:8]), row_sums(outs[8:])], axis=0)
            gate = both_ref[rows, width + b * LB:width + (b + 1) * LB]
            sig = sigmoid(gate)
            mixed = y + vec_ref[6:7, lanes] * conv
            gate_ref[rows, lanes] = gate * sig
            gated_ref[rows, lanes] = (mixed * (gate * sig)).astype(BF16)
            slope_ref[rows, lanes] = mixed * (sig * (1.0 + gate * (1.0 - sig)))
        return 0

    lax.fori_loop(0, TB // CH, scan_chunk, 0)


def mid_fwd(both, segment, vec, wx, wdt, rates, rank):
    length = both.shape[0]
    states, width = rates.shape
    row = lambda i: (i, 0)
    fix = lambda i: (0, 0)
    tall = pl.BlockSpec((TB, width), row)
    like = jax.ShapeDtypeStruct((length, width), F32)
    return pl.pallas_call(
        functools.partial(mid_fwd_kernel, rank),
        grid=(length // TB,),
        out_shape=(jax.ShapeDtypeStruct((length, width), BF16), like, like, like, like, like, like,
                   jax.ShapeDtypeStruct((length, 128), F32),
                   jax.ShapeDtypeStruct((length // CH, states, width), F32)),
        in_specs=[pl.BlockSpec((TB, 2 * width), row), pl.BlockSpec((TB, 128), row), pl.BlockSpec(vec.shape, fix),
                  pl.BlockSpec(wx.shape, fix), pl.BlockSpec(wdt.shape, fix), pl.BlockSpec(rates.shape, fix)],
        out_specs=(tall, tall, tall, tall, tall, tall, tall, pl.BlockSpec((TB, 128), row),
                   pl.BlockSpec((TB // CH, states, width), lambda i: (i, 0, 0))),
        scratch_shapes=[pltpu.VMEM((TB + 8, width), F32),
                        pltpu.VMEM((states, width), F32), pltpu.VMEM((128, TB), F32),
                        pltpu.VMEM((TB + 8, 128), jnp.int32), pltpu.VMEM((CH, 2 * states, 128), F32),
                        pltpu.VMEM((width // LB, CH + 8, LB), F32), pltpu.VMEM((width // LB, CH + 8, LB), F32),
                        pltpu.VMEM((TB, width), F32)],
        compiler_params=pltpu.CompilerParams(vmem_limit_bytes=60 << 20),
        name="mid_fwd",
    )(both, segment, vec, wx, wdt, rates)


def mid_bwd_kernel(rank, both_ref, dg_ref, conv_ref, bend_ref, step_ref, rise_ref, gate_ref, slope_ref, proj_ref, hs_ref, segment_ref, vec_ref, wxt_ref,
                   wdt_ref, rates_ref,
                   dboth_ref, gvec_ref, gwx_ref, gwdt_ref, gr_ref,
                   ext_ref, g_ref, dec_ref, p_ref, part_ref, dproj_ref, dconv_ref, dpdt_ref, turned_ref,
                   acc_ref, seg_ref, spread_ref, decay_ref, source_ref, dy_ref):
    states, width = rates_ref.shape
    steps = TB // CH

    @pl.when(pl.program_id(0) == 0)
    def _():
        ext_ref[TB:, :] = jnp.zeros((8, width), F32)
        seg_ref[TB:, :] = jnp.full((8, 128), -2, jnp.int32)
        g_ref[...] = jnp.zeros_like(g_ref)
        acc_ref[...] = jnp.zeros_like(acc_ref)
        gwx_ref[...] = jnp.zeros_like(gwx_ref)
        gwdt_ref[...] = jnp.zeros_like(gwdt_ref)
        gr_ref[...] = jnp.zeros_like(gr_ref)

    @pl.when(pl.program_id(0) > 0)
    def _():
        ext_ref[TB:, :] = ext_ref[:8, :]
        seg_ref[TB:, :] = seg_ref[:8, :]

    turned_ref[...] = proj_ref[...].T
    seg_ref[:TB, :] = segment_ref[...]
    ones = jnp.ones((128, 128), BF16)
    lane = lax.broadcasted_iota(jnp.int32, (2 * states, 128), 1)
    place = lax.broadcasted_iota(jnp.int32, (2 * states, 128), 0) + rank

    def fold(x):
        out = x[:, :128]
        for i in range(1, LB // 128):
            out = out + x[:, i * 128:(i + 1) * 128]
        return out

    def halves(x):
        out = x[:8]
        for i in range(1, CH // 8):
            out = out + x[i * 8:(i + 1) * 8]
        return out

    def every(ref, k):
        row = ref[pl.ds(k, 8, stride=0), :]
        return jnp.concatenate([row] * (states // 8), axis=0)

    def wide(k, side):
        return jnp.concatenate([spread_ref[k, side * states:(side + 1) * states, :]] * (LB // 128), axis=1)

    def scan_chunk(i, _):
        c = steps - 1 - i
        rows = pl.ds(pl.multiple_of(c * CH, CH), CH)
        tile = pltpu.roll(turned_ref[rank:rank + 2 * states, :], TB - c * CH, 1)
        keep = proj_ref[rows, 127:]
        for k in range(CH):
            spread_ref[k] = jnp.broadcast_to(tile[:, k:k + 1], (2 * states, 128))
        for b in range(width // LB):
            lanes = slice(b * LB, (b + 1) * LB)
            rates = rates_ref[:, lanes]
            h = hs_ref[c, :, lanes]
            conv = conv_ref[rows, lanes]
            step = step_ref[rows, lanes]
            source_ref[b, :CH] = step * conv
            decay_ref[b, :CH] = jnp.where(keep > 0.0, step, 1e4)
            skip = vec_ref[6:7, lanes]
            dg = dg_ref[rows, lanes]
            dboth_ref[rows, width + b * LB:width + (b + 1) * LB] = (dg * slope_ref[rows, lanes]).astype(BF16)
            dy = dg * gate_ref[rows, lanes]
            dy_ref[b, :CH] = dy
            for k in range(CH):
                dec = jnp.exp2(every(decay_ref.at[b], k) * rates)
                p = dec * h
                dec_ref[k] = dec
                p_ref[k] = p
                h = p + wide(k, 0) * every(source_ref.at[b], k)
                out = fold(every(dy_ref.at[b], k) * h)
                part_ref[k, states:, :] = out if b == 0 else part_ref[k, states:, :] + out
            g = g_ref[:, lanes]
            dr = gr_ref[:, lanes]
            dus, dss = [None] * CH, [None] * CH
            for k in reversed(range(CH)):
                dh = g + wide(k, 1) * every(dy_ref.at[b], k)
                out = fold(dh * every(source_ref.at[b], k))
                part_ref[k, :states, :] = out if b == 0 else part_ref[k, :states, :] + out
                dus[k] = halves(dh * wide(k, 0))
                da = dh * p_ref[k]
                dss[k] = halves(da * rates)
                dr = dr + da * every(decay_ref.at[b], k)
                g = dec_ref[k] * dh
            g_ref[:, lanes] = g
            gr_ref[:, lanes] = dr
            du = jnp.concatenate([row_sums(dus[:8]), row_sums(dus[8:])], axis=0)
            dpdt = (jnp.concatenate([row_sums(dss[:8]), row_sums(dss[8:])], axis=0) * LN2 + du * conv) * rise_ref[rows, lanes]
            dpdt_ref[rows, lanes] = dpdt
            dconv_ref[rows, lanes] = dy * skip + du * step
            acc_ref[5, :, lanes] += halves(dpdt)
            acc_ref[6, :, lanes] += halves(dy * conv)
        high, rest = split(part_ref[...].reshape(CH * 2 * states, 128))
        sums = (mxu(high, ones, NN) + mxu(rest, ones, NN)).reshape(CH, 2 * states, 128)
        picked = jnp.where((lane == place)[None], sums, 0.0)
        dproj_ref[rows, :] = jnp.sum(picked, axis=1)
        return 0

    lax.fori_loop(0, steps, scan_chunk, 0)
    dpdt = dpdt_ref[...]
    dproj = dproj_ref[...] + dot2(dpdt, wdt_ref[...], NT)
    gwdt_ref[...] += dot3(turned_ref[...], dpdt, NN)
    gwx_ref[...] += dot3(dproj.T, conv_ref[...], NN)
    dconv_ref[...] += dot2(dproj, wxt_ref[...], NN)

    def act_chunk(c, _):
        rows = pl.ds(pl.multiple_of(c * CH, CH), CH)
        ext_ref[rows, :] = dconv_ref[rows, :] * bend_ref[rows, :]
        return 0

    lax.fori_loop(0, steps, act_chunk, 0)

    def conv_chunk(c):
        at = c * CH
        rows = slice(at, at + CH)
        masks = [(seg_ref[at + k:at + k + CH, :] == seg_ref[rows, :]).astype(F32)[:, :1] for k in range(1, 4)]
        for b in range(width // LB):
            lanes = slice(b * LB, (b + 1) * LB)
            inner = both_ref[rows, lanes]
            here = ext_ref[rows, lanes]
            total = vec_ref[3:4, lanes] * here
            acc_ref[4, :, lanes] += halves(here)
            acc_ref[3, :, lanes] += halves(here * inner)
            for k in range(1, 4):
                later = ext_ref[at + k:at + k + CH, lanes] * masks[k - 1]
                total = total + vec_ref[3 - k:4 - k, lanes] * later
                acc_ref[3 - k, :, lanes] += halves(later * inner)
            dboth_ref[rows, lanes] = total.astype(BF16)

    for c in range(steps):
        conv_chunk(c)

    @pl.when(pl.program_id(0) == pl.num_programs(0) - 1)
    def _():
        gvec_ref[...] = jnp.concatenate(
            [jnp.sum(acc_ref[k], axis=0, keepdims=True) for k in range(8)], axis=0)


def mid_bwd(both, dg, saved, proj, hs, segment, vec, wxt, wdt, rates, rank):
    length = both.shape[0]
    states, width = rates.shape
    blocks = length // TB
    row = lambda i: (blocks - 1 - i, 0)
    fix = lambda i: (0, 0)
    tall = pl.BlockSpec((TB, width), row)
    return pl.pallas_call(
        functools.partial(mid_bwd_kernel, rank),
        grid=(blocks,),
        out_shape=(jax.ShapeDtypeStruct((length, 2 * width), BF16), jax.ShapeDtypeStruct((8, width), F32),
                   jax.ShapeDtypeStruct((128, width), F32), jax.ShapeDtypeStruct((128, width), F32),
                   jax.ShapeDtypeStruct((states, width), F32)),
        in_specs=[tall, tall] + [tall] * 6 + [pl.BlockSpec((TB, 128), row),
                  pl.BlockSpec((TB // CH, states, width), lambda i: (blocks - 1 - i, 0, 0)),
                  pl.BlockSpec((TB, 128), row), pl.BlockSpec(vec.shape, fix), pl.BlockSpec(wxt.shape, fix),
                  pl.BlockSpec(wdt.shape, fix), pl.BlockSpec(rates.shape, fix)],
        out_specs=(pl.BlockSpec((TB, 2 * width), row), pl.BlockSpec((8, width), fix),
                   pl.BlockSpec((128, width), fix), pl.BlockSpec((128, width), fix), pl.BlockSpec((states, width), fix)),
        scratch_shapes=[pltpu.VMEM((TB + 8, width), F32), pltpu.VMEM((states, width), F32),
                        pltpu.VMEM((CH, states, LB), F32), pltpu.VMEM((CH, states, LB), F32),
                        pltpu.VMEM((CH, 2 * states, 128), F32), pltpu.VMEM((TB, 128), F32),
                        pltpu.VMEM((TB, width), F32), pltpu.VMEM((TB, width), F32),
                        pltpu.VMEM((128, TB), F32), pltpu.VMEM((8, 8, width), F32),
                        pltpu.VMEM((TB + 8, 128), jnp.int32), pltpu.VMEM((CH, 2 * states, 128), F32),
                        pltpu.VMEM((width // LB, CH + 8, LB), F32), pltpu.VMEM((width // LB, CH + 8, LB), F32), pltpu.VMEM((width // LB, CH + 8, LB), F32)],
        compiler_params=pltpu.CompilerParams(vmem_limit_bytes=60 << 20),
        name="mid_bwd",
    )(both, dg, *saved, proj, hs, segment, vec, wxt, wdt, rates)


CHUNK = (256, 1024)


def bit_orders(groups, members):
    ep_bits, tp_bits = groups.bit_length() - 1, members.bit_length() - 1
    x = [("ep", b) for b in range(ep_bits - 2)]
    z = [("ep", b) for b in range(ep_bits - 2, ep_bits)]
    y = [("tp", b) for b in range(1, tp_bits)]
    core = [("tp", 0)]
    return [core + x + y + z, core + y + x + z, core + x + z + y, core + y + z + x]


def region_sizes(stages, rows, cols):
    sizes = []
    for _ in range(stages):
        if rows > 16:
            rows //= 2
            sizes.append((rows, cols, True))
        else:
            cols //= 2
            sizes.append((rows, cols, False))
    return sizes


def sum_scratch(chunks, stages):
    return [pltpu.VMEM((chunks, r, c), BF16) for r, c, _ in region_sizes(stages, *CHUNK)] + [
        pltpu.VMEM((chunks,) + CHUNK, BF16),
        pltpu.VMEM((chunks,) + CHUNK, BF16),
        pltpu.SemaphoreType.DMA((2 * stages, chunks)),
        pltpu.SemaphoreType.DMA((2 * stages, chunks)),
        pltpu.SemaphoreType.DMA((chunks,)),
    ]


def sum_steps(orders, g_ref, out_ref, scratch):
    stages = len(orders[0])
    land = scratch[:stages]
    work_ref, full_ref, send_sem, recv_sem, done_sem = scratch[stages:]
    sizes = region_sizes(stages, *CHUNK)
    me = {"ep": lax.axis_index("ep"), "tp": lax.axis_index("tp")}

    def bit(stage):
        axis, b = stage
        return lax.rem(me[axis] // (1 << b), 2)

    def partner(stage):
        axis, b = stage
        there = dict(me)
        there[axis] = me[axis] + (1 << b) - 2 * (1 << b) * bit(stage)
        return (there["ep"], there["tp"])

    def greet():
        barrier = pltpu.get_barrier_semaphore()
        for stage in orders[0]:
            pl.semaphore_signal(barrier, inc=1, device_id=partner(stage), device_id_type=MESH)
        pl.semaphore_wait(barrier, stages)

    def part(c, order, upto, flip):
        r0, c0 = 0, 0
        for s in range(upto + 1):
            b = bit(order[s])
            if s == upto and flip:
                b = 1 - b
            if sizes[s][2]:
                r0 = r0 + b * sizes[s][0]
            else:
                c0 = c0 + b * sizes[s][1]
        return (c, pl.ds(pl.multiple_of(r0, 16), sizes[upto][0]),
                pl.ds(c0 if isinstance(c0, int) else pl.multiple_of(c0, 128), sizes[upto][1]))

    def scatter(s, v, c):
        order = orders[v]
        return pltpu.make_async_remote_copy(
            src_ref=(g_ref if s == 0 else work_ref).at[part(c, order, s, True)], dst_ref=land[s].at[c],
            send_sem=send_sem.at[s, c], recv_sem=recv_sem.at[s, c], device_id=partner(order[s]), device_id_type=MESH)

    def gather(s, v, c, flip=False):
        order = orders[v]
        piece = full_ref.at[part(c, order, s, flip)]
        return pltpu.make_async_remote_copy(
            src_ref=piece, dst_ref=piece, send_sem=send_sem.at[stages + s, c], recv_sem=recv_sem.at[stages + s, c],
            device_id=partner(order[s]), device_id_type=MESH)

    def done(c):
        return pltpu.make_async_copy(full_ref.at[c], out_ref.at[c], done_sem.at[c])

    def step(n, v, c):
        if n == 0:
            scatter(0, v, c).start()
        elif n <= stages:
            s = n - 1
            scatter(s, v, c).wait_recv()
            where = part(c, orders[v], s, False)
            total = ((g_ref if s == 0 else work_ref)[where].astype(F32) + land[s][c].astype(F32)).astype(BF16)
            if s + 1 < stages:
                work_ref[where] = total
                scatter(s + 1, v, c).start()
            else:
                full_ref[where] = total
                gather(s, v, c).start()
        else:
            s = 2 * stages - n
            gather(s, v, c, True).wait_recv()
            if s > 0:
                gather(s - 1, v, c).start()
            else:
                done(c).start()

    def settle(v, c):
        for s in range(stages):
            scatter(s, v, c).wait_send()
            gather(s, v, c).wait_send()
        done(c).wait()

    return greet, step, settle, 2 * stages + 1


def tail_kernel(orders, tall, across, used, rank, normed_ref, d_both_ref, vec_ref, g_two_ref, gx_ref, gdt_ref, gr_ref,
                rates_ref, gvec_ref, router_ref, w_in_hbm, gated_hbm, d_mixed_hbm, tokens_hbm, d_after_hbm,
                out_ref, d_tokens_ref, g_ref, gains_ref, w_in_ref, gated_ref, d_mixed_ref, tokens_ref, d_after_ref, load_sem,
                *scratch):
    greet, step, settle, steps = sum_steps(orders, g_ref, out_ref, scratch)
    kinds, chunks = len(orders), g_ref.shape[0]
    rows, cols = CHUNK
    width = d_mixed_ref.shape[1]
    loads = [pltpu.make_async_copy(src, dst, load_sem.at[n]) for n, (src, dst) in enumerate(
        ((w_in_hbm, w_in_ref), (tokens_hbm, tokens_ref), (d_after_hbm, d_after_ref), (gated_hbm, gated_ref),
         (d_mixed_hbm, d_mixed_ref)))]
    for load in loads:
        load.start()
    greet()

    def produce(c):
        @pl.when(c < tall)
        def _():
            left = pl.multiple_of(c // across * rows, rows)
            right = pl.multiple_of(lax.rem(c, across) * cols, cols)
            g_ref[c] = mxu(normed_ref[:, pl.ds(left, rows)], d_both_ref[:, pl.ds(right, cols)], TN).astype(BF16)

        @pl.when(c >= tall)
        def _():
            at = pl.ds(pl.multiple_of((c - tall) * rows, rows), rows)
            g_ref[c, :, :width] = mxu(gated_ref[:, at], d_mixed_ref[...], TN).astype(BF16)
            pieces = [gx_ref[:used, at], gdt_ref[:rank, at], gr_ref[:, at] * rates_ref[:, at] * LN2, gvec_ref[:, at],
                      gains_ref[:, at]]
            high = sum(p.shape[0] for p in pieces) + router_ref.shape[0]
            pieces += [jnp.zeros((256 - high, rows), F32), router_ref[:, at]]
            g_ref[c, :, width:] = jnp.concatenate(pieces, axis=0).T.astype(BF16)

    def input_grads():
        for load in loads[:3]:
            load.wait()
        values = tokens_ref[...].astype(F32)
        scale = lax.rsqrt(jnp.mean(values * values, axis=-1, keepdims=True) + EPS)
        plain = values * scale
        d_normed = mxu(d_both_ref[...], w_in_ref[...], NT)
        gains_ref[:, :width] = jnp.broadcast_to(jnp.sum(d_normed * plain, axis=0, keepdims=True), (8, width))
        gains_ref[:, width:] = g_two_ref[...]
        d_plain = d_normed * vec_ref[7:8, :width]
        d_tokens_ref[...] = d_after_ref[...] + scale * (d_plain - plain * jnp.mean(d_plain * plain, axis=-1, keepdims=True))
        for load in loads[3:]:
            load.wait()

    waves = -(-chunks // kinds)
    ready = tall // kinds

    def slot(i, _):
        for n in reversed(range(1, steps)):
            group = i - n
            for v in range(kinds):
                c = group * kinds + v

                @pl.when((group >= 0) & (c < chunks))
                def _(n=n, v=v, c=c):
                    step(n, v, c)

        @pl.when(i == ready)
        def _():
            input_grads()

        def begin(v, _):
            c = i * kinds + v

            @pl.when(c < chunks)
            def _():
                produce(c)
                step(0, 0, c)
            return 0

        lax.fori_loop(0, kinds, begin, 0)
        return 0

    lax.fori_loop(0, waves + steps - 1, slot, 0)

    def drain(group, _):
        for v in range(kinds):
            c = group * kinds + v

            @pl.when(c < chunks)
            def _(v=v, c=c):
                settle(v, c)
        return 0

    lax.fori_loop(0, waves, drain, 0)


SUM_ORDERS = (0, 1, 2, 3)


def tail_sum(normed, d_both, w_in, gated, d_mixed, tokens, d_after, vec, g_two, gx, gdt, gr, rates, gvec, router, used, rank,
             groups, members):
    length, width = normed.shape
    rows, cols = CHUNK
    across = d_both.shape[1] // cols
    tall = width // rows * across
    chunks = tall + gated.shape[1] // rows
    orders = [bit_orders(groups, members)[v] for v in SUM_ORDERS]
    vmem, anywhere = pl.BlockSpec(memory_space=pltpu.VMEM), pl.BlockSpec(memory_space=pl.ANY)
    held = lambda a: pltpu.VMEM(a.shape, a.dtype)
    return pl.pallas_call(
        functools.partial(tail_kernel, orders, tall, across, used, rank),
        out_shape=(jax.ShapeDtypeStruct((chunks,) + CHUNK, BF16), jax.ShapeDtypeStruct((length, width), F32)),
        in_specs=[vmem] * 10 + [anywhere] * 5,
        out_specs=(anywhere, vmem),
        scratch_shapes=[pltpu.VMEM((chunks,) + CHUNK, BF16), pltpu.VMEM((8, 2 * width), F32), held(w_in), held(gated),
                        held(d_mixed), held(tokens), held(d_after), pltpu.SemaphoreType.DMA((5,))]
        + sum_scratch(chunks, len(orders[0])),
        compiler_params=pltpu.CompilerParams(collective_id=0, has_side_effects=True, vmem_limit_bytes=60 << 20),
        name="tail_sum",
    )(normed, d_both, vec, g_two, gx, gdt, gr, rates, gvec, router, w_in, gated, d_mixed, tokens, d_after)


CARRIED = 3


def unpack_kernel(tall_ref, wide_ref, *refs):
    sources, refs = refs[:CARRIED], refs[CARRIED:]
    in_ref, out_ref, x_ref, router_ref, *row_refs = refs[:-CARRIED]
    in_ref[...] = tall_ref[0].astype(F32)

    @pl.when(pl.program_id(0) < 8)
    def _():
        for source, target in zip(sources, refs[-CARRIED:]):
            target[...] = source[...]

    width = out_ref.shape[1]

    @pl.when(pl.program_id(0) < pl.num_programs(0) * 2 // 3)
    def _():
        out_ref[...] = wide_ref[0, :, :width].astype(F32)
        small = wide_ref[0, :, width:].astype(F32)
        turned = small.T
        at = x_ref.shape[0]
        x_ref[...] = turned[:at]
        router_ref[...] = turned[256 - router_ref.shape[0] :]
        for ref in row_refs[:3]:
            ref[...] = turned[at : at + ref.shape[0]]
            at += ref.shape[0]
        for ref in row_refs[3:6]:
            ref[...] = turned[at]
            at += 1
        c, half = pl.program_id(0), width // CHUNK[0]

        @pl.when(c < half)
        def _():
            row_refs[6][...] = turned[at + 1]

        @pl.when(c >= half)
        def _():
            row_refs[7][...] = turned[at + 1]


def unpack_grads(total, carried, width, inner, used, experts, heights):
    rows, cols = CHUNK
    across = 2 * inner // cols
    tall, wide = width // rows * across, inner // rows
    hold = lambda c: jnp.minimum(c, wide - 1)
    half = width // rows
    eighth = [pl.BlockSpec((a.shape[0] // 8, a.shape[1]), lambda c: (jnp.minimum(c, 7), 0)) for a in carried]
    return pl.pallas_call(
        unpack_kernel,
        grid=(tall,),
        out_shape=(jax.ShapeDtypeStruct((width, 2 * inner), F32), jax.ShapeDtypeStruct((inner, width), F32),
                   jax.ShapeDtypeStruct((used, inner), F32), jax.ShapeDtypeStruct((experts, inner), F32))
        + tuple(jax.ShapeDtypeStruct((h, inner), F32) for h in heights)
        + tuple(jax.ShapeDtypeStruct((w,), F32) for w in (inner, inner, inner, width, width))
        + tuple(jax.ShapeDtypeStruct(a.shape, a.dtype) for a in carried),
        in_specs=[pl.BlockSpec((1,) + CHUNK, lambda c: (c, 0, 0)),
                  pl.BlockSpec((1,) + CHUNK, lambda c: (tall + hold(c), 0, 0))] + eighth,
        out_specs=(pl.BlockSpec(CHUNK, lambda c: (c // across, lax.rem(c, across))),
                   pl.BlockSpec((rows, width), lambda c: (hold(c), 0)),
                   pl.BlockSpec((used, rows), lambda c: (0, hold(c))),
                   pl.BlockSpec((experts, rows), lambda c: (0, hold(c))))
        + tuple(pl.BlockSpec((h, rows), lambda c: (0, hold(c))) for h in heights)
        + (pl.BlockSpec((rows,), lambda c: (hold(c),)),) * 3
        + (pl.BlockSpec((rows,), lambda c: (jnp.minimum(c, half - 1),)), pl.BlockSpec((rows,), lambda c: (jnp.maximum(hold(c) - half, 0),)))
        + tuple(eighth),
        compiler_params=pltpu.CompilerParams(vmem_limit_bytes=60 << 20),
        name="unpack_grads",
    )(total, total, *carried)


def front_kernel(rank, used, tokens_ref, taps_ref, bias_ref, step_ref, skip_ref, gain_one_ref, gain_two_ref, segment_ref,
                 route_ref, w_in_ref, wx_ref, wdt_ref, log_ref,
                 normed_ref, both_ref, wx_out, wxt_out, wdt_out, rates_out, vec_ref, segment_out, route_out):
    @pl.when(pl.program_id(0) == 0)
    def _():
        values = tokens_ref[...].astype(F32)
        width = values.shape[1]
        vec_ref[:4, :] = taps_ref[...].astype(F32)
        for n, ref in ((4, bias_ref), (5, step_ref), (6, skip_ref)):
            vec_ref[n:n + 1, :] = ref[...].astype(F32).reshape(1, -1)
        vec_ref[7:8, :width] = gain_one_ref[...].astype(F32).reshape(1, -1)
        vec_ref[7:8, width:] = gain_two_ref[...].astype(F32).reshape(1, -1)
        for source, target in ((segment_ref, segment_out), (route_ref, route_out)):
            for n in range(source.shape[0]):
                row = source[n:n + 1, :].astype(F32)
                target[n * 128:(n + 1) * 128, :] = jnp.broadcast_to(row, (128, 128)).T.astype(jnp.int32)
        scale = lax.rsqrt(jnp.mean(values * values, axis=-1, keepdims=True) + EPS)
        normed_ref[...] = (values * scale * vec_ref[7:8, :width]).astype(BF16)
        wxt_out[...] = jnp.zeros_like(wxt_out)
        wxt_out[:used, :] = wx_ref[...]
        wx_out[...] = wxt_out[...].astype(F32).T.astype(BF16)
        wdt_out[...] = jnp.zeros_like(wdt_out)
        wdt_out[:rank, :] = wdt_ref[...]
        rates_out[...] = -jnp.exp(log_ref[...].astype(F32)) * LOG2E

    both_ref[...] = mxu(normed_ref[...], w_in_ref[...], NN)


def front(tokens, rows, w_in, w_x, w_dt, a_log):
    length, width = tokens.shape
    used, inner = w_x.shape
    rank, states = w_dt.shape[0], a_log.shape[0]
    cols = inner // 2
    fix = lambda a: pl.BlockSpec(a, lambda j: (0,) * len(a))
    return pl.pallas_call(
        functools.partial(front_kernel, rank, used),
        grid=(w_in.shape[1] // cols,),
        out_shape=(jax.ShapeDtypeStruct((length, width), BF16), jax.ShapeDtypeStruct((length, w_in.shape[1]), F32),
                   jax.ShapeDtypeStruct((inner, 128), BF16), jax.ShapeDtypeStruct((128, inner), BF16),
                   jax.ShapeDtypeStruct((128, inner), BF16), jax.ShapeDtypeStruct((states, inner), F32),
                   jax.ShapeDtypeStruct((8, inner), F32), jax.ShapeDtypeStruct((length, 128), jnp.int32),
                   jax.ShapeDtypeStruct((length, 128), jnp.int32)),
        in_specs=[fix(tokens.shape)] + [fix(a.shape) for a in rows] + [ pl.BlockSpec((width, cols), lambda j: (0, j)), fix(w_x.shape),
                  fix(w_dt.shape), fix(a_log.shape)],
        out_specs=(fix((length, width)), pl.BlockSpec((length, cols), lambda j: (0, j)), fix((inner, 128)),
                   fix((128, inner)), fix((128, inner)), fix((states, inner)), fix((8, inner)), fix((length, 128)),
                   fix((length, 128))),
        compiler_params=pltpu.CompilerParams(vmem_limit_bytes=60 << 20),
        name="front",
    )(tokens, *rows, w_in, w_x, w_dt, a_log)


def choose(experts, segment, route):
    lane = lax.broadcasted_iota(jnp.int32, (segment.shape[0], 128), 1)
    return (lane == route) & (segment >= 0)


def route_kernel(slots, gated_ref, w_out_ref, tokens_ref, d_out_ref, segment_ref, route_ref, gain_ref, w_router_ref,
                 after_ref, leaving_ref, count_ref, aux_ref):
    length, width = tokens_ref.shape
    experts = w_router_ref.shape[0]
    segment, route = segment_ref[:, :1], route_ref[:, :1]
    picked = choose(experts, segment, route)
    picks = picked.astype(F32)
    row = lax.broadcasted_iota(jnp.int32, (length, length), 0)
    col = lax.broadcasted_iota(jnp.int32, (length, length), 1)
    upto = mxu((col <= row).astype(BF16), picks.astype(BF16), NN)
    rank = jnp.sum(picks * upto, axis=1, keepdims=True) - 1.0
    slot = jnp.where(segment >= 0, route * slots + rank.astype(jnp.int32), -1)
    count_ref[...] = jnp.broadcast_to(jnp.sum(picks, axis=0, keepdims=True).astype(jnp.int32), count_ref.shape)

    mixed = mxu(gated_ref[...], w_out_ref[...], NN)
    after = tokens_ref[...].astype(F32) + jnp.where(segment >= 0, mixed, 0.0)
    after_ref[...] = after
    normed = after * lax.rsqrt(jnp.mean(after * after, axis=-1, keepdims=True) + EPS) * gain_ref[7:8, width:]
    logits = dot2(normed, w_router_ref[...], NT)
    logits = logits - jnp.max(logits, axis=-1, keepdims=True)
    weights = jnp.exp(logits)
    probs = weights / jnp.sum(weights, axis=-1, keepdims=True)
    aux_ref[...] = jnp.zeros_like(aux_ref)
    aux_ref[:, :experts] = probs
    gate = jnp.sum(aux_ref[...] * picks, axis=1, keepdims=True)
    lane = lax.broadcasted_iota(jnp.int32, (length, 128), 1)
    extra = jnp.where(lane == 125, rank, jnp.where(lane == 126, slot.astype(F32), jnp.where(lane == 127, gate, 0.0)))
    aux_ref[...] += extra
    places = (lax.broadcasted_iota(jnp.int32, (length, experts * slots), 1) == slot).astype(BF16)
    leaving_ref[0] = mxu(places, normed.astype(BF16), TN).astype(BF16)
    leaving_ref[1] = mxu(places, (gate * d_out_ref[...].astype(F32)).astype(BF16), TN).astype(BF16)


def route_out(gated, w_out, tokens, d_out, segment, route, gain, w_router, slots):
    length, width = tokens.shape
    experts = w_router.shape[0]
    return pl.pallas_call(
        functools.partial(route_kernel, slots),
        out_shape=(jax.ShapeDtypeStruct((length, width), F32), jax.ShapeDtypeStruct((2, experts * slots, width), BF16),
                   jax.ShapeDtypeStruct((8, 128), jnp.int32), jax.ShapeDtypeStruct((length, 128), F32)),
        compiler_params=pltpu.CompilerParams(vmem_limit_bytes=60 << 20),
        name="route_out",
    )(gated, w_out, tokens, d_out, segment, route, gain, w_router)


def home_kernel(slots, capacity, back_ref, after_ref, d_out_ref, aux_ref, segment_ref, route_ref, here_ref, gain_ref,
                w_router_ref, w_out_ref, final_ref, d_after_ref, d_mixed_ref, d_gated_ref, g_gain_ref, g_router_ref,
                counts_ref):
    length, width = after_ref.shape
    experts = w_router_ref.shape[0]
    segment, route, aux = segment_ref[:, :1], route_ref[:, :1], aux_ref[...]
    picks = choose(experts, segment, route).astype(F32)
    lane = lax.broadcasted_iota(jnp.int32, (length, 128), 1)
    rank, slot, gate = (jnp.sum(jnp.where(lane == n, aux, 0.0), axis=1, keepdims=True) for n in (125, 126, 127))
    prior = jnp.sum(picks * here_ref[0:1, :], axis=1, keepdims=True)
    keep = jnp.where((segment >= 0) & (prior + rank < capacity), 1.0, 0.0)
    named = here_ref[1:2, :].astype(jnp.int32)
    counts_ref[0:1, :] = named[:, :experts]
    counts_ref[1:2, :] = jnp.maximum(named - capacity, 0)[:, :experts]

    places = (lax.broadcasted_iota(jnp.int32, (length, experts * slots), 1) == slot.astype(jnp.int32)).astype(BF16)
    token_out = mxu(places, back_ref[0], NN)
    upstream = d_out_ref[...].astype(F32)
    after = after_ref[...]
    final_ref[...] = (after + gate * keep * token_out).astype(BF16)
    d_gate = keep * jnp.sum(upstream * token_out, axis=1, keepdims=True)
    probs = jnp.where(lane < experts, aux, 0.0)
    d_logits = (gate * d_gate * (picks - probs))[:, :experts]
    scale = lax.rsqrt(jnp.mean(after * after, axis=-1, keepdims=True) + EPS)
    plain = after * scale
    gain = gain_ref[7:8, width:]
    g_router_ref[...] = jnp.zeros_like(g_router_ref)
    g_router_ref[:, :width] = dot3(d_logits, plain * gain, TN)
    d_normed = mxu(places, back_ref[1], NN) + dot2(d_logits, w_router_ref[...], NN)
    g_gain_ref[...] = jnp.broadcast_to(jnp.sum(d_normed * plain, axis=0, keepdims=True), g_gain_ref.shape)
    d_plain = d_normed * gain
    d_after = upstream + scale * (d_plain - plain * jnp.mean(d_plain * plain, axis=-1, keepdims=True))
    d_after_ref[...] = d_after
    d_mixed = jnp.where(segment >= 0, d_after, 0.0).astype(BF16)
    d_mixed_ref[...] = d_mixed
    d_gated_ref[...] = mxu(d_mixed, w_out_ref[...], NT)


def come_home(back, after, d_out, aux, segment, route, here, gain, w_router, w_out, slots, capacity):
    length, width = after.shape
    inner, experts = w_out.shape[0], w_router.shape[0]
    return pl.pallas_call(
        functools.partial(home_kernel, slots, capacity),
        out_shape=(jax.ShapeDtypeStruct((length, width), BF16), jax.ShapeDtypeStruct((length, width), F32),
                   jax.ShapeDtypeStruct((length, width), BF16), jax.ShapeDtypeStruct((length, inner), F32),
                   jax.ShapeDtypeStruct((8, width), F32), jax.ShapeDtypeStruct((experts, inner), F32),
                   jax.ShapeDtypeStruct((2, experts), jnp.int32)),
        compiler_params=pltpu.CompilerParams(vmem_limit_bytes=60 << 20),
        name="come_home",
    )(back, after, d_out, aux, segment, route, here, gain, w_router, w_out)


def entry_barrier(groups, chips):
    e, t = lax.axis_index("ep"), lax.axis_index("tp")
    y, c = t // 2, lax.rem(t, 2)
    barrier = pltpu.get_barrier_semaphore()
    for k in range(1, groups):
        pl.semaphore_signal(barrier, inc=1, device_id=(lax.rem(e + k, groups), t), device_id_type=MESH)
    for k in range(1, chips):
        pl.semaphore_signal(barrier, inc=1, device_id=(e, lax.rem(y + k, chips) * 2 + c), device_id_type=MESH)
    pl.semaphore_signal(barrier, inc=1, device_id=(e, t + 1 - 2 * c), device_id_type=MESH)
    pl.semaphore_wait(barrier, groups + chips - 1)
    return e, t, y, c


def dispatch_kernel(groups, chips, rows_ref, count_ref, out_ref, table_ref,
                    own_sem, far_send, far_recv, row_send, row_recv, pair_send, pair_recv):
    e, t, y, c = entry_barrier(groups, chips)
    held = rows_ref.shape[1] // groups
    sibling = (e, t + 1 - 2 * c)

    def block(kind, ref, i, member):
        return ref.at[:, :, member, i] if kind == 0 else ref.at[member, i]

    kinds = ((0, rows_ref, out_ref), (1, count_ref, table_ref))

    def mine(kind, src, peer):
        return src.at[:, pl.ds(peer * held, held)] if kind == 0 else src

    def far(kind, src, dst, peer, source):
        return pltpu.make_async_remote_copy(
            src_ref=mine(kind, src, peer), dst_ref=block(kind, dst, source, t), send_sem=far_send.at[kind, peer],
            recv_sem=far_recv.at[kind, source], device_id=(peer, t), device_id_type=MESH)

    def across(kind, dst, i, to, source):
        there = block(kind, dst, i, source * 2 + c)
        return pltpu.make_async_remote_copy(
            src_ref=there, dst_ref=there, send_sem=row_send.at[kind, i, to], recv_sem=row_recv.at[kind, i, source],
            device_id=(e, to * 2 + c), device_id_type=MESH)

    def beside(kind, dst, i, source, core):
        there = block(kind, dst, i, source * 2 + core)
        return pltpu.make_async_remote_copy(
            src_ref=there, dst_ref=there, send_sem=pair_send.at[kind, i, source],
            recv_sem=pair_recv.at[kind, i, source], device_id=sibling, device_id_type=MESH)

    for kind, src, dst in kinds:
        pltpu.make_async_copy(mine(kind, src, e), block(kind, dst, e, t), own_sem.at[kind]).start()

    def send(k, _):
        peer = lax.rem(e + k, groups)
        for kind, src, dst in kinds:
            far(kind, src, dst, peer, e).start()
        return 0

    lax.fori_loop(1, groups, send, 0)
    for kind, src, dst in kinds:
        pltpu.make_async_copy(mine(kind, src, e), block(kind, dst, e, t), own_sem.at[kind]).wait()

    def pass_on(i):
        for kind, src, dst in kinds:
            for k in range(1, chips):
                across(kind, dst, i, lax.rem(y + k, chips), y).start()
            beside(kind, dst, i, y, c).start()

    def hand_over(i):
        for kind, src, dst in kinds:
            for k in range(1, chips):
                source = lax.rem(y + k, chips)
                across(kind, dst, i, source, source).wait_recv()
                beside(kind, dst, i, source, c).start()

    pass_on(e)

    def middle(k, _):
        i = lax.rem(e + groups - k, groups)
        for kind, src, dst in kinds:
            far(kind, src, dst, i, i).wait_recv()
        pass_on(i)
        hand_over(lax.rem(i + 1, groups))
        return 0

    lax.fori_loop(1, groups, middle, 0)
    hand_over(lax.rem(e + 1, groups))

    def finish(k, _):
        i = lax.rem(e + groups - k, groups)
        for kind, src, dst in kinds:
            for source in range(chips):
                beside(kind, dst, i, source, 1 - c).wait_recv()
                beside(kind, dst, i, source, c).wait_send()
            for j in range(1, chips):
                across(kind, dst, i, lax.rem(y + j, chips), y).wait_send()
        return 0

    lax.fori_loop(0, groups, finish, 0)

    def drain(k, _):
        peer = lax.rem(e + k, groups)
        for kind, src, dst in kinds:
            far(kind, src, dst, peer, e).wait_send()
        return 0

    lax.fori_loop(1, groups, drain, 0)


def dispatch(rows, count, groups, members):
    kinds, experts, slots, width = rows.shape
    chips = members // 2
    any_space = pl.BlockSpec(memory_space=pl.ANY)
    dma = pltpu.SemaphoreType.DMA
    return pl.pallas_call(
        functools.partial(dispatch_kernel, groups, chips),
        out_shape=(jax.ShapeDtypeStruct((kinds, experts // groups, members, groups, slots, width), BF16),
                   jax.ShapeDtypeStruct((members, groups) + count.shape, jnp.int32)),
        in_specs=[any_space, any_space],
        out_specs=(any_space, any_space),
        scratch_shapes=[dma((2,)), dma((2, groups)), dma((2, groups)), dma((2, groups, chips)), dma((2, groups, chips)),
                        dma((2, groups, chips)), dma((2, groups, chips))],
        compiler_params=pltpu.CompilerParams(collective_id=1, has_side_effects=True),
        name="dispatch",
    )(rows, count)


def collect_kernel(groups, chips, part_ref, out_ref, own_ref, pair_ref, row_ref, ready_ref,
                   own_sem, last_sem, pair_send, pair_recv, row_send, row_recv, far_send, far_recv):
    e, t, y, c = entry_barrier(groups, chips)
    kinds, held = part_ref.shape[:2]
    sibling = (e, t + 1 - 2 * c)

    def local(i, to):
        return pltpu.make_async_copy(part_ref.at[:, :, to * 2 + c, i], own_ref.at[to, i], own_sem.at[to, i])

    def beside(i, to):
        return pltpu.make_async_remote_copy(
            src_ref=part_ref.at[:, :, to * 2 + 1 - c, i], dst_ref=pair_ref.at[to, i], send_sem=pair_send.at[to, i],
            recv_sem=pair_recv.at[to, i], device_id=sibling, device_id_type=MESH)

    def across(i, to, source):
        return pltpu.make_async_remote_copy(
            src_ref=own_ref.at[to, i], dst_ref=row_ref.at[source, i], send_sem=row_send.at[to, i],
            recv_sem=row_recv.at[source, i], device_id=(e, to * 2 + c), device_id_type=MESH)

    def far(i, source):
        return pltpu.make_async_remote_copy(
            src_ref=ready_ref.at[i], dst_ref=out_ref.at[:, pl.ds(source * held, held)], send_sem=far_send.at[i],
            recv_sem=far_recv.at[source], device_id=(i, t), device_id_type=MESH)

    def turn(k):
        return lax.rem(e + k, groups)

    def start(k, _):
        i = turn(k)
        for j in range(1, chips + 1):
            to = lax.rem(y + j, chips)
            local(i, to).start()
            beside(i, to).start()
        return 0

    lax.fori_loop(1, groups + 1, start, 0)

    def first(k, _):
        i = turn(k)
        for j in range(1, chips):
            to = lax.rem(y + j, chips)
            local(i, to).wait()
            beside(i, to).wait_recv()
            for a in range(kinds):
                for x in range(held):
                    own_ref[to, i, a, x] = (own_ref[to, i, a, x].astype(F32) + pair_ref[to, i, a, x].astype(F32)).astype(BF16)
            across(i, to, y).start()
        local(i, y).wait()
        beside(i, y).wait_recv()
        return 0

    lax.fori_loop(1, groups + 1, first, 0)

    def total(i):
        for j in range(1, chips):
            source = lax.rem(y + j, chips)
            across(i, source, source).wait_recv()
        for a in range(kinds):
            for x in range(held):
                value = own_ref[y, i, a, x].astype(F32) + pair_ref[y, i, a, x].astype(F32)
                for j in range(1, chips):
                    value = value + row_ref[lax.rem(y + j, chips), i, a, x].astype(F32)
                ready_ref[i, a, x] = value.astype(BF16)

    def second(k, _):
        i = turn(k)
        total(i)
        far(i, e).start()
        return 0

    lax.fori_loop(1, groups, second, 0)
    total(e)
    last = pltpu.make_async_copy(ready_ref.at[e], out_ref.at[:, pl.ds(e * held, held)], last_sem)
    last.start()

    def finish(k, _):
        i = turn(k)
        far(i, e).wait_send()
        far(i, i).wait_recv()
        return 0

    lax.fori_loop(1, groups, finish, 0)

    def drain(k, _):
        i = turn(k)
        for j in range(1, chips + 1):
            beside(i, lax.rem(y + j, chips)).wait_send()
        for j in range(1, chips):
            across(i, lax.rem(y + j, chips), y).wait_send()
        return 0

    lax.fori_loop(1, groups + 1, drain, 0)
    last.wait()


def collect(parts, groups, members):
    kinds, held, _, _, slots, width = parts.shape
    chips = members // 2
    any_space = pl.BlockSpec(memory_space=pl.ANY)
    dma = pltpu.SemaphoreType.DMA
    block = (kinds, held, slots, width)
    return pl.pallas_call(
        functools.partial(collect_kernel, groups, chips),
        out_shape=jax.ShapeDtypeStruct((kinds, held * groups, slots, width), BF16),
        in_specs=[any_space],
        out_specs=any_space,
        scratch_shapes=[pltpu.VMEM((chips, groups) + block, BF16), pltpu.VMEM((chips, groups) + block, BF16),
                        pltpu.VMEM((chips, groups) + block, BF16), pltpu.VMEM((groups,) + block, BF16),
                        dma((chips, groups)), dma(()), dma((chips, groups)), dma((chips, groups)),
                        dma((chips, groups)), dma((chips, groups)), dma((groups,)), dma((groups,))],
        compiler_params=pltpu.CompilerParams(collective_id=2, has_side_effects=True, vmem_limit_bytes=60 << 20),
        name="collect",
    )(parts)


def expert_kernel(rows_ref, mask_ref, up_ref, down_ref, out_ref, gup_ref, gdown_ref):
    @pl.when(pl.program_id(1) == 0)
    def _():
        gup_ref[...] = jnp.zeros_like(gup_ref)
        gdown_ref[...] = jnp.zeros_like(gdown_ref)

    x = rows_ref[0, 0]
    d = (rows_ref[1, 0].astype(F32) * mask_ref[0]).astype(BF16)
    up, down = up_ref[0], down_ref[0]
    pre = mxu(x, up, NN)
    cdf = 0.5 * (1.0 + lax.erf(pre * 0.7071067811865476))
    hidden = (pre * cdf).astype(BF16)
    slope = cdf + pre * (0.3989422804014327 * jnp.exp(-0.5 * pre * pre))
    out_ref[0, 0] = mxu(hidden, down, NN).astype(BF16)
    d_pre = (mxu(d, down, NT) * slope).astype(BF16)
    out_ref[1, 0] = mxu(d_pre, up, NT).astype(BF16)
    gdown_ref[0] += mxu(hidden, d, TN)
    gup_ref[0] += mxu(x, d_pre, TN)


def expert_block(rows, mask, w_up, w_down, block=256):
    kinds, held, count, width = rows.shape
    hidden = w_up.shape[2]
    both = pl.BlockSpec((kinds, 1, block, width), lambda x, r: (0, x, r, 0))
    up = pl.BlockSpec((1, width, hidden), lambda x, r: (x, 0, 0))
    down = pl.BlockSpec((1, hidden, width), lambda x, r: (x, 0, 0))
    return pl.pallas_call(
        expert_kernel,
        grid=(held, count // block),
        out_shape=(jax.ShapeDtypeStruct(rows.shape, BF16), jax.ShapeDtypeStruct(w_up.shape, F32),
                   jax.ShapeDtypeStruct(w_down.shape, F32)),
        in_specs=[both, pl.BlockSpec((1, block, 1), lambda x, r: (x, r, 0)), up, down],
        out_specs=(both, up, down),
        compiler_params=pltpu.CompilerParams(vmem_limit_bytes=60 << 20),
        name="experts",
    )(rows, mask, w_up, w_down)


ORDER = (0, 1, 4, 2, 5, 3, 6, 7)
WINDOW, AHEAD = 3, 2


def visit_kernel(groups, members, capacity, send_ref, count_ref, up_ref, down_ref,
                 out_ref, gup_ref, gdown_ref, here_ref,
                 rows_ref, parts_ref, hidden_ref, dpre_ref, pair_ref, row_ref, table_ref, grad_ref, prior_ref,
                 own_sem, last_sem, grad_sem, count_send, count_recv, far_send, far_recv, row_send, row_recv,
                 core_send, core_recv, pair_send, pair_recv, back_send, back_recv, home_send, home_recv):
    kinds, held = rows_ref.shape[:2]
    slots, width = rows_ref.shape[4:]
    chips = members // 2
    devices = groups * members
    e, t = lax.axis_index("ep"), lax.axis_index("tp")
    y, c = t // 2, lax.rem(t, 2)
    me = e * members + t
    sibling = (e, t + 1 - 2 * c)

    def other(k):
        d = lax.rem(me + k, devices)
        return d, (d // members, lax.rem(d, members))

    def far(peer, source):
        return pltpu.make_async_remote_copy(
            src_ref=send_ref.at[:, pl.ds(peer * held, held)], dst_ref=rows_ref.at[:, :, source, t],
            send_sem=far_send.at[peer], recv_sem=far_recv.at[source], device_id=(peer, t), device_id_type=MESH)

    def tell(to, device, source):
        return pltpu.make_async_remote_copy(
            src_ref=count_ref, dst_ref=table_ref.at[source], send_sem=count_send.at[to],
            recv_sem=count_recv.at[source], device_id=device, device_id_type=MESH)

    def across(i, to, source):
        there = rows_ref.at[:, :, i, source * 2 + c]
        return pltpu.make_async_remote_copy(
            src_ref=there, dst_ref=there, send_sem=row_send.at[i, to], recv_sem=row_recv.at[i, source],
            device_id=(e, to * 2 + c), device_id_type=MESH)

    def beside(i, source, core):
        there = rows_ref.at[:, :, i, source * 2 + core]
        return pltpu.make_async_remote_copy(
            src_ref=there, dst_ref=there, send_sem=core_send.at[i, source], recv_sem=core_recv.at[i, source],
            device_id=sibling, device_id_type=MESH)

    def to_pair(i, to):
        return pltpu.make_async_remote_copy(
            src_ref=parts_ref.at[:, :, i, to * 2 + 1 - c], dst_ref=pair_ref.at[i, to], send_sem=pair_send.at[i, to],
            recv_sem=pair_recv.at[i, to], device_id=sibling, device_id_type=MESH)

    def lap(source, to):
        return lax.rem(source - to - 1 + 2 * chips, chips)

    def to_row(i, to, source):
        return pltpu.make_async_remote_copy(
            src_ref=pair_ref.at[i, to], dst_ref=row_ref.at[i, lap(source, to)], send_sem=back_send.at[i, to],
            recv_sem=back_recv.at[i, source], device_id=(e, to * 2 + c), device_id_type=MESH)

    def from_row(i, source):
        there = row_ref.at[i, lap(source, y)]
        return pltpu.make_async_remote_copy(
            src_ref=there, dst_ref=there, send_sem=back_send.at[i, source], recv_sem=back_recv.at[i, source],
            device_id=(e, source * 2 + c), device_id_type=MESH)

    def home(i, source):
        return pltpu.make_async_remote_copy(
            src_ref=pair_ref.at[i, y], dst_ref=out_ref.at[:, pl.ds(source * held, held)], send_sem=home_send.at[i],
            recv_sem=home_recv.at[source], device_id=(i, t), device_id_type=MESH)

    def came(n):
        out, k, span = 0, 0, groups * groups
        for m in range(groups):
            k = k + ORDER[m] * ((span - (n - m) * (n - m)) // span)
        for b in range(groups.bit_length() - 1):
            w = 1 << b
            mine, its = lax.rem(e // w, 2), lax.rem(k // w, 2)
            out = out + w * (mine + its - 2 * mine * its)
        return out

    own = pltpu.make_async_copy(send_ref.at[:, pl.ds(e * held, held)], rows_ref.at[:, :, e, t], own_sem)
    own.start()
    barrier = pltpu.get_barrier_semaphore()

    def greet(k, _):
        pl.semaphore_signal(barrier, inc=1, device_id=other(k)[1], device_id_type=MESH)
        return 0

    lax.fori_loop(1, devices, greet, 0)
    pl.semaphore_wait(barrier, devices - 1)

    def send(k, _):
        far(came(k), e).start()
        return 0

    lax.fori_loop(1, WINDOW, send, 0)

    def spread(k, _):
        d, device = other(k)
        tell(d, device, me).start()
        return 0

    lax.fori_loop(1, devices, spread, 0)
    table_ref[me] = count_ref[...]
    own.wait()

    def pass_on(k):
        i = came(k)

        @pl.when(k > 0)
        def _():
            far(i, i).wait_recv()

        @pl.when((k >= WINDOW - AHEAD) & (k + AHEAD < groups))
        def _():
            far(came(k + AHEAD), e).start()

        for j in range(1, chips):
            across(i, lax.rem(y + j, chips), y).start()
        beside(i, y, c).start()

    def hand_over(k):
        i = came(k)
        for j in range(1, chips):
            source = lax.rem(y + j, chips)
            across(i, source, source).wait_recv()
            beside(i, source, c).start()

    def ranks():
        def hear(k, _):
            d, device = other(k)
            tell(d, device, d).wait_recv()
            return 0

        lax.fori_loop(1, devices, hear, 0)
        counts = table_ref[:, 0, :].astype(F32).astype(BF16)
        row = lax.broadcasted_iota(jnp.int32, (devices, devices), 0)
        col = lax.broadcasted_iota(jnp.int32, (devices, devices), 1)
        prior_ref[...] = mxu((col < row).astype(BF16), counts, NN)
        top = lax.broadcasted_iota(jnp.int32, (8, 128), 0) == 0
        here_ref[...] = jnp.where(top, prior_ref[pl.ds(me, 1), :], mxu(jnp.ones((8, devices), BF16), counts, NN))

    def compute(k):
        i = came(k)
        for source in range(chips):
            beside(i, source, 1 - c).wait_recv()
        for x in range(held):
            lane = lax.broadcasted_iota(jnp.int32, (1, 128), 1)
            place = lax.broadcasted_iota(jnp.int32, (slots, 1), 0).astype(F32)
            kept = []
            for j in range(members):
                prior = prior_ref[pl.ds(i * members + j, 1), :]
                prior = jnp.sum(jnp.where(lane == e * held + x, prior, 0.0), axis=1, keepdims=True)
                kept.append((prior + place < capacity).astype(F32))
            kept = jnp.concatenate(kept, axis=0)
            rows = rows_ref[0, x, i].reshape(members * slots, width)
            grads = rows_ref[1, x, i].reshape(members * slots, width)
            pre = mxu(rows, up_ref[x], NN)
            cdf = 0.5 * (1.0 + lax.erf(pre * 0.7071067811865476))
            hidden = (pre * cdf * kept).astype(BF16)
            slope = (cdf + pre * (0.3989422804014327 * jnp.exp(-0.5 * pre * pre))) * kept
            hidden_ref[x, i] = hidden
            parts_ref[0, x, i] = mxu(hidden, down_ref[x], NN).astype(BF16).reshape(members, slots, width)
            d_pre = (mxu(grads, down_ref[x], NT) * slope).astype(BF16)
            dpre_ref[x, i] = d_pre
            parts_ref[1, x, i] = mxu(d_pre, up_ref[x], NT).astype(BF16).reshape(members, slots, width)
        for to in range(chips):
            to_pair(i, to).start()

    def first(k):
        i = came(k)
        for j in range(1, chips + 1):
            to = lax.rem(y + j, chips)
            to_pair(i, to).wait_recv()
            if j < chips:
                for a in range(kinds):
                    for x in range(held):
                        mine = parts_ref[a, x, i, to * 2 + c].astype(F32)
                        pair_ref[i, to, a, x] = (mine + pair_ref[i, to, a, x].astype(F32)).astype(BF16)
                to_row(i, to, y).start()

    def second(k):
        i = came(k)
        for j in range(1, chips):
            source = lax.rem(y + j, chips)
            from_row(i, source).wait_recv()
        for a in range(kinds):
            for x in range(held):
                value = parts_ref[a, x, i, t].astype(F32) + pair_ref[i, y, a, x].astype(F32)
                for j in range(chips - 1):
                    value = value + row_ref[i, j, a, x].astype(F32)
                pair_ref[i, y, a, x] = value.astype(BF16)

        @pl.when(k > 0)
        def _():
            home(i, e).start()

    def slot(n, _):
        @pl.when((n >= 4) & (n < groups + 4))
        def _():
            second(n - 4)

        @pl.when((n >= 3) & (n < groups + 3))
        def _():
            first(n - 3)

        @pl.when(n < groups)
        def _():
            pass_on(n)

        @pl.when((n >= 1) & (n < groups + 1))
        def _():
            hand_over(n - 1)

        @pl.when(n == 2)
        def _():
            ranks()

        @pl.when((n >= 2) & (n < groups + 2))
        def _():
            compute(n - 2)
        return 0

    lax.fori_loop(0, groups + 2, slot, 0)

    def weight_grad(n, x, buffer, which):
        if which == 0:
            left, right, dst = hidden_ref, rows_ref.at[1], gdown_ref
        else:
            left, right, dst = rows_ref.at[0], dpre_ref, gup_ref
        total = mxu(left[x].reshape(-1, width), right[x].reshape(-1, width), TN)
        grad_ref[buffer] = total
        return pltpu.make_async_copy(grad_ref.at[buffer], dst.at[x], grad_sem.at[n])

    copies = []
    plan = [(x, which) for x in range(held) for which in range(2)]
    for n, (x, which) in enumerate(plan):
        if n >= 2:
            copies[n - 2].wait()
        copies.append(weight_grad(n, x, n % 2, which))
        copies[n].start()
        if n < 2:
            slot(groups + 2 + n, 0)
    last = pltpu.make_async_copy(pair_ref.at[e, y], out_ref.at[:, pl.ds(e * held, held)], last_sem)
    last.start()
    for n in range(max(0, len(plan) - 2), len(plan)):
        copies[n].wait()

    def finish(k, _):
        i = lax.rem(e + k, groups)
        home(i, e).wait_send()
        home(i, i).wait_recv()
        far(i, e).wait_send()
        return 0

    lax.fori_loop(1, groups, finish, 0)

    def drain(i, _):
        for source in range(chips):
            beside(i, source, c).wait_send()
            to_pair(i, source).wait_send()
        for j in range(1, chips):
            to = lax.rem(y + j, chips)
            across(i, to, y).wait_send()
            to_row(i, to, y).wait_send()
        return 0

    lax.fori_loop(0, groups, drain, 0)

    def told(k, _):
        d, device = other(k)
        tell(d, device, me).wait_send()
        return 0

    lax.fori_loop(1, devices, told, 0)
    last.wait()


def expert_visit(rows, count, w_up, w_down, groups, members, capacity):
    kinds, experts, slots, width = rows.shape
    held, hidden = w_up.shape[0], w_up.shape[2]
    chips, devices = members // 2, groups * members
    any_space = pl.BlockSpec(memory_space=pl.ANY)
    vmem = pl.BlockSpec(memory_space=pltpu.VMEM)
    dma = pltpu.SemaphoreType.DMA
    block = (kinds, held, slots, width)
    buffer = pltpu.VMEM((kinds, held, groups, members, slots, width), BF16)
    return pl.pallas_call(
        functools.partial(visit_kernel, groups, members, capacity),
        out_shape=(jax.ShapeDtypeStruct(rows.shape, BF16), jax.ShapeDtypeStruct(w_up.shape, F32),
                   jax.ShapeDtypeStruct(w_down.shape, F32), jax.ShapeDtypeStruct((8, 128), F32)),
        in_specs=[any_space, vmem, vmem, vmem],
        out_specs=(any_space, any_space, any_space, vmem),
        scratch_shapes=[buffer, buffer, pltpu.VMEM((held, groups, members * slots, hidden), BF16),
                        pltpu.VMEM((held, groups, members * slots, hidden), BF16),
                        pltpu.VMEM((groups, chips) + block, BF16), pltpu.VMEM((groups, chips - 1) + block, BF16),
                        pltpu.VMEM((devices,) + count.shape, jnp.int32), pltpu.VMEM((2,) + w_up.shape[1:], F32), pltpu.VMEM((devices, 128), F32),
                        dma(()), dma(()), dma((2 * held,)), dma((devices,)), dma((devices,)), dma((groups,)), dma((groups,)),
                        dma((groups, chips)), dma((groups, chips)), dma((groups, chips)), dma((groups, chips)),
                        dma((groups, chips)), dma((groups, chips)), dma((groups, chips)), dma((groups, chips)),
                        dma((groups,)), dma((groups,))],
        compiler_params=pltpu.CompilerParams(collective_id=3, has_side_effects=True, vmem_limit_bytes=60 << 20),
        name="expert_visit",
    )(rows, count, w_up, w_down)


def expert_steps(rows, count, w_up, w_down, groups, members, capacity):
    _, experts, slots, width = rows.shape
    held = w_up.shape[0]
    rows, table = dispatch(rows, count, groups, members)
    everyone = table[:, :, 0, :experts].transpose(1, 0, 2).reshape(groups * members, experts)
    device = jnp.arange(groups * members)
    before = device[None, :] < device[:, None]
    prior = jnp.sum(jnp.where(before[:, :, None], everyone[None], 0), axis=1)
    named = jnp.sum(everyone, axis=0)
    mine = lax.dynamic_slice_in_dim(prior.reshape(groups, members, experts), lax.axis_index("ep") * held, held, 2)
    room = mine.transpose(2, 1, 0)[..., None] + jnp.arange(slots)[None, None, None] < capacity
    room = room.reshape(held, members * groups * slots, 1).astype(F32)
    parts, grad_up, grad_down = expert_block(rows.reshape(2, held, members * groups * slots, width), room, w_up, w_down)
    return collect(parts.reshape(rows.shape), groups, members), grad_up, grad_down, prior, named


def local(tokens, d_out, segment, route, gain_one, w_in, conv_w, conv_b, w_x, w_dt, b_dt, a_log, d_skip, w_out,
          gain_two, w_router, w_up, w_down):
    length, width = tokens.shape
    inner = w_in.shape[1] // 2
    experts = w_router.shape[1]
    groups, members = lax.axis_size("ep"), lax.axis_size("tp")
    slots = 3 * length // (2 * experts)
    capacity = 5 * length * groups * members // (4 * experts)
    rank, states, taps = w_dt.shape[0], a_log.shape[0], conv_w.shape[0]
    used = rank + 2 * states
    labels = (segment.reshape(-1, 128), route.reshape(-1, 128))
    rows = (conv_w, conv_b, b_dt, d_skip, gain_one, gain_two) + labels
    normed, both, wx, wxt, wdt, rates, vec, column, route = front(tokens, rows, w_in, w_x.T, w_dt, a_log)
    gated, *saved, proj, starts = mid_fwd(both, column, vec, wx, wdt, rates, rank)
    after, leaving, count, aux = route_out(gated, w_out, tokens, d_out, column, route, vec, w_router.T, slots)
    leaving = leaving.reshape(2, experts, slots, width)
    if members == 4:
        back, grad_up, grad_down, here = expert_visit(leaving, count, w_up, w_down, groups, members, capacity)
    else:
        back, grad_up, grad_down, prior, named = expert_steps(leaving, count, w_up, w_down, groups, members, capacity)
        this = jnp.arange(groups * members) == lax.axis_index(("ep", "tp"))
        here = jnp.stack([jnp.sum(jnp.where(this[:, None], prior, 0), axis=0), named]).astype(F32)
        here = jnp.pad(here, ((0, 6), (0, 128 - experts)))
    final, d_after, d_mixed, d_gated, g_two, g_router, counts = come_home(
        back.reshape(2, experts * slots, width), after, d_out, aux, column, route, here, vec, w_router.T, w_out, slots,
        capacity,
    )
    d_both, g_vec, g_x, g_dt, g_rates = mid_bwd(
        both, d_gated, saved, proj, starts, column, vec, wxt, wdt, rates, rank
    )
    total, d_tokens = tail_sum(
        normed, d_both, w_in, gated, d_mixed, tokens, d_after, vec, g_two, g_x, g_dt, g_rates, rates, g_vec, g_router, used,
        rank, groups, members,
    )
    total_in, total_out, total_x, total_router, total_dt, total_log, total_taps, total_bias, total_step, total_skip, *gains, up_rows, down_rows, d_tokens = (
        unpack_grads(total, (grad_up.reshape(-1, w_up.shape[2]), grad_down.reshape(-1, width), d_tokens), width, inner, used, experts, (rank, states, taps))
    )
    return (
        final,
        d_tokens,
        counts,
        gains[0],
        total_in,
        total_taps,
        total_bias,
        total_x.T,
        total_dt,
        total_step,
        total_log,
        total_skip,
        total_out,
        gains[1],
        total_router[:, :width].T,
        up_rows.reshape(w_up.shape),
        down_rows.reshape(w_down.shape),
    )


def solution(mesh):
    in_specs = (
        P(("ep", "tp"), None),
        P(("ep", "tp"), None),
        P(("ep", "tp")),
        P(("ep", "tp"), None),
        P(),
        P(),
        P(),
        P(),
        P(),
        P(),
        P(),
        P(),
        P(),
        P(),
        P(),
        P(),
        P("ep", None, "tp"),
        P("ep", "tp", None),
    )
    out_specs = (
        P(("ep", "tp"), None),
        P(("ep", "tp"), None),
        P(),
        P(),
        P(),
        P(),
        P(),
        P(),
        P(),
        P(),
        P(),
        P(),
        P(),
        P(),
        P(),
        P("ep", None, "tp"),
        P("ep", "tp", None),
    )
    return jax.shard_map(local, mesh=mesh, in_specs=in_specs, out_specs=out_specs, check_vma=False)
```

time: 534 us -> 368 us (0.69)
  local copies, waits for them, and re-layouts: 45.3 us -> 1.42 us
  Pallas kernels: 409 us -> 366 us
  matrix products: 40.1 us -> 0 us
  other arithmetic: 34.7 us -> 0 us
    dot_general x13 -> x0, matrix products: 40.1 us -> none  [the longest x4 11.7 us: contract_rows(): return lax.dot_general(left, right, TN, preferred_element_type=F32)]
    pallas_call x4 -> x6, Pallas kernels: 296 us -> 270 us  [the longest x1 130 us: expert_visit(): pl.pallas_call(functools.partial(visit_kernel, groups, members, capacity)...]
    slice x12 -> x0, local copies, waits for them, and re-layouts: 21.9 us -> none  [the longest x1 3.81 us: local(): small[at + taps + 2]]
    convert_element_type x10 -> x0, other arithmetic: 15.8 us -> none  [the longest x1 7.37 us: local(): total_in.astype(F32)]
    unnamed x95 -> x0, local copies, waits for them, and re-layouts: 13.2 us -> none
    pallas_call x1, Pallas kernels: 76.7 us -> 64.7 us  [mid_bwd(): pl.pallas_call(functools.partial(mid_bwd_kernel, rank), grid=(blocks,), o...]
where the time goes in v4:
time: 368 us
  Pallas kernels  366 us (99%)
    pallas_call x1, Pallas kernels, expert_visit(): pl.pallas_call(functools.partial(visit_kernel, groups, members, capacity)...  130 us
    pallas_call x1, Pallas kernels, tail_sum(): pl.pallas_call(functools.partial(tail_kernel, orders, tall, across, used,...  96.1 us
    pallas_call x1, Pallas kernels, mid_bwd(): pl.pallas_call(functools.partial(mid_bwd_kernel, rank), grid=(blocks,), o...  64.7 us
    pallas_call x1, Pallas kernels, mid_fwd(): pl.pallas_call(functools.partial(mid_fwd_kernel, rank), grid=(length // T...  30.8 us
    pallas_call x1, Pallas kernels, unpack_grads(): pl.pallas_call(unpack_kernel, grid=(tall,), out_shape=(jax.ShapeDtypeStru...  16.5 us
    pallas_call x1, Pallas kernels, come_home(): pl.pallas_call(functools.partial(home_kernel, slots, capacity), out_shape...  10.3 us
    pallas_call x1, Pallas kernels, front(): pl.pallas_call(functools.partial(front_kernel, rank, used), grid=(w_in.sh...  8.46 us
    pallas_call x1, Pallas kernels, route_out(): pl.pallas_call(functools.partial(route_kernel, slots), out_shape=(jax.Sha...  8.38 us

profile of v4, /device:TPU:1, one launch (start us, length us, event | category | flops | bytes accessed | tf_op | source)
XLA Modules:
  0.0 367.9 jit_solution(2563676557833885379)
XLA Ops:
  0.7 8.5 %front.1 = (bf16[512,768]{1,0:T(8,128)(2,1)}, f32[512,3072]{1,0:T(8,128)}, bf16[1536,128]{1,0:T(8,128)(2,1)}, bf16[128,1536]{1,0:T(8,128)(2,1)}, bf16[128,1536]{...) custom-call(bf16[512,768]{1,0:T(8,128)(2,1)} %tokens_hbm.1, ...), custom_call_target="tpu_custom_call" | custom-call | tf_op jit(solution)/shard_map/front/pallas_call | solution.py:688
  9.1 30.8 %mid_fwd.1 = (bf16[512,1536]{1,0:T(8,128)(2,1)}, f32[512,1536]{1,0:T(8,128)}, f32[512,1536]{1,0:T(8,128)}, f32[512,1536]{1,0:T(8,128)}, f32[512,1536]{1,0:T(8,12...) custom-call(f32[512,3072]{1,0:T(8,128)} %get-tuple-element.72.both_ref, ...), custom_call_target="tpu_custom_call" | custom-call | tf_op jit(solution)/shard_map/mid_fwd/pallas_call | solution.py:159
  40.0 8.4 %route_out.1 = (f32[512,768]{1,0:T(8,128)}, bf16[2,768,768]{2,1,0:T(8,128)(2,1)}, s32[8,128]{1,0:T(8,128)}, f32[512,128]{1,0:T(8,128)}) custom-call(bf16[512,1536]{1,0:T(8,128)(2,1)} %get-tuple-element.78.gated_ref.gated_hbm, bf16[1536,768]{1,0:T(8,128)(2,1)} %w_out_ref.3, bf16[512,768]{1,0:T(8,128)(2,1)} %tokens_hbm.1, bf16[512,768]{1,0:T(8,128)(2,1)} %d_out_ref.3, ...), custom_call_target="tpu_custom_call" | custom-call | tf_op jit(solution)/shard_map/route_out/pallas_call | solution.py:747
  48.4 130.4 %expert_visit.1 = (bf16[2,16,48,768]{3,2,1,0:T(8,128)(2,1)}, f32[2,768,768]{2,1,0:T(8,128)}, f32[2,768,768]{2,1,0:T(8,128)}, f32[8,128]{1,0:T(8,128)}) custom-call(bf16[2,16,48,768]{3,2,1,0:T(8,128)(2,1)} %bitcast.15, s32[8,128]{1,0:T(8,128)} %get-tuple-element.81.count_ref, bf16[2,768,768]{2,1,0:T(8,128)(2,1)} %up_ref.1, bf16[2,768,768]{2,1,0:T(8,128)(2,1)} %down_ref.1), custom_call_target="tpu_custom_call" | custom-call | tf_op jit(solution)/shard_map/expert_visit/pallas_call | solution.py:1368
  178.8 10.3 %come_home.1 = (bf16[512,768]{1,0:T(8,128)(2,1)}, f32[512,768]{1,0:T(8,128)}, bf16[512,768]{1,0:T(8,128)(2,1)}, f32[512,1536]{1,0:T(8,128)}, f32[8,768]{1,0:T(8,...) custom-call(bf16[2,768,768]{2,1,0:T(8,128)(2,1)} %bitcast.16, f32[512,768]{1,0:T(8,128)} %get-tuple-element.83.after_ref, ...), custom_call_target="tpu_custom_call" | custom-call | tf_op jit(solution)/shard_map/come_home/pallas_call | solution.py:797
  189.1 64.7 %mid_bwd.1 = (bf16[512,3072]{1,0:T(8,128)(2,1)}, f32[8,1536]{1,0:T(8,128)}, f32[128,1536]{1,0:T(8,128)}, f32[128,1536]{1,0:T(8,128)}, f32[16,1536]{1,0:T(8,128)}) custom-call(f32[512,3072]{1,0:T(8,128)} %get-tuple-element.72.both_ref, f32[512,1536]{1,0:T(8,128)} %get-tuple-element.88.dg_ref, f32[512,1536]{1,0:T(8,128)} %get-tuple-element.89.conv_ref, ...), custom_call_target="tpu_custom_call" | custom-call | tf_op jit(solution)/shard_map/mid_bwd/pallas_call | solution.py:328
  253.9 96.1 %tail_sum.1 = (bf16[15,256,1024]{2,1,0:T(8,128)(2,1)}, f32[512,768]{1,0:T(8,128)}) custom-call(bf16[512,768]{1,0:T(8,128)(2,1)} %get-tuple-element.87.normed_ref, bf16[512,3072]{1,0:T(8,128)(2,1)} %get-tuple-element.98.d_both_ref, f32[8,1536]{1,0:T(8,128)} %get-tuple-element.74.vec_ref.gain_ref, f32[8,768]{1,0:T(8,128)} %get-tuple-element.99.g_two_ref, ...), custom_call_target="tpu_custom_call" | custom-call | tf_op jit(solution)/shard_map/tail_sum/pallas_call | solution.py:571
  350.0 16.5 %unpack_grads.1 = (f32[768,3072]{1,0:T(8,128)}, f32[1536,768]{1,0:T(8,128)}, f32[80,1536]{1,0:T(8,128)}, f32[16,1536]{1,0:T(8,128)}, f32[48,1536]{1,0:T(8,128)},...) custom-call(bf16[15,256,1024]{2,1,0:T(8,128)(2,1)} %get-tuple-elemen, ...), custom_call_target="tpu_custom_call" | custom-call | tf_op jit(solution)/shard_map/unpack_grads/pallas_call | solution.py:631
  366.5 1.4 slice_bitcast_fusion

commit v5 on v4

--- a/solution.py
+++ b/solution.py
@@ -1180,8 +1180,6 @@
         tell(d, device, me).start()
         return 0
 
-    lax.fori_loop(1, devices, spread, 0)
-    table_ref[me] = count_ref[...]
     own.wait()
 
     def pass_on(k):
@@ -1287,6 +1285,11 @@
         @pl.when(n < groups)
         def _():
             pass_on(n)
+
+        @pl.when(n == 0)
+        def _():
+            lax.fori_loop(1, devices, spread, 0)
+            table_ref[me] = count_ref[...]
 
         @pl.when((n >= 1) & (n < groups + 1))
         def _():

time: 368 us -> 368 us (level)
  no operation moved by 1% of the time
where the time goes in v5:
time: 368 us
  Pallas kernels  366 us (99%)
    pallas_call x1, Pallas kernels, expert_visit(): pl.pallas_call(functools.partial(visit_kernel, groups, members, capacity)...  130 us
    pallas_call x1, Pallas kernels, tail_sum(): pl.pallas_call(functools.partial(tail_kernel, orders, tall, across, used,...  96.1 us
    pallas_call x1, Pallas kernels, mid_bwd(): pl.pallas_call(functools.partial(mid_bwd_kernel, rank), grid=(blocks,), o...  64.7 us
    pallas_call x1, Pallas kernels, mid_fwd(): pl.pallas_call(functools.partial(mid_fwd_kernel, rank), grid=(length // T...  30.8 us
    pallas_call x1, Pallas kernels, unpack_grads(): pl.pallas_call(unpack_kernel, grid=(tall,), out_shape=(jax.ShapeDtypeStru...  16.5 us
    pallas_call x1, Pallas kernels, come_home(): pl.pallas_call(functools.partial(home_kernel, slots, capacity), out_shape...  10.3 us
    pallas_call x1, Pallas kernels, front(): pl.pallas_call(functools.partial(front_kernel, rank, used), grid=(w_in.sh...  8.46 us
    pallas_call x1, Pallas kernels, route_out(): pl.pallas_call(functools.partial(route_kernel, slots), out_shape=(jax.Sha...  8.38 us

profile of v5, /device:TPU:1, one launch (start us, length us, event | category | flops | bytes accessed | tf_op | source)
XLA Modules:
  0.0 367.9 jit_solution(17609608225291830079)
XLA Ops:
  0.7 8.5 %front.1 = (bf16[512,768]{1,0:T(8,128)(2,1)}, f32[512,3072]{1,0:T(8,128)}, bf16[1536,128]{1,0:T(8,128)(2,1)}, bf16[128,1536]{1,0:T(8,128)(2,1)}, bf16[128,1536]{...) custom-call(bf16[512,768]{1,0:T(8,128)(2,1)} %tokens_hbm.1, ...), custom_call_target="tpu_custom_call" | custom-call | tf_op jit(solution)/shard_map/front/pallas_call | solution.py:688
  9.1 30.8 %mid_fwd.1 = (bf16[512,1536]{1,0:T(8,128)(2,1)}, f32[512,1536]{1,0:T(8,128)}, f32[512,1536]{1,0:T(8,128)}, f32[512,1536]{1,0:T(8,128)}, f32[512,1536]{1,0:T(8,12...) custom-call(f32[512,3072]{1,0:T(8,128)} %get-tuple-element.72.both_ref, ...), custom_call_target="tpu_custom_call" | custom-call | tf_op jit(solution)/shard_map/mid_fwd/pallas_call | solution.py:159
  40.0 8.4 %route_out.1 = (f32[512,768]{1,0:T(8,128)}, bf16[2,768,768]{2,1,0:T(8,128)(2,1)}, s32[8,128]{1,0:T(8,128)}, f32[512,128]{1,0:T(8,128)}) custom-call(bf16[512,1536]{1,0:T(8,128)(2,1)} %get-tuple-element.78.gated_ref.gated_hbm, bf16[1536,768]{1,0:T(8,128)(2,1)} %w_out_ref.3, bf16[512,768]{1,0:T(8,128)(2,1)} %tokens_hbm.1, bf16[512,768]{1,0:T(8,128)(2,1)} %d_out_ref.3, ...), custom_call_target="tpu_custom_call" | custom-call | tf_op jit(solution)/shard_map/route_out/pallas_call | solution.py:747
  48.4 130.4 %expert_visit.1 = (bf16[2,16,48,768]{3,2,1,0:T(8,128)(2,1)}, f32[2,768,768]{2,1,0:T(8,128)}, f32[2,768,768]{2,1,0:T(8,128)}, f32[8,128]{1,0:T(8,128)}) custom-call(bf16[2,16,48,768]{3,2,1,0:T(8,128)(2,1)} %bitcast.15, s32[8,128]{1,0:T(8,128)} %get-tuple-element.81.count_ref, bf16[2,768,768]{2,1,0:T(8,128)(2,1)} %up_ref.1, bf16[2,768,768]{2,1,0:T(8,128)(2,1)} %down_ref.1), custom_call_target="tpu_custom_call" | custom-call | tf_op jit(solution)/shard_map/expert_visit/pallas_call | solution.py:1371
  178.8 10.3 %come_home.1 = (bf16[512,768]{1,0:T(8,128)(2,1)}, f32[512,768]{1,0:T(8,128)}, bf16[512,768]{1,0:T(8,128)(2,1)}, f32[512,1536]{1,0:T(8,128)}, f32[8,768]{1,0:T(8,...) custom-call(bf16[2,768,768]{2,1,0:T(8,128)(2,1)} %bitcast.16, f32[512,768]{1,0:T(8,128)} %get-tuple-element.83.after_ref, ...), custom_call_target="tpu_custom_call" | custom-call | tf_op jit(solution)/shard_map/come_home/pallas_call | solution.py:797
  189.1 64.7 %mid_bwd.1 = (bf16[512,3072]{1,0:T(8,128)(2,1)}, f32[8,1536]{1,0:T(8,128)}, f32[128,1536]{1,0:T(8,128)}, f32[128,1536]{1,0:T(8,128)}, f32[16,1536]{1,0:T(8,128)}) custom-call(f32[512,3072]{1,0:T(8,128)} %get-tuple-element.72.both_ref, f32[512,1536]{1,0:T(8,128)} %get-tuple-element.88.dg_ref, f32[512,1536]{1,0:T(8,128)} %get-tuple-element.89.conv_ref, ...), custom_call_target="tpu_custom_call" | custom-call | tf_op jit(solution)/shard_map/mid_bwd/pallas_call | solution.py:328
  253.9 96.1 %tail_sum.1 = (bf16[15,256,1024]{2,1,0:T(8,128)(2,1)}, f32[512,768]{1,0:T(8,128)}) custom-call(bf16[512,768]{1,0:T(8,128)(2,1)} %get-tuple-element.87.normed_ref, bf16[512,3072]{1,0:T(8,128)(2,1)} %get-tuple-element.98.d_both_ref, f32[8,1536]{1,0:T(8,128)} %get-tuple-element.74.vec_ref.gain_ref, f32[8,768]{1,0:T(8,128)} %get-tuple-element.99.g_two_ref, ...), custom_call_target="tpu_custom_call" | custom-call | tf_op jit(solution)/shard_map/tail_sum/pallas_call | solution.py:571
  350.0 16.5 %unpack_grads.1 = (f32[768,3072]{1,0:T(8,128)}, f32[1536,768]{1,0:T(8,128)}, f32[80,1536]{1,0:T(8,128)}, f32[16,1536]{1,0:T(8,128)}, f32[48,1536]{1,0:T(8,128)},...) custom-call(bf16[15,256,1024]{2,1,0:T(8,128)(2,1)} %get-tuple-elemen, ...), custom_call_target="tpu_custom_call" | custom-call | tf_op jit(solution)/shard_map/unpack_grads/pallas_call | solution.py:631
  366.5 1.4 slice_bitcast_fusion
